TPU v7x, 32 devices: a whole 2x2x4 slice. The times are simulated.
32 devices in a mesh: seq: 16 (over z, y, x), head: 2 (over core).
Axes of the slice: x: 2, y: 2, z: 4, core: 2. Of those that a mesh axis runs over, the one named last changes fastest.
Arguments:
- queries: bfloat16 [2048, 16, 128], P('seq', 'head'), may hold values from -6 to 6
- key_vectors: bfloat16 [2048, 16, 128], P('seq', 'head'), may hold values from -16 to 16
- values: bfloat16 [2048, 16, 128], P('seq', 'head'), may hold values from -6 to 6
- out_gate: bfloat16 [2048, 16, 128], P('seq', 'head'), may hold values from -6 to 6
- inputs: bfloat16 [2048, 2048], P('seq', 'head'), may hold values from -6 to 6
- beta_weight: bfloat16 [16, 2048], P(None, 'head'), may hold values from -0.1875 to 0.1875
- log_decay: float32 [16, 2048], P('head', 'seq'), may hold values from -1 to 0
- initial_state: float32 [16, 128, 128], P('head'), may hold values from -6 to 6
Outputs:
- gated_out: bfloat16 [2048, 16, 128], P('seq', 'head')
- block_states: float32 [32, 16, 128, 128], P('seq', 'head')
All inputs are finite; a program needn't handle non-finite values.
Results may differ from a plain program's by a relative error of at most 0.0012.
Values sent between devices are 32-bit elements; how exact they have to be, the bound alone decides.
No kernel may reach another device: no remote copies, remote signals or barrier semaphores. Data moves between devices by JAX's collectives and lax.ppermute only.
A program may use at most 64 MiB of HBM per device.

v0:
```python
import jax
import jax.numpy as jnp
from jax import lax
from jax.sharding import PartitionSpec as P

BLOCK = 64


EPSILON = 1e-06


def entering(value, axis, join, neutral):
    count, mine = (lax.axis_size(axis), lax.axis_index(axis))
    pieces = jax.tree.map(lambda part: lax.all_gather(part, axis), value)
    so_far = jax.tree.map(
        lambda part, zero: jnp.full_like(part, 0) + jnp.asarray(zero, part.dtype), value, neutral
    )

    def step(position, so_far):
        longer = join(so_far, jax.tree.map(lambda part: part[position], pieces))
        return jax.tree.map(lambda new, old: jnp.where(position < mine, new, old), longer, so_far)

    return lax.fori_loop(0, count - 1, step, so_far)


def matmul(matrix, operand):
    return jnp.einsum("...ij,...jk->...ik", matrix, operand, precision=lax.Precision.HIGHEST)


def normalize(query_block, key_block, key_limit):
    query_float = query_block.astype(jnp.float32)
    key_float = key_block.astype(jnp.float32)
    queries_unit = (
        query_float
        / jnp.sqrt(jnp.sum(query_float * query_float, -1, keepdims=True) + EPSILON)
        * query_float.shape[-1] ** (-0.5)
    )
    keys_unit = key_float / jnp.maximum(
        jnp.sqrt(jnp.sum(key_float * key_float, -1, keepdims=True)), key_limit
    )
    return (queries_unit, keys_unit)


def block_parts(queries_unit, keys_unit, value_rows, beta_gate, decay_rows):
    length = decay_rows.shape[-1]
    feature = keys_unit.shape[-1]
    cumulative = jnp.cumsum(decay_rows, axis=-1)
    inside = jnp.tril(jnp.ones((length, length), jnp.float32))
    strict = jnp.tril(jnp.ones((length, length), jnp.float32), -1)
    spread = jnp.where(inside > 0, cumulative[..., :, None] - cumulative[..., None, :], 0.0)
    damping = jnp.exp(spread) * inside
    intersections = jnp.einsum(
        "...id,...jd->...ij", keys_unit, keys_unit, precision=lax.Precision.HIGHEST
    )
    system = (
        jnp.eye(length, dtype=jnp.float32)
        + beta_gate[..., :, None] * intersections * damping * strict
    )
    right_side = jnp.concatenate(
        [
            (beta_gate * jnp.exp(cumulative))[..., None] * keys_unit,
            beta_gate[..., None] * value_rows,
        ],
        axis=-1,
    )
    solved = lax.linalg.triangular_solve(
        system, right_side, left_side=True, lower=True, unit_diagonal=True
    )
    write_keys = solved[..., :feature]
    write_values = solved[..., feature:]
    final_sum = cumulative[..., -1:]
    carried = keys_unit * jnp.exp(final_sum - cumulative)[..., None]
    transition = jnp.exp(final_sum)[..., None] * jnp.eye(feature, dtype=jnp.float32) - jnp.einsum(
        "...ld,...le->...de", carried, write_keys, precision=lax.Precision.HIGHEST
    )
    offset = jnp.einsum(
        "...ld,...le->...de", carried, write_values, precision=lax.Precision.HIGHEST
    )
    reached = queries_unit * jnp.exp(cumulative)[..., None]
    scores = (
        jnp.einsum("...id,...jd->...ij", queries_unit, keys_unit, precision=lax.Precision.HIGHEST)
        * damping
    )
    return (write_keys, write_values, transition, offset, reached, scores)


def block_out(block_info, state_now):
    write_keys, write_values, transition, offset, reached, scores = block_info
    corrected = write_values - matmul(write_keys, state_now)
    return matmul(reached, state_now) + matmul(scores, corrected)


def gate_norm(raw_out, gate_rows):
    inverse_rms = 1.0 / jnp.sqrt(jnp.mean(raw_out * raw_out, -1, keepdims=True) + EPSILON)
    return (raw_out * inverse_rms * jax.nn.silu(gate_rows.astype(jnp.float32))).astype(jnp.bfloat16)


def combine(earlier, latter):
    return (matmul(latter[0], earlier[0]), matmul(latter[0], earlier[1]) + latter[1])


def advance(queries_unit, keys_unit, value_rows, beta_gate, decay_rows, start_state):
    block_info = block_parts(queries_unit, keys_unit, value_rows, beta_gate, decay_rows)
    transition = jnp.moveaxis(block_info[2], 1, 0)
    offset = jnp.moveaxis(block_info[3], 1, 0)
    head_count = transition.shape[1]
    feature = transition.shape[2]
    identity_map = jnp.broadcast_to(
        jnp.eye(feature, dtype=jnp.float32), (head_count, feature, feature)
    )
    zero_state = jnp.zeros((head_count, feature, value_rows.shape[-1]), jnp.float32)

    def compose(carried_map, block_map):
        return (
            (
                matmul(block_map[0], carried_map[0]),
                matmul(block_map[0], carried_map[1]) + block_map[1],
            ),
            carried_map,
        )

    (device_map, device_offset), prefixes = lax.scan(
        compose, (identity_map, zero_state), (transition, offset)
    )
    before_map, before_offset = entering(
        (device_map, device_offset), "seq", combine, (identity_map, zero_state)
    )
    entry_state = matmul(before_map, start_state) + before_offset
    starts = matmul(prefixes[0], entry_state[None]) + prefixes[1]
    raw_out = block_out(block_info, jnp.moveaxis(starts, 0, 1))
    return (raw_out, starts)


def on_device(
    queries, key_vectors, values, out_gate, inputs, beta_weight, log_decay, initial_state
):
    token_count, head_count, feature = queries.shape
    blocks = token_count // BLOCK
    logits = lax.psum_scatter(
        lax.dot_general(
            beta_weight, inputs, (((1,), (1,)), ((), ())), preferred_element_type=jnp.float32
        ),
        "head",
        scatter_dimension=0,
        tiled=True,
    )
    beta_gate = jax.nn.sigmoid(logits)
    key_float = key_vectors.astype(jnp.float32)
    key_total = lax.psum(jnp.sum(key_float * key_float, axis=(0, 2)), "seq")
    key_limit = jnp.sqrt(key_total / (token_count * lax.axis_size("seq")) + EPSILON)
    queries_unit, keys_unit = normalize(queries, key_vectors, key_limit[:, None])

    def arrange(tensor):
        return tensor.reshape(blocks, BLOCK, head_count, -1).transpose(2, 0, 1, 3)

    query_blocks = arrange(queries_unit)
    key_blocks = arrange(keys_unit)
    value_blocks = arrange(values.astype(jnp.float32))
    beta_blocks = beta_gate.reshape(head_count, blocks, BLOCK)
    decay_blocks = log_decay.reshape(head_count, blocks, BLOCK)
    raw_out, starts = advance(
        query_blocks, key_blocks, value_blocks, beta_blocks, decay_blocks, initial_state
    )
    gated_out = gate_norm(
        raw_out.transpose(1, 2, 0, 3).reshape(token_count, head_count, feature), out_gate
    )
    return (gated_out, starts)


def solution(mesh):
    return jax.shard_map(
        on_device,
        mesh=mesh,
        in_specs=(
            P("seq", "head", None),
            P("seq", "head", None),
            P("seq", "head", None),
            P("seq", "head", None),
            P("seq", "head"),
            P(None, "head"),
            P("head", "seq"),
            P("head", None, None),
        ),
        out_specs=(P("seq", "head", None), P("seq", "head", None, None)),
        check_vma=False,
    )
```

profile of v0, /device:TPU:0, one launch (start us, length us, event | category | flops | bytes accessed | tf_op | source)
XLA Modules:
  0.0 458.2 jit_solution(17087418341831936964)
XLA Ops:
  7.4 0.8 reshape.130
  8.9 1.3 fusion.37
  10.1 43.5 %psum.7 = f32[8]{0:T(128)S(1)} all-reduce(f32[8]{0:T(128)S(1)} %get-tuple-element.239), channel_id=1, replica_groups=mesh['seq'=16,'head'=2] {'seq'}, use_global_device_ids=true, to_apply=%region_4.0 | all-reduce | flops 8 | bytes 64 | tf_op jit(solution)/shard_map/psum | solution.py:149
  53.7 1.2 convert_divide_fusion
  55.0 1.3 fusion.68
  56.3 2.5 all-reduce
  58.8 1.2 dynamic-slice
  60.8 1.0 fusion.30
  61.8 78.6 %custom-call.3 = f32[8,2,1,64,64]{3,4,2,1,0:T(8,128)S(1)} custom-call(f32[8,2,1,64,64]{4,3,2,1,0:T(8,128)S(1)} %fusion.30), custom_call_target="InvertDiagBlocksLowerTriangular" | custom-call | tf_op jit(solution)/shard_map/triangular_solve | solution.py:66
  140.5 1.0 copy.83
  142.0 1.1 fusion.31
  143.0 3.0 convolution_bitcast_fusion
  146.0 2.0 fusion.22
  148.1 12.5 %while.33 = (s32[]{:T(128)}, f32[8,128,128]{2,1,0:T(8,128)S(1)}, f32[8,128,128]{2,1,0:T(8,128)}, f32[2,8,128,128]{3,2,0,1:T(8,128)}, f32[2,8,128,128]{2,3,0,1:T(...) while((s32[]{:T(128)}, f32[8,128,128]{2,1,0:T(8,128)S(1)}, ...), condition=%wide.region_7.8_spmd.clone, body=%wide.region_6.7_spmd.clone.sunk | while | flops 403046400 | bytes 9963628 | solution.py:122
  148.1 1.1 copy.164
  149.2 2.5 convolution_add_fusion.5
  151.9 0.9 constant_dynamic-update-slice_fusion.2
  152.8 0.8 bitcast_dynamic-update-slice_fusion.2
  153.7 0.7 fusion.97
  154.3 1.0 copy.164
  155.4 2.5 convolution_add_fusion.5
  158.1 0.9 constant_dynamic-update-slice_fusion.2
  159.1 0.8 bitcast_dynamic-update-slice_fusion.2
  160.6 0.8 copy-done.1
  162.7 2.8 convolution_multiply_fusion
  165.5 104.3 %all-gather.5.cloned.1.call-done = f32[128,128,128]{2,1,0:T(8,128)} async-done(((f32[8,128,128]{2,1,0:T(8,128)}), f32[128,128,128]{2,1,0:T(8,128)}) %all-gather.5.cloned.1.call-update) | async-done | bytes 8388624 | tf_op jit(solution)/shard_map/all_gather | solution.py:14
  269.8 113.3 %all-gather.7.cloned.1.call-done = f32[128,128,128]{2,1,0:T(8,128)} async-done(((f32[8,128,128]{2,1,0:T(8,128)}), f32[128,128,128]{2,1,0:T(8,128)}) %all-gather.7.cloned.1.call-update) | async-done | bytes 8388624 | tf_op jit(solution)/shard_map/all_gather | solution.py:14
  383.1 55.4 %while.34 = (s32[]{:T(128)}, f32[8,128,128]{2,1,0:T(8,128)S(1)}, f32[8,128,128]{2,1,0:T(8,128)S(1)}, s32[]{:T(128)}, f32[16,8,128,128]{3,2,1,0:T(8,128)}, /*index=5*/f32[16,8,128,128]{3,2,1,0:T(8,128)}, s32[]{:T(128)}, s32[]{:T(128)}) while((s32[]{:T(128)}, f32[8,128,128]{2,1,0:T(8,128)S(1)}, f32[8,128,128]{2,1,0:T(8,128)S(1)}, ...), condition=%wide.region_9.10_spmd.clone, body=%wide.region_8.9_spmd.clone.sunk | while | flops 403308544 | bytes 6818920 | solution.py:23
  383.2 1.9 fusion.102
  385.2 1.7 convolution_select_fusion.2
  386.9 1.9 fusion.102
  388.9 1.7 convolution_select_fusion.2
  390.6 1.9 fusion.102
  392.5 1.7 convolution_select_fusion.2
  394.3 1.9 fusion.102
  396.2 1.7 convolution_select_fusion.2
  398.0 1.9 fusion.102
  399.9 1.7 convolution_select_fusion.2
  401.7 1.9 fusion.102
  403.6 1.7 convolution_select_fusion.2
  405.4 1.9 fusion.102
  407.3 1.7 convolution_select_fusion.2
  409.1 1.9 fusion.102
  411.0 1.7 convolution_select_fusion.2
  412.8 1.9 fusion.102
  414.7 1.7 convolution_select_fusion.2
  416.4 1.9 fusion.102
  418.4 1.7 convolution_select_fusion.2
  420.1 1.9 fusion.102
  422.1 1.7 convolution_select_fusion.2
  423.8 1.9 fusion.102
  425.7 1.7 convolution_select_fusion.2
  427.5 1.9 fusion.102
  429.4 1.7 convolution_select_fusion.2
  431.2 1.9 fusion.102
  433.1 1.7 convolution_select_fusion.2
  434.9 1.9 fusion.102
  436.8 1.7 convolution_select_fusion.2
  439.2 2.6 fusion.23
  441.8 2.9 convolution_subtract_fusion
  444.7 1.3 copy.94
  446.0 1.8 fusion.69
  447.9 2.2 fusion.45
  450.3 1.1 fusion.48
  (87 shorter events, 5.9 us)
Async XLA Ops:
  7.2 431.4 %copy-start = (f32[8,128,128]{2,1,0:T(8,128)S(1)}, f32[8,128,128]{2,1,0:T(8,128)}, u32[]{:S(2)}) copy-start(f32[8,128,128]{2,1,0:T(8,128)} %param.19) | copy-start | bytes 1572868
  7.2 262.6 %all-gather.5.cloned.1.call-start = ((), (), s32[]{:S(2)}) async-start(), calls=%async_computation | async-start | bytes 8912896 | tf_op jit(solution)/shard_map/all_gather | solution.py:14
  55.0 91.0 %copy-start.2 = (f32[128,8,128]{2,0,1:T(8,128)}, f32[128,8,128]{2,0,1:T(8,128)S(1)}, u32[]{:S(2)}) copy-start(f32[128,8,128]{2,0,1:T(8,128)S(1)} %copy.77) | copy-start | bytes 1572868
  143.0 5.0 %copy-start.3 = (f32[8,2,64,256]{3,2,1,0:T(8,128)}, f32[8,2,64,256]{3,2,1,0:T(8,128)S(1)}, u32[]{:S(2)}) copy-start(f32[8,2,64,256]{3,2,1,0:T(8,128)S(1)} %fusion.31) | copy-start | bytes 3145732
  148.1 14.1 %copy-start.5 = (bf16[128,8,128]{2,1,0:T(8,128)(2,1)S(1)}, bf16[128,8,128]{2,1,0:T(8,128)(2,1)}, u32[]{:S(2)}) copy-start(bf16[128,8,128]{2,1,0:T(8,128)(2,1)} %param.12) | copy-start | bytes 786436
  160.6 0.8 copy-start.1
  161.4 221.7 %all-gather.7.cloned.1.call-start = ((), (), s32[]{:S(2)}) async-start(), calls=%async_computation.1 | async-start | bytes 8912896 | tf_op jit(solution)/shard_map/all_gather | solution.py:14
  383.1 58.7 %copy-start.4 = (f32[8,2,64,256]{3,2,1,0:T(8,128)S(1)}, f32[8,2,64,256]{3,2,1,0:T(8,128)}, u32[]{:S(2)}) copy-start(f32[8,2,64,256]{3,2,1,0:T(8,128)} %copy-done.3) | copy-start | bytes 3145732
  438.5 11.7 %copy-start.6 = (bf16[128,8,128]{2,1,0:T(8,128)(2,1)S(1)}, bf16[128,8,128]{2,1,0:T(8,128)(2,1)}, u32[]{:S(2)}) copy-start(bf16[128,8,128]{2,1,0:T(8,128)(2,1)} %param.15) | copy-start | bytes 786436
Sparse Core Ops, SparseCore 0:
  161.5 108.2 all-gather.4
  272.6 110.4 all-gather.6
where the time goes:
time: 460 us; the launch traced here: 458 us
  waiting for transfers between devices  218 us (47%)
  other arithmetic  83.8 us (18%)
  matrix products  81.3 us (18%)
  blocking collectives  46 us (10%)
  between operations  15 us (3%)
  local copies, waits for them, and re-layouts  12.8 us (3%)
    all_gather x2, waiting for transfers between devices, entering(): pieces = jax.tree.map(lambda part: lax.all_gather(part, axis), value)  218 us
    another operation x4, other arithmetic, block_parts(): lax.linalg.triangular_solve(system, right_side, left_side=True, lower=Tru...  78.7 us
    dot_general x39, matrix products, matmul(): jnp.einsum('...ij,...jk->...ik', matrix, operand, precision=lax.Precision...  70 us
    psum x1, blocking collectives, on_device(): key_total = lax.psum(jnp.sum(key_float * key_float, axis=(0, 2)), 'seq')  43.5 us
  transfers between devices with their start and end apart: 2, of which 2 were waited for; matrix products, arithmetic and copies ran while one was open for 1% of the time, Pallas kernels for 0%

commit v1 on v0

v1 whole, which is shorter than its diff:
```python
import functools
import math

import jax
import jax.numpy as jnp
from jax import lax
from jax.experimental import pallas as pl
from jax.experimental.pallas import tpu as pltpu
from jax.sharding import PartitionSpec as P

BLOCK = 64
EPSILON = 1e-06
F32 = jnp.float32
BF16 = jnp.bfloat16
VMEM_LIMIT = 56 * 1024 * 1024


def split(x):
    high = x.astype(BF16)
    return high, (x - high.astype(F32)).astype(BF16)


def mm(a, b):
    return jnp.dot(a, b, preferred_element_type=F32)


def dot_split(left, right):
    (lh, ll), (rh, rl) = left, right
    return mm(jnp.concatenate([lh, ll], 1), jnp.concatenate([rh, rh], 0)) + mm(lh, rl)


def dot_square(left, right):
    (lh, ll), (rh, rl) = left, right
    n = rh.shape[1]
    wide = mm(
        jnp.concatenate([lh, ll], 1),
        jnp.concatenate(
            [jnp.concatenate([rh, rl], 1), jnp.concatenate([rh, jnp.zeros_like(rl)], 1)], 0
        ),
    )
    return wide[:, :n] + wide[:, n:]


def iotas(n, m):
    return (
        lax.broadcasted_iota(jnp.int32, (n, m), 0),
        lax.broadcasted_iota(jnp.int32, (n, m), 1),
    )


def vmem(count):
    return [pl.BlockSpec(memory_space=pltpu.VMEM)] * count


def smem():
    return pl.BlockSpec(memory_space=pltpu.SMEM)


def call(kernel, out_shape, scratch=(), scalars=0, operands=0, flops=0, name=None):
    single = not isinstance(out_shape, (list, tuple))
    return pl.pallas_call(
        kernel,
        out_shape=out_shape,
        in_specs=[smem()] * scalars + vmem(operands),
        out_specs=vmem(1)[0] if single else vmem(len(out_shape)),
        scratch_shapes=list(scratch),
        compiler_params=pltpu.CompilerParams(vmem_limit_bytes=VMEM_LIMIT),
        cost_estimate=pl.CostEstimate(flops=flops, bytes_accessed=1 << 20, transcendentals=0),
        name=name,
    )


def shape(*dims, dtype=F32):
    return jax.ShapeDtypeStruct(dims, dtype)


def stats_kernel(heads, key_ref, weight_ref, inputs_ref, total_ref, logits_ref):
    keys = key_ref[...].astype(F32)
    squares = keys * keys
    rows = squares.shape[0]
    total = squares.reshape(rows // heads, heads, squares.shape[1]).sum(0)
    total_ref[...] = total
    logits_ref[...] = lax.dot_general(
        weight_ref[...], inputs_ref[...], (((1,), (1,)), ((), ())), preferred_element_type=F32
    )


def gather_rows(source_ref, rows_ref, order, at):
    for item, head in enumerate(order):
        rows_ref[at + item : at + item + 1, :] = source_ref[pl.ds(head, 1), :]


def item_heads(rank_ref, groups, per):
    return [(slot ^ rank_ref[0]) * per + i for slot in range(groups) for i in range(per)]


def solve_kernel(
    groups,
    per,
    tokens_all,
    rank_ref,
    key_ref,
    value_ref,
    logit_ref,
    total_ref,
    decay_ref,
    maps_ref,
    wu_ref,
    cum_ref,
    flat_ref,
    rows_ref,
):
    heads = groups * per
    n = decay_ref.shape[1]
    d = key_ref.shape[1]
    order = item_heads(rank_ref, groups, per)
    row, col = iotas(n, n)
    lane = lax.broadcasted_iota(jnp.int32, (heads, n), 1)

    cum = decay_ref[...]
    step = 1
    while step < n:
        cum = cum + jnp.where(lane >= step, pltpu.roll(cum, step, 1), 0.0)
        step *= 2
    cum_ref[...] = cum
    limit = jnp.sqrt(jnp.sum(total_ref[...], 1, keepdims=True) / tokens_all + EPSILON)

    flat_ref[...] = key_ref[...].astype(F32)
    keys, keys_t, grams = [], [], []
    for item, head in enumerate(order):
        key = flat_ref[pl.ds(head, n, stride=heads), :].astype(BF16)
        keys.append(key)
        keys_t.append(key.T)
    for item in range(heads):
        gram = mm(keys[item], keys_t[item])
        grams.append(gram)
        rows_ref[item : item + 1, :] = jnp.sum(jnp.where(row == col, gram, 0.0), 0, keepdims=True)
    gather_rows(cum_ref, rows_ref, order, heads)
    rows_ref[2 * heads : 3 * heads, :] = 1.0 / (1.0 + jnp.exp(-logit_ref[...]))
    rows_ref[3 * heads : 4 * heads, :] = jnp.broadcast_to(limit, (heads, n))
    gather_rows(rows_ref, rows_ref, [2 * heads + h for h in order], 4 * heads)
    gather_rows(rows_ref, rows_ref, [3 * heads + h for h in order], 5 * heads)
    norm = rows_ref[0:heads, :]
    cum = rows_ref[heads : 2 * heads, :]
    beta = rows_ref[4 * heads : 5 * heads, :]
    inverse = 1.0 / jnp.maximum(jnp.sqrt(norm), rows_ref[5 * heads : 6 * heads, :])
    last = cum[:, n - 1 : n]
    carry = inverse * jnp.exp(last - cum)
    lift = jnp.exp(last)
    rows_ref[6 * heads : 7 * heads, :] = beta * inverse
    rows_ref[7 * heads : 8 * heads, :] = carry
    columns = rows_ref[...].T

    def column(kind, item):
        at = kind * heads + item
        return columns[:, at : at + 1]

    systems, inverses = [], []
    for item in range(heads):
        spread = column(1, item) - cum[item : item + 1, :]
        damping = jnp.exp(jnp.where(row > col, spread, 0.0))
        system = jnp.where(
            row > col,
            grams[item] * damping * column(6, item) * inverse[item : item + 1, :],
            0.0,
        )
        systems.append(split(system))
        inverses.append(
            jnp.where(row == col, 1.0, jnp.where((row ^ col) == 1, -system, 0.0))
        )
    size = 2
    while size < n:
        joins = ((row ^ col) & ~(2 * size - 1)) == 0
        joins = joins & ((row & size) != 0) & ((col & size) == 0)
        parts = [split(x) for x in inverses]
        mids = [split(dot_square(a, x)) for a, x in zip(systems, parts)]
        ends = [dot_square(x, t) for x, t in zip(parts, mids)]
        inverses = [x - jnp.where(joins, e, 0.0) for x, e in zip(inverses, ends)]
        size *= 2

    flat_ref[...] = value_ref[...].astype(F32)
    write_scale = beta * jnp.exp(cum) * inverse
    for item, head in enumerate(order):
        x = inverses[item]
        value = flat_ref[pl.ds(head, n, stride=heads), :].astype(BF16)
        key = keys[item]
        w = mm(
            jnp.concatenate(split(x * write_scale[item : item + 1, :]), 1),
            jnp.concatenate([key, key], 0),
        )
        u = mm(
            jnp.concatenate(split(x * beta[item : item + 1, :]), 1),
            jnp.concatenate([value, value], 0),
        )
        wu = jnp.concatenate([w, u], 1)
        wu_ref[item] = wu
        scaled = split(wu * column(7, item))
        both = mm(
            jnp.concatenate([keys_t[item], keys_t[item]], 1), jnp.concatenate(scaled, 0)
        )
        ends = jnp.where(row == col, lift[item : item + 1, :], 0.0)
        maps_ref[item // per, item % per] = jnp.concatenate([ends - both[:, :d], both[:, d:]], 1)


def output_kernel(
    groups,
    per,
    tokens_all,
    rank_ref,
    query_ref,
    key_ref,
    total_ref,
    cum_ref,
    wu_ref,
    left_ref,
    right_ref,
    flat_ref,
    rows_ref,
):
    heads = groups * per
    n = cum_ref.shape[1]
    d = key_ref.shape[1]
    blocks = n // BLOCK
    order = item_heads(rank_ref, groups, per)
    row, col = iotas(n, n)
    limit = jnp.sqrt(jnp.sum(total_ref[...], 1, keepdims=True) / tokens_all + EPSILON)
    rows_ref[0:heads, :] = jnp.broadcast_to(limit, (heads, n))
    gather_rows(rows_ref, rows_ref, order, heads)
    gather_rows(cum_ref, rows_ref, order, 2 * heads)
    limit = rows_ref[heads : 2 * heads, :]
    cum = rows_ref[2 * heads : 3 * heads, :]
    flat_ref[...] = key_ref[...].astype(F32)
    keys = [flat_ref[pl.ds(head, n, stride=heads), :] for head in order]
    flat_ref[...] = query_ref[...].astype(F32)
    queries = [flat_ref[pl.ds(head, n, stride=heads), :] for head in order]
    norms = []
    for item in range(heads):
        norms.append(jnp.sum(keys[item] * keys[item], 1, keepdims=True))
    position = lax.broadcasted_iota(jnp.int32, (heads, n), 1)
    kinds = [cum]
    for b in range(1, blocks):
        end = b * BLOCK
        kinds.append(
            jnp.where(position < end, jnp.exp(jnp.minimum(cum[:, end - 1 : end] - cum, 0.0)), 0.0)
        )
    kinds.append(limit)
    for at, kind in enumerate(kinds):
        rows_ref[at * heads : (at + 1) * heads, :] = kind
    columns = rows_ref[...].T
    spare = len(kinds) * heads
    inverse_columns = [
        1.0
        / jnp.maximum(
            jnp.sqrt(norms[item]),
            columns[:, (len(kinds) - 1) * heads + item : (len(kinds) - 1) * heads + item + 1],
        )
        for item in range(heads)
    ]
    for item in range(heads):
        wu = wu_ref[item]
        key = keys[item].astype(BF16)
        key_t = key.T
        query = queries[item]
        cum_column = columns[:, item : item + 1]
        inverse = inverse_columns[item]
        reach = (
            1.0
            / jnp.sqrt(jnp.sum(query * query, 1, keepdims=True) + EPSILON)
            * (d**-0.5)
        )
        scores = mm(query.astype(BF16), key_t)
        spread = jnp.where(row >= col, cum_column - cum[item : item + 1, :], 0.0)
        scores = jnp.where(row >= col, scores * jnp.exp(spread), 0.0) * reach
        scaled = split(wu * inverse)
        both = dot_split(split(scores), scaled)
        rest = [query * (reach * jnp.exp(cum_column)) - both[:, :d]]
        outs = [both[:, d:]]
        for b in range(1, blocks):
            carry = columns[:, b * heads + item : b * heads + item + 1]
            part = split(wu * (inverse * carry))
            inner = mm(jnp.concatenate([key_t, key_t], 1), jnp.concatenate(part, 0))
            at = b * BLOCK - 1
            ends = jnp.where(row == col, jnp.exp(cum[item : item + 1, at : at + 1]), 0.0)
            rest.append(ends - inner[:, :d])
            outs.append(inner[:, d:])
        left_ref[item] = jnp.concatenate(split(jnp.concatenate(rest, 0)), 1)
        right_ref[item] = jnp.concatenate(outs, 0)


def join(latter, earlier):
    d = latter.shape[0]
    both = dot_split(split(latter[:, :d]), split(earlier))
    return jnp.concatenate([both[:, :d], both[:, d:] + latter[:, d:]], 1)


def apply(step, state):
    d = state.shape[0]
    return dot_split(split(step[:, :d]), split(state)) + step[:, d:]


def compose_kernel(groups, per, rank_ref, *refs):
    parts, (prefix_ref, total_ref, held_ref) = refs[:groups], refs[groups:]
    for slot in range(groups):
        held_ref[slot ^ rank_ref[0]] = parts[slot][...]
    so_far = [held_ref[0, i] for i in range(per)]
    for place in range(1, groups):
        for i in range(per):
            prefix_ref[place - 1, i] = so_far[i]
        so_far = [join(held_ref[place, i], so_far[i]) for i in range(per)]
    for i in range(per):
        total_ref[i] = so_far[i]


def middle_kernel(per, upper_ref, mine_ref, other_ref, start_ref, state_ref):
    for i in range(per):
        mine, other = mine_ref[i], other_ref[i]
        upper = upper_ref[0] != 0
        earlier = jnp.where(upper, other, mine)
        latter = jnp.where(upper, mine, other)
        state_ref[i] = apply(latter, apply(earlier, start_ref[i]))


def enter_kernel(
    groups, per, rank_ref, upper_ref, later_ref, prefix_ref, before_ref, start_ref, came_ref, out_ref
):
    for i in range(per):
        state = jnp.where(later_ref[0] != 0, came_ref[i], start_ref[i])
        moved = apply(before_ref[i], state)
        state = jnp.where(upper_ref[0] != 0, moved, state)
        out_ref[rank_ref[0], i] = state
        for place in range(1, groups):
            out_ref[place ^ rank_ref[0], i] = apply(prefix_ref[place - 1, i], state)


def finish_kernel(groups, per, rank_ref, *refs):
    states = refs[:groups]
    left_ref, right_ref, gate_ref, out_ref, block_ref, flat_ref, gates_ref = refs[groups:]
    heads = groups * per
    order = item_heads(rank_ref, groups, per)
    d = gate_ref.shape[1]
    n = gate_ref.shape[0] // heads
    blocks = block_ref.shape[0]
    gates_ref[...] = gate_ref[...].astype(F32)
    for item, head in enumerate(order):
        state = states[item // per][item % per]
        high, low = split(state)
        left = left_ref[item]
        both = mm(left, jnp.concatenate([high, high], 0)) + mm(left[:, :d], low) + right_ref[item]
        raw = both[:n]
        block_ref[0, head] = state
        for b in range(1, blocks):
            block_ref[b, head] = both[n + (b - 1) * d : n + b * d]
        gate = gates_ref[pl.ds(head, n, stride=heads), :]
        scale = 1.0 / jnp.sqrt(jnp.mean(raw * raw, 1, keepdims=True) + EPSILON)
        flat_ref[pl.ds(head, n, stride=heads), :] = raw * scale * (gate / (1.0 + jnp.exp(-gate)))
    out_ref[...] = flat_ref[...].astype(BF16)


def exact(matrix, operand):
    return jnp.einsum("...ij,...jk->...ik", matrix, operand, precision=lax.Precision.HIGHEST)


def chain(latter, earlier):
    d = latter.shape[-2]
    both = exact(latter[..., :d], earlier)
    return jnp.concatenate([both[..., :d], both[..., d:] + latter[..., d:]], -1)


def flag(value):
    return jnp.reshape(value, (1,)).astype(jnp.int32)


def on_device(
    queries, key_vectors, values, out_gate, inputs, beta_weight, log_decay, initial_state
):
    n, heads, d = queries.shape
    blocks = n // BLOCK
    count, place = lax.axis_size("seq"), lax.axis_index("seq")
    groups = math.gcd(math.gcd(4, heads), count)
    per = heads // groups
    runs = count // groups
    rounds = runs.bit_length() - 1
    assert runs == 1 << rounds
    rank = flag(place % groups)
    run = place // groups

    def flipped(mask):
        return [(i, i ^ mask) for i in range(count)]

    def flat(tensor):
        return tensor.reshape(n * heads, d)

    total, logits = call(
        functools.partial(stats_kernel, heads),
        (shape(heads, d), shape(beta_weight.shape[0], n)),
        operands=3,
        name="stats",
    )(flat(key_vectors), beta_weight, inputs)
    if lax.axis_size("head") == 2:
        side = lax.axis_index("head")
        halves = logits.reshape(2, heads, n)
        own = lax.dynamic_index_in_dim(halves, side, 0, keepdims=False)
        theirs = lax.dynamic_index_in_dim(halves, 1 - side, 0, keepdims=False)
        logits = own + lax.ppermute(theirs, "head", [(0, 1), (1, 0)])
    else:
        logits = lax.psum_scatter(logits, "head", scatter_dimension=0, tiled=True)
    mask = 1
    while mask < count:
        total = total + lax.ppermute(total, "seq", flipped(mask))
        mask *= 2

    tokens_all = n * count
    maps, wu, cum = call(
        functools.partial(solve_kernel, groups, per, tokens_all),
        (shape(groups, per, d, 2 * d), shape(heads, n, 2 * d), shape(heads, n)),
        scratch=(pltpu.VMEM((n * heads, d), F32), pltpu.VMEM((128, n), F32)),
        scalars=1,
        operands=5,
        flops=1 << 30,
        name="solve",
    )(rank, flat(key_vectors), flat(values), logits, total, log_decay)

    parts = [maps[0]] + [
        lax.ppermute(maps[slot], "seq", flipped(slot)) for slot in range(1, groups)
    ]
    left, right = call(
        functools.partial(output_kernel, groups, per, tokens_all),
        (shape(heads, n + (blocks - 1) * d, 2 * d, dtype=BF16), shape(heads, n + (blocks - 1) * d, d)),
        scratch=(pltpu.VMEM((n * heads, d), F32), pltpu.VMEM((128, n), F32)),
        scalars=1,
        operands=5,
        flops=1 << 30,
        name="outputs",
    )(rank, flat(queries), flat(key_vectors), total, cum, wu)

    prefix, run_map = call(
        functools.partial(compose_kernel, groups, per),
        (shape(max(groups - 1, 1), per, d, 2 * d), shape(per, d, 2 * d)),
        scratch=(pltpu.VMEM((groups, per, d, 2 * d), F32),),
        scalars=1,
        operands=groups,
        flops=1 << 27,
        name="compose",
    )(rank, *parts)
    start = lax.dynamic_slice_in_dim(initial_state, (place % groups) * per, per, 0)

    before, upper, came, later = run_map, flag(0), start, flag(0)
    if rounds == 2:
        other = lax.ppermute(run_map, "seq", flipped(groups))
        upper = flag(run & 1)
        before = other
        middle = call(
            functools.partial(middle_kernel, per),
            shape(per, d, d),
            scalars=1,
            operands=3,
            name="middle",
        )(upper, run_map, other, start)
    elif rounds:
        eye = jnp.broadcast_to(jnp.eye(d, 2 * d, dtype=F32), run_map.shape)
        before, upper, window = eye, flag(1), run_map
        for r in range(rounds - 1):
            other = lax.ppermute(window, "seq", flipped(groups << r))
            high = (run >> r) & 1 == 1
            before = jnp.where(high, chain(before, other), before)
            window = chain(jnp.where(high, window, other), jnp.where(high, other, window))
        middle = exact(window[..., :d], start) + window[..., d:]
    if rounds:
        half = count // 2
        came = lax.ppermute(middle, "seq", [(i, i + half) for i in range(half)])
        later = flag(run >= runs // 2)
    entries = call(
        functools.partial(enter_kernel, groups, per),
        shape(groups, per, d, d),
        scalars=3,
        operands=4,
        flops=1 << 27,
        name="enter",
    )(rank, upper, later, prefix, before, start, came)

    states = [entries[0]] + [
        lax.ppermute(entries[slot], "seq", flipped(slot)) for slot in range(1, groups)
    ]
    gated, block_states = call(
        functools.partial(finish_kernel, groups, per),
        (shape(n * heads, d, dtype=BF16), shape(blocks, heads, d, d)),
        scratch=(pltpu.VMEM((n * heads, d), F32), pltpu.VMEM((n * heads, d), F32)),
        scalars=1,
        operands=groups + 3,
        flops=1 << 28,
        name="finish",
    )(rank, *states, left, right, flat(out_gate))
    return (gated.reshape(n, heads, d), block_states)


def solution(mesh):
    return jax.shard_map(
        on_device,
        mesh=mesh,
        in_specs=(
            P("seq", "head", None),
            P("seq", "head", None),
            P("seq", "head", None),
            P("seq", "head", None),
            P("seq", "head"),
            P(None, "head"),
            P("head", "seq"),
            P("head", None, None),
        ),
        out_specs=(P("seq", "head", None), P("seq", "head", None, None)),
        check_vma=False,
    )
```

time: 460 us -> 81 us (0.18)
  waiting for transfers between devices: 218 us -> 23.8 us
  other arithmetic: 83.8 us -> 1.88 us
  matrix products: 81.3 us -> 0 us
  blocking collectives: 46 us -> 0 us
  Pallas kernels: 0 us -> 25.1 us
  starting transfers between devices: 0.26 us -> 21.9 us
  between operations: 15 us -> 0.7 us
  local copies, waits for them, and re-layouts: 12.8 us -> 7.12 us
    all_gather x2 -> x0, waiting for transfers between devices: 218 us -> none  [entering(): pieces = jax.tree.map(lambda part: lax.all_gather(part, axis), value)]
    dot_general x44 -> x0, matrix products: 80.2 us -> none  [the longest x39 70 us: matmul(): jnp.einsum('...ij,...jk->...ik', matrix, operand, precision=lax.Precision...]
    another operation x7 -> x0, other arithmetic: 79.2 us -> none  [the longest x4 78.7 us: block_parts(): lax.linalg.triangular_solve(system, right_side, left_side=True, lower=Tru...]
    psum x1 -> x0, blocking collectives: 43.5 us -> none  [on_device(): key_total = lax.psum(jnp.sum(key_float * key_float, axis=(0, 2)), 'seq')]
    pallas_call x0 -> x7, Pallas kernels: none -> 25.1 us  [the longest x1 7.35 us: on_device(): call(functools.partial(solve_kernel, groups, per, tokens_all), (shape(gro...]
    ppermute x0 -> x13, waiting for transfers between devices: none -> 23.8 us  [the longest x3 9 us: on_device(): lax.ppermute(maps[slot], 'seq', flipped(slot))]
    ppermute x0 -> x13, starting transfers between devices: none -> 21.9 us  [the longest x4 10.1 us: on_device(): total = total + lax.ppermute(total, 'seq', flipped(mask))]
  transfers between devices with their start and end apart: 2 -> 13, of which waited for: 2 -> 10; matrix products, arithmetic and copies ran while one was open for 1% -> 2% of each run, Pallas kernels for 0% -> 6%
where the time goes in v1:
time: 81 us; the launch traced here: 80.6 us
  Pallas kernels  25.1 us (31%)
  waiting for transfers between devices  23.8 us (29%)
  starting transfers between devices  21.9 us (27%)
  local copies, waits for them, and re-layouts  7.12 us (9%)
  other arithmetic  1.88 us (2%)
    ppermute x4, starting transfers between devices, on_device(): total = total + lax.ppermute(total, 'seq', flipped(mask))  10.1 us
    ppermute x3, waiting for transfers between devices, on_device(): lax.ppermute(maps[slot], 'seq', flipped(slot))  9 us
    pallas_call x1, Pallas kernels, on_device(): call(functools.partial(solve_kernel, groups, per, tokens_all), (shape(gro...  7.35 us
    ppermute x4, waiting for transfers between devices, on_device(): total = total + lax.ppermute(total, 'seq', flipped(mask))  5.94 us
    ppermute x1, waiting for transfers between devices, on_device(): other = lax.ppermute(run_map, 'seq', flipped(groups))  5.93 us
    pallas_call x1, Pallas kernels, on_device(): call(functools.partial(output_kernel, groups, per, tokens_all), (shape(he...  4.76 us
    ppermute x1, starting transfers between devices, on_device(): came = lax.ppermute(middle, 'seq', [(i, i + half) for i in range(half)])  4.32 us
    pallas_call x1, Pallas kernels, on_device(): call(functools.partial(finish_kernel, groups, per), (shape(n * heads, d,...  3.59 us
  transfers between devices with their start and end apart: 13, of which 10 were waited for; matrix products, arithmetic and copies ran while one was open for 2% of the time, Pallas kernels for 6%

profile of v1, /device:TPU:0, one launch (start us, length us, event | category | flops | bytes accessed | tf_op | source)
XLA Modules:
  0.0 80.6 jit_solution(4106846320569488728)
XLA Ops:
  0.6 0.0 copy-start
  0.6 1.9 %stats.1 = (f32[8,128]{1,0:T(8,128)}, f32[16,128]{1,0:T(8,128)}) custom-call(bf16[1024,128]{1,0:T(8,128)(2,1)} %bitcast.30, bf16[16,1024]{1,0:T(8,128)(2,1)} %weight_ref.1, bf16[128,1024]{1,0:T(8,128)(2,1)} %inputs_ref.1), custom_call_target="tpu_custom_call" | custom-call | bytes 1048576 | tf_op jit(solution)/shard_map/stats/pallas_call | solution.py:393
  2.5 3.0 %collective-permute-start.1 = (f32[8,128]{1,0:T(8,128)}, f32[8,128]{1,0:T(8,128)S(1)}, u32[]{:S(2)}, u32[]{:S(2)}) collective-permute-start(f32[8,128]{1,0:T(8,128)} %get-tuple-element.14), channel_id=1, source_target_pairs={{0,2},{2,0},{4,6},{6,4},{8,10},{10,8},{12,14},{14,12},{16,18},{18,... | collective-permute-start | bytes 12296 | tf_op jit(solution)/shard_map/ppermute | solution.py:409
  5.5 1.8 %collective-permute-done.1 = f32[8,128]{1,0:T(8,128)S(1)} collective-permute-done((f32[8,128]{1,0:T(8,128)}, f32[8,128]{1,0:T(8,128)S(1)}, u32[]{:S(2)}, u32[]{:S(2)}) %collective-permute-start.1) | collective-permute-done | bytes 4128 | tf_op jit(solution)/shard_map/ppermute | solution.py:409
  7.3 0.7 add.36
  8.0 2.1 %collective-permute-start.2 = (f32[8,128]{1,0:T(8,128)S(1)}, f32[8,128]{1,0:T(8,128)S(1)}, u32[]{:S(2)}, u32[]{:S(2)}) collective-permute-start(f32[8,128]{1,0:T(8,128)S(1)} %add.36), channel_id=1, source_target_pairs={{0,4},{2,6},{4,0},{6,2},{8,12},{10,14},{12,8},{14,10},{16,20},{18,... | collective-permute-start | bytes 12296 | tf_op jit(solution)/shard_map/ppermute | solution.py:409
  10.0 0.0 copy-start.9
  10.0 1.6 %collective-permute-done.2 = f32[8,128]{1,0:T(8,128)S(1)} collective-permute-done((f32[8,128]{1,0:T(8,128)S(1)}, f32[8,128]{1,0:T(8,128)S(1)}, u32[]{:S(2)}, u32[]{:S(2)}) %collective-permute-start.2) | collective-permute-done | bytes 4128 | tf_op jit(solution)/shard_map/ppermute | solution.py:409
  11.6 2.1 %collective-permute-start.3 = (f32[8,128]{1,0:T(8,128)S(1)}, f32[8,128]{1,0:T(8,128)S(1)}, u32[]{:S(2)}, u32[]{:S(2)}) collective-permute-start(f32[8,128]{1,0:T(8,128)S(1)} %add.37), channel_id=1, source_target_pairs={{0,8},{2,10},{4,12},{6,14},{8,0},{10,2},{12,4},{14,6},{16,24},{18,... | collective-permute-start | bytes 12296 | tf_op jit(solution)/shard_map/ppermute | solution.py:409
  13.7 0.0 copy-done.9
  13.7 0.0 collective-permute-start
  13.7 1.6 %collective-permute-done.3 = f32[8,128]{1,0:T(8,128)S(1)} collective-permute-done((f32[8,128]{1,0:T(8,128)S(1)}, f32[8,128]{1,0:T(8,128)S(1)}, u32[]{:S(2)}, u32[]{:S(2)}) %collective-permute-start.3) | collective-permute-done | bytes 4128 | tf_op jit(solution)/shard_map/ppermute | solution.py:409
  15.3 3.0 %collective-permute-start.4 = (f32[8,128]{1,0:T(8,128)S(1)}, f32[8,128]{1,0:T(8,128)S(1)}, u32[]{:S(2)}, u32[]{:S(2)}) collective-permute-start(f32[8,128]{1,0:T(8,128)S(1)} %add.38), channel_id=1, source_target_pairs={{0,16},{2,18},{4,20},{6,22},{8,24},{10,26},{12,28},{14,30},{16,0},... | collective-permute-start | bytes 12296 | tf_op jit(solution)/shard_map/ppermute | solution.py:409
  18.3 0.0 collective-permute-done
  18.3 0.6 bitcast_add_fusion.logit_ref
  18.9 1.0 %collective-permute-done.4 = f32[8,128]{1,0:T(8,128)S(1)} collective-permute-done((f32[8,128]{1,0:T(8,128)S(1)}, f32[8,128]{1,0:T(8,128)S(1)}, u32[]{:S(2)}, u32[]{:S(2)}) %collective-permute-start.4) | collective-permute-done | bytes 4128 | tf_op jit(solution)/shard_map/ppermute | solution.py:409
  19.9 0.6 add.39.total_ref
  20.5 7.3 %solve.1 = (f32[4,2,128,256]{3,2,1,0:T(8,128)}, f32[8,128,256]{2,1,0:T(8,128)}, f32[8,128]{1,0:T(8,128)}) custom-call(s32[1]{0:T(128)} %bitcast.rank_ref, bf16[1024,128]{1,0:T(8,128)(2,1)} %bitcast.31, bf16[1024,128]{1,0:T(8,128)(2,1)} %bitcast.35, f32[8,128]{1,0:T(8,128)} %bitcast_add_fusion.logit_ref, f32[8,128]{1,0:T(8,128)} %add.39.total_ref, ...), custom_call_target="tpu_custom_call" | custom-call | flops 1073741824 | bytes 1048576 | tf_op jit(solution)/shard_map/solve/pallas_call | solution.py:413
  27.9 2.0 %slice_bitcast_fusion = (f32[2,128,256]{2,1,0:T(8,128)S(1)}, f32[2,128,256]{2,1,0:T(8,128)S(1)}, f32[2,128,256]{2,1,0:T(8,128)S(1)}, f32[2,128,256]{2,1,0:T(8,128)}) fusion(f32[4,2,128,256]{3,2,1,0:T(8,128)} %get-tuple-element.15), kind=kLoop, calls=%fused_computation | loop fusion | bytes 2097152 | tf_op jit(solution)/shard_map/squeeze | solution.py:424
  29.8 2.8 %collective-permute-start.7 = (f32[2,128,256]{2,1,0:T(8,128)S(1)}, f32[2,128,256]{2,1,0:T(8,128)S(1)}, u32[]{:S(2)}, u32[]{:S(2)}) collective-permute-start(f32[2,128,256]{2,1,0:T(8,128)S(1)} %get-tuple-element.24), channel_id=1, source_target_pairs={{0,6},{2,4},{4,2},{6,0},{8,14},{10,12},{12,10},{14,8},{16,22},{18,... | collective-permute-start | bytes 786440 | tf_op jit(solution)/shard_map/ppermute | solution.py:424
  32.6 0.5 collective-permute-start.6
  33.1 0.2 collective-permute-start.5
  33.3 6.1 %collective-permute-done.7.refs_3_ = f32[2,128,256]{2,1,0:T(8,128)S(1)} collective-permute-done((f32[2,128,256]{2,1,0:T(8,128)S(1)}, f32[2,128,256]{2,1,0:T(8,128)S(1)}, u32[]{:S(2)}, u32[]{:S(2)}) %collective-permute-start.7) | collective-permute-done | bytes 262176 | tf_op jit(solution)/shard_map/ppermute | solution.py:424
  39.4 0.0 copy-start.2
  39.4 2.8 %collective-permute-done.6.refs_2_ = f32[2,128,256]{2,1,0:T(8,128)S(1)} collective-permute-done((f32[2,128,256]{2,1,0:T(8,128)S(1)}, f32[2,128,256]{2,1,0:T(8,128)S(1)}, u32[]{:S(2)}, u32[]{:S(2)}) %collective-permute-start.6) | collective-permute-done | bytes 262176 | tf_op jit(solution)/shard_map/ppermute | solution.py:424
  42.2 0.0 copy-start.3
  42.2 0.1 collective-permute-done.5.refs_1_
  42.3 0.0 copy-start.4
  42.3 0.0 copy-done.2
  42.3 0.6 copy-done.3
  42.9 0.1 copy-done.4
  43.0 2.7 %compose.1 = (f32[3,2,128,256]{3,2,1,0:T(8,128)}, f32[2,128,256]{2,1,0:T(8,128)}) custom-call(s32[1]{0:T(128)} %bitcast.rank_ref, f32[2,128,256]{2,1,0:T(8,128)} %get-tuple-element.27.refs_0_, f32[2,128,256]{2,1,0:T(8,128)} %copy-done.4, f32[2,128,256]{2,1,0:T(8,128)} %copy-done.3, f32[2,128,256]{2,1,0:T(8,128)} %copy-done.2), custom_call_target="tpu_custom_call" | custom-call | flops 134217728 | bytes 1048576 | tf_op jit(solution)/shard_map/compose/pallas_call | solution.py:436
  45.7 0.5 collective-permute-start.8
  46.2 0.0 copy-done
  46.2 0.7 constant_dynamic-slice_fusion.start_ref
  46.8 5.9 %collective-permute-done.8.other_ref.before_ref = f32[2,128,256]{2,1,0:T(8,128)S(1)} collective-permute-done((f32[2,128,256]{2,1,0:T(8,128)}, f32[2,128,256]{2,1,0:T(8,128)S(1)}, u32[]{:S(2)}, u32[]{:S(2)}) %collective-permute-start.8) | collective-permute-done | bytes 262176 | tf_op jit(solution)/shard_map/ppermute | solution.py:449
  52.8 0.0 copy-start.1
  52.8 0.7 copy-done.1
  53.5 2.1 %middle.1 = f32[2,128,128]{2,1,0:T(8,128)} custom-call(s32[1]{0:T(128)} %bitcast.1.upper_ref, f32[2,128,256]{2,1,0:T(8,128)} %get-tuple-element.17.mine_ref, f32[2,128,256]{2,1,0:T(8,128)} %copy-done.1, f32[2,128,128]{2,1,0:T(8,128)} %constant_dynamic-slice_fusion.start_ref), custom_call_target="tpu_custom_call" | custom-call | bytes 1048576 | tf_op jit(solution)/shard_map/middle/pallas_call | solution.py:452
  55.6 4.3 %collective-permute-start.9 = (f32[2,128,128]{2,1,0:T(8,128)}, f32[2,128,128]{2,1,0:T(8,128)S(1)}, u32[]{:S(2)}, u32[]{:S(2)}) collective-permute-start(f32[2,128,128]{2,1,0:T(8,128)} %middle.1), channel_id=1, source_target_pairs={{0,16},{2,18},{4,20},{6,22},{8,24},{10,26},{12,28},{14,30},{1,17},... | collective-permute-start | bytes 393224 | tf_op jit(solution)/shard_map/ppermute | solution.py:470
  59.9 2.8 %collective-permute-done.9.came_ref = f32[2,128,128]{2,1,0:T(8,128)S(1)} collective-permute-done((f32[2,128,128]{2,1,0:T(8,128)}, f32[2,128,128]{2,1,0:T(8,128)S(1)}, u32[]{:S(2)}, u32[]{:S(2)}) %collective-permute-start.9) | collective-permute-done | bytes 131104 | tf_op jit(solution)/shard_map/ppermute | solution.py:470
  62.7 0.0 copy-start.8
  62.7 0.6 copy-done.8
  63.4 2.7 %enter.1 = f32[4,2,128,128]{3,2,1,0:T(8,128)} custom-call(s32[1]{0:T(128)} %bitcast.rank_ref, s32[1]{0:T(128)} %bitcast.1.upper_ref, s32[1]{0:T(128)} %bitcast.2.later_ref, f32[3,2,128,256]{3,2,1,0:T(8,128)} %get-tuple-element.16.prefix_ref, f32[2,128,256]{2,1,0:T(8,128)} %copy-done.1, f32[2,128,128]{2,1,0:T(8,128)} %constant_dynamic-slice_fusion.start_ref, ...), custom_call_target="tpu_custom_call" | custom-call | flops 134217728 | bytes 1048576 | tf_op jit(solution)/shard_map/enter/pallas_call | solution.py:472
  66.1 1.8 %slice_bitcast_fusion.4 = (f32[2,128,128]{2,1,0:T(8,128)S(1)}, f32[2,128,128]{2,1,0:T(8,128)S(1)}, f32[2,128,128]{2,1,0:T(8,128)S(1)}, f32[2,128,128]{2,1,0:T(8,128)}) fusion(f32[4,2,128,128]{3,2,1,0:T(8,128)} %enter.1), kind=kLoop, calls=%fused_computation.4 | loop fusion | bytes 1048576 | tf_op jit(solution)/shard_map/squeeze | solution.py:482
  67.9 2.2 %collective-permute-start.12 = (f32[2,128,128]{2,1,0:T(8,128)S(1)}, f32[2,128,128]{2,1,0:T(8,128)S(1)}, u32[]{:S(2)}, u32[]{:S(2)}) collective-permute-start(f32[2,128,128]{2,1,0:T(8,128)S(1)} %get-tuple-element.28), channel_id=1, source_target_pairs={{0,6},{2,4},{4,2},{6,0},{8,14},{10,12},{12,10},{14,8},{16,22},{18,... | collective-permute-start | bytes 393224 | tf_op jit(solution)/shard_map/ppermute | solution.py:482
  70.2 1.2 %collective-permute-start.11 = (f32[2,128,128]{2,1,0:T(8,128)S(1)}, f32[2,128,128]{2,1,0:T(8,128)S(1)}, u32[]{:S(2)}, u32[]{:S(2)}) collective-permute-start(f32[2,128,128]{2,1,0:T(8,128)S(1)} %get-tuple-element.29), channel_id=1, source_target_pairs={{0,4},{2,6},{4,0},{6,2},{8,12},{10,14},{12,8},{14,10},{16,20},{18,... | collective-permute-start | bytes 393224 | tf_op jit(solution)/shard_map/ppermute | solution.py:482
  71.4 0.1 collective-permute-start.10
  71.4 4.8 %outputs.1 = (bf16[8,256,256]{2,1,0:T(8,128)(2,1)}, f32[8,256,128]{2,1,0:T(8,128)}) custom-call(s32[1]{0:T(128)} %bitcast.rank_ref, bf16[1024,128]{1,0:T(8,128)(2,1)} %bitcast.36, bf16[1024,128]{1,0:T(8,128)(2,1)} %bitcast.32, f32[8,128]{1,0:T(8,128)} %add.39.total_ref, f32[8,128]{1,0:T(8,128)} %get-tuple-element.18.cum_ref, ...), custom_call_target="tpu_custom_call" | custom-call | flops 1073741824 | bytes 1048576 | tf_op jit(solution)/shard_map/outputs/pallas_call | solution.py:426
  76.2 0.0 collective-permute-done.12.refs_3_
  76.2 0.0 copy-start.5
  76.2 0.0 collective-permute-done.11.refs_2_
  76.2 0.0 copy-start.6
  76.2 0.1 collective-permute-done.10.refs_1_
  76.3 0.0 copy-start.7
  76.3 0.5 copy-done.5
  76.8 0.1 copy-done.6
  76.9 0.1 copy-done.7
  77.0 3.6 %finish.1 = (bf16[1024,128]{1,0:T(8,128)(2,1)}, f32[2,8,128,128]{3,2,1,0:T(8,128)}) custom-call(s32[1]{0:T(128)} %bitcast.rank_ref, f32[2,128,128]{2,1,0:T(8,128)} %get-tuple-element.31.refs_0_, f32[2,128,128]{2,1,0:T(8,128)} %copy-done.7, f32[2,128,128]{2,1,0:T(8,128)} %copy-done.6, f32[2,128,128]{2,1,0:T(8,128)} %copy-done.5, ...), custom_call_target="tpu_custom_call" | custom-call | flops 268435456 | bytes 1048576 | tf_op jit(solution)/shard_map/finish/pallas_call | solution.py:484
  (3 shorter events, 0.0 us)
Async XLA Ops:
  0.6 45.5 %copy-start = (f32[8,128,128]{2,1,0:T(8,128)S(1)}, f32[8,128,128]{2,1,0:T(8,128)}, u32[]{:S(2)}) copy-start(f32[8,128,128]{2,1,0:T(8,128)} %param.15) | copy-start | bytes 1572868
  2.5 4.8 %collective-permute-start.1 = (f32[8,128]{1,0:T(8,128)}, f32[8,128]{1,0:T(8,128)S(1)}, u32[]{:S(2)}, u32[]{:S(2)}) collective-permute-start(f32[8,128]{1,0:T(8,128)} %get-tuple-element.14), channel_id=1, source_target_pairs={{0,2},{2,0},{4,6},{6,4},{8,10},{10,8},{12,14},{14,12},{16,18},{18,... | collective-permute-start | bytes 12296 | tf_op jit(solution)/shard_map/ppermute | solution.py:409
  8.0 3.6 %collective-permute-start.2 = (f32[8,128]{1,0:T(8,128)S(1)}, f32[8,128]{1,0:T(8,128)S(1)}, u32[]{:S(2)}, u32[]{:S(2)}) collective-permute-start(f32[8,128]{1,0:T(8,128)S(1)} %add.36), channel_id=1, source_target_pairs={{0,4},{2,6},{4,0},{6,2},{8,12},{10,14},{12,8},{14,10},{16,20},{18,... | collective-permute-start | bytes 12296 | tf_op jit(solution)/shard_map/ppermute | solution.py:409
  10.0 3.7 %copy-start.9 = (f32[16,128]{1,0:T(8,128)S(1)}, f32[16,128]{1,0:T(8,128)}, u32[]{:S(2)}) copy-start(f32[16,128]{1,0:T(8,128)} %get-tuple-element.13) | copy-start | bytes 24580
  11.6 3.7 %collective-permute-start.3 = (f32[8,128]{1,0:T(8,128)S(1)}, f32[8,128]{1,0:T(8,128)S(1)}, u32[]{:S(2)}, u32[]{:S(2)}) collective-permute-start(f32[8,128]{1,0:T(8,128)S(1)} %add.37), channel_id=1, source_target_pairs={{0,8},{2,10},{4,12},{6,14},{8,0},{10,2},{12,4},{14,6},{16,24},{18,... | collective-permute-start | bytes 12296 | tf_op jit(solution)/shard_map/ppermute | solution.py:409
  13.7 4.6 %collective-permute-start = (f32[8,128]{1,0:T(8,128)S(1)}, f32[8,128]{1,0:T(8,128)S(1)}, u32[]{:S(2)}, u32[]{:S(2)}) collective-permute-start(f32[8,128]{1,0:T(8,128)S(1)} %dynamic-slice_bitcast_fusion), channel_id=1, source_target_pairs={{0,1},{1,0},{2,3},{3,2},{4,5},{5,4},{6,7},{7,6},{8,9},{9,8},{10,11... | collective-permute-start | bytes 12296 | tf_op jit(solution)/shard_map/ppermute | solution.py:404
  15.3 4.6 %collective-permute-start.4 = (f32[8,128]{1,0:T(8,128)S(1)}, f32[8,128]{1,0:T(8,128)S(1)}, u32[]{:S(2)}, u32[]{:S(2)}) collective-permute-start(f32[8,128]{1,0:T(8,128)S(1)} %add.38), channel_id=1, source_target_pairs={{0,16},{2,18},{4,20},{6,22},{8,24},{10,26},{12,28},{14,30},{16,0},... | collective-permute-start | bytes 12296 | tf_op jit(solution)/shard_map/ppermute | solution.py:409
  29.8 9.6 %collective-permute-start.7 = (f32[2,128,256]{2,1,0:T(8,128)S(1)}, f32[2,128,256]{2,1,0:T(8,128)S(1)}, u32[]{:S(2)}, u32[]{:S(2)}) collective-permute-start(f32[2,128,256]{2,1,0:T(8,128)S(1)} %get-tuple-element.24), channel_id=1, source_target_pairs={{0,6},{2,4},{4,2},{6,0},{8,14},{10,12},{12,10},{14,8},{16,22},{18,... | collective-permute-start | bytes 786440 | tf_op jit(solution)/shard_map/ppermute | solution.py:424
  32.6 9.6 %collective-permute-start.6 = (f32[2,128,256]{2,1,0:T(8,128)S(1)}, f32[2,128,256]{2,1,0:T(8,128)S(1)}, u32[]{:S(2)}, u32[]{:S(2)}) collective-permute-start(f32[2,128,256]{2,1,0:T(8,128)S(1)} %get-tuple-element.25), channel_id=1, source_target_pairs={{0,4},{2,6},{4,0},{6,2},{8,12},{10,14},{12,8},{14,10},{16,20},{18,... | collective-permute-start | bytes 786440 | tf_op jit(solution)/shard_map/ppermute | solution.py:424
  33.1 9.2 %collective-permute-start.5 = (f32[2,128,256]{2,1,0:T(8,128)S(1)}, f32[2,128,256]{2,1,0:T(8,128)S(1)}, u32[]{:S(2)}, u32[]{:S(2)}) collective-permute-start(f32[2,128,256]{2,1,0:T(8,128)S(1)} %get-tuple-element.26), channel_id=1, source_target_pairs={{0,2},{2,0},{4,6},{6,4},{8,10},{10,8},{12,14},{14,12},{16,18},{18,... | collective-permute-start | bytes 786440 | tf_op jit(solution)/shard_map/ppermute | solution.py:424
  39.4 2.9 %copy-start.2 = (f32[2,128,256]{2,1,0:T(8,128)}, f32[2,128,256]{2,1,0:T(8,128)S(1)}, u32[]{:S(2)}) copy-start(f32[2,128,256]{2,1,0:T(8,128)S(1)} %collective-permute-done.7.refs_3_) | copy-start | bytes 786436
  42.2 0.7 copy-start.3
  42.3 0.7 copy-start.4
  45.7 7.1 %collective-permute-start.8 = (f32[2,128,256]{2,1,0:T(8,128)}, f32[2,128,256]{2,1,0:T(8,128)S(1)}, u32[]{:S(2)}, u32[]{:S(2)}) collective-permute-start(f32[2,128,256]{2,1,0:T(8,128)} %get-tuple-element.17.mine_ref), channel_id=1, source_target_pairs={{0,8},{2,10},{4,12},{6,14},{8,0},{10,2},{12,4},{14,6},{16,24},{18,... | collective-permute-start | bytes 786440 | tf_op jit(solution)/shard_map/ppermute | solution.py:449
  52.8 0.7 copy-start.1
  55.6 7.2 %collective-permute-start.9 = (f32[2,128,128]{2,1,0:T(8,128)}, f32[2,128,128]{2,1,0:T(8,128)S(1)}, u32[]{:S(2)}, u32[]{:S(2)}) collective-permute-start(f32[2,128,128]{2,1,0:T(8,128)} %middle.1), channel_id=1, source_target_pairs={{0,16},{2,18},{4,20},{6,22},{8,24},{10,26},{12,28},{14,30},{1,17},... | collective-permute-start | bytes 393224 | tf_op jit(solution)/shard_map/ppermute | solution.py:470
  62.7 0.7 copy-start.8
  67.9 8.3 %collective-permute-start.12 = (f32[2,128,128]{2,1,0:T(8,128)S(1)}, f32[2,128,128]{2,1,0:T(8,128)S(1)}, u32[]{:S(2)}, u32[]{:S(2)}) collective-permute-start(f32[2,128,128]{2,1,0:T(8,128)S(1)} %get-tuple-element.28), channel_id=1, source_target_pairs={{0,6},{2,4},{4,2},{6,0},{8,14},{10,12},{12,10},{14,8},{16,22},{18,... | collective-permute-start | bytes 393224 | tf_op jit(solution)/shard_map/ppermute | solution.py:482
  70.2 6.0 %collective-permute-start.11 = (f32[2,128,128]{2,1,0:T(8,128)S(1)}, f32[2,128,128]{2,1,0:T(8,128)S(1)}, u32[]{:S(2)}, u32[]{:S(2)}) collective-permute-start(f32[2,128,128]{2,1,0:T(8,128)S(1)} %get-tuple-element.29), channel_id=1, source_target_pairs={{0,4},{2,6},{4,0},{6,2},{8,12},{10,14},{12,8},{14,10},{16,20},{18,... | collective-permute-start | bytes 393224 | tf_op jit(solution)/shard_map/ppermute | solution.py:482
  71.4 5.0 %collective-permute-start.10 = (f32[2,128,128]{2,1,0:T(8,128)S(1)}, f32[2,128,128]{2,1,0:T(8,128)S(1)}, u32[]{:S(2)}, u32[]{:S(2)}) collective-permute-start(f32[2,128,128]{2,1,0:T(8,128)S(1)} %get-tuple-element.30), channel_id=1, source_target_pairs={{0,2},{2,0},{4,6},{6,4},{8,10},{10,8},{12,14},{14,12},{16,18},{18,... | collective-permute-start | bytes 393224 | tf_op jit(solution)/shard_map/ppermute | solution.py:482
  76.2 0.6 copy-start.5
  76.2 0.7 copy-start.6
  76.3 0.7 copy-start.7

commit v2 on v1

--- a/solution.py
+++ b/solution.py
@@ -12,7 +12,7 @@
 EPSILON = 1e-06
 F32 = jnp.float32
 BF16 = jnp.bfloat16
-VMEM_LIMIT = 56 * 1024 * 1024
+VMEM_LIMIT = 20 * 1024 * 1024
 
 
 def split(x):
@@ -104,12 +104,9 @@
     logit_ref,
     total_ref,
     decay_ref,
-    maps_ref,
-    wu_ref,
-    cum_ref,
-    flat_ref,
-    rows_ref,
+    *refs,
 ):
+    maps_refs, (wu_ref, cum_ref, flat_ref, rows_ref) = refs[:groups], refs[groups:]
     heads = groups * per
     n = decay_ref.shape[1]
     d = key_ref.shape[1]
@@ -199,7 +196,7 @@
             jnp.concatenate([keys_t[item], keys_t[item]], 1), jnp.concatenate(scaled, 0)
         )
         ends = jnp.where(row == col, lift[item : item + 1, :], 0.0)
-        maps_ref[item // per, item % per] = jnp.concatenate([ends - both[:, :d], both[:, d:]], 1)
+        maps_refs[item // per][item % per] = jnp.concatenate([ends - both[:, :d], both[:, d:]], 1)
 
 
 def output_kernel(
@@ -321,8 +318,9 @@
 
 
 def enter_kernel(
-    groups, per, rank_ref, upper_ref, later_ref, prefix_ref, before_ref, start_ref, came_ref, out_ref
+    groups, per, rank_ref, upper_ref, later_ref, prefix_ref, before_ref, start_ref, came_ref, *refs
 ):
+    out_refs, out_ref = refs[:groups], refs[groups]
     for i in range(per):
         state = jnp.where(later_ref[0] != 0, came_ref[i], start_ref[i])
         moved = apply(before_ref[i], state)
@@ -330,6 +328,8 @@
         out_ref[rank_ref[0], i] = state
         for place in range(1, groups):
             out_ref[place ^ rank_ref[0], i] = apply(prefix_ref[place - 1, i], state)
+    for slot in range(groups):
+        out_refs[slot][...] = out_ref[slot]
 
 
 def finish_kernel(groups, per, rank_ref, *refs):
@@ -410,9 +410,9 @@
         mask *= 2
 
     tokens_all = n * count
-    maps, wu, cum = call(
+    *maps, wu, cum = call(
         functools.partial(solve_kernel, groups, per, tokens_all),
-        (shape(groups, per, d, 2 * d), shape(heads, n, 2 * d), shape(heads, n)),
+        [shape(per, d, 2 * d)] * groups + [shape(heads, n, 2 * d), shape(heads, n)],
         scratch=(pltpu.VMEM((n * heads, d), F32), pltpu.VMEM((128, n), F32)),
         scalars=1,
         operands=5,
@@ -471,7 +471,8 @@
         later = flag(run >= runs // 2)
     entries = call(
         functools.partial(enter_kernel, groups, per),
-        shape(groups, per, d, d),
+        [shape(per, d, d)] * groups,
+        scratch=(pltpu.VMEM((groups, per, d, d), F32),),
         scalars=3,
         operands=4,
         flops=1 << 27,

time: 81 us -> 64 us (0.79)
  Pallas kernels: 25.1 us -> 11.2 us
  local copies, waits for them, and re-layouts: 7.12 us -> 2.75 us
  waiting for transfers between devices: 23.8 us -> 26.2 us
  other arithmetic: 1.88 us -> 0.02 us
    pallas_call x2, Pallas kernels: 10.1 us -> 5.88 us  [the longest x1 5.16 us: on_device(): call(functools.partial(solve_kernel, groups, per, tokens_all), [shape(per...]
    squeeze x2 -> x0, local copies, waits for them, and re-layouts: 3.74 us -> none  [the longest x1 1.96 us: on_device(): maps[slot]]
    pallas_call x1, Pallas kernels: 4.76 us -> 2.12 us  [on_device(): call(functools.partial(output_kernel, groups, per, tokens_all), (shape(he...]
    ppermute x3, waiting for transfers between devices: 0.13 us -> 2.29 us  [on_device(): lax.ppermute(entries[slot], 'seq', flipped(slot))]
    pallas_call x1, Pallas kernels: 2.66 us -> 0.72 us  [on_device(): call(functools.partial(compose_kernel, groups, per), (shape(max(groups -...]
    pallas_call x1, Pallas kernels: 3.59 us -> 1.85 us  [on_device(): call(functools.partial(finish_kernel, groups, per), (shape(n * heads, d,...]
    pallas_call x1, Pallas kernels: 2.12 us -> 0.41 us  [on_device(): call(functools.partial(middle_kernel, per), shape(per, d, d), scalars=1,...]
    pallas_call x1, Pallas kernels: 1.89 us -> 0.19 us  [on_device(): call(functools.partial(stats_kernel, heads), (shape(heads, d), shape(beta...]
  transfers between devices with their start and end apart: 13 -> 13, of which waited for: 10 -> 10; matrix products, arithmetic and copies ran while one was open for 2% -> 0% of each run, Pallas kernels for 6% -> 3%
where the time goes in v2:
time: 64 us; the launch traced here: 63.2 us
  waiting for transfers between devices  26.2 us (41%)
  starting transfers between devices  22.3 us (35%)
  Pallas kernels  11.2 us (18%)
  local copies, waits for them, and re-layouts  2.75 us (4%)
  between operations  0.74 us (1%)
    ppermute x4, starting transfers between devices, on_device(): total = total + lax.ppermute(total, 'seq', flipped(mask))  10.1 us
    ppermute x3, waiting for transfers between devices, on_device(): lax.ppermute(maps[slot], 'seq', flipped(slot))  9.23 us
    ppermute x4, waiting for transfers between devices, on_device(): total = total + lax.ppermute(total, 'seq', flipped(mask))  6.32 us
    ppermute x1, waiting for transfers between devices, on_device(): other = lax.ppermute(run_map, 'seq', flipped(groups))  5.86 us
    pallas_call x1, Pallas kernels, on_device(): call(functools.partial(solve_kernel, groups, per, tokens_all), [shape(per...  5.16 us
    ppermute x1, starting transfers between devices, on_device(): came = lax.ppermute(middle, 'seq', [(i, i + half) for i in range(half)])  4.5 us
    ppermute x3, starting transfers between devices, on_device(): lax.ppermute(maps[slot], 'seq', flipped(slot))  3.55 us
    ppermute x3, starting transfers between devices, on_device(): lax.ppermute(entries[slot], 'seq', flipped(slot))  3.55 us
  transfers between devices with their start and end apart: 13, of which 10 were waited for; matrix products, arithmetic and copies ran while one was open for 0% of the time, Pallas kernels for 3%

profile of v2, /device:TPU:0, one launch (start us, length us, event | category | flops | bytes accessed | tf_op | source)
XLA Modules:
  0.0 63.2 jit_solution(14771040426820368205)
XLA Ops:
  0.6 0.0 copy-start
  0.6 0.0 copy-start.2
  0.7 1.0 %copy-done.2 = bf16[128,1024]{1,0:T(8,128)(2,1)S(1)} copy-done((bf16[128,1024]{1,0:T(8,128)(2,1)S(1)}, bf16[128,1024]{1,0:T(8,128)(2,1)}, u32[]{:S(2)}) %copy-start.2) | copy-done | bytes 262168
  1.7 0.0 copy-start.3
  1.7 0.9 %copy-done.3 = bf16[128,8,128]{2,1,0:T(8,128)(2,1)S(1)} copy-done((bf16[128,8,128]{2,1,0:T(8,128)(2,1)S(1)}, bf16[128,8,128]{2,1,0:T(8,128)(2,1)}, u32[]{:S(2)}) %copy-start.3) | copy-done | bytes 262168
  2.6 0.0 copy-start.5
  2.6 0.8 %copy-done.5 = bf16[16,1024]{1,0:T(8,128)(2,1)S(1)} copy-done((bf16[16,1024]{1,0:T(8,128)(2,1)S(1)}, bf16[16,1024]{1,0:T(8,128)(2,1)}, u32[]{:S(2)}) %copy-start.5) | copy-done | bytes 32792
  3.4 0.0 copy-start.4
  3.4 0.0 copy-start.6
  3.4 0.2 stats.1
  3.6 3.0 %collective-permute-start.1 = (f32[8,128]{1,0:T(8,128)S(1)}, f32[8,128]{1,0:T(8,128)S(1)}, u32[]{:S(2)}, u32[]{:S(2)}) collective-permute-start(f32[8,128]{1,0:T(8,128)S(1)} %get-tuple-element.21), channel_id=1, source_target_pairs={{0,2},{2,0},{4,6},{6,4},{8,10},{10,8},{12,14},{14,12},{16,18},{18,... | collective-permute-start | bytes 12296 | tf_op jit(solution)/shard_map/ppermute | solution.py:409
  6.5 1.6 %collective-permute-done.1 = f32[8,128]{1,0:T(8,128)S(1)} collective-permute-done((f32[8,128]{1,0:T(8,128)S(1)}, f32[8,128]{1,0:T(8,128)S(1)}, u32[]{:S(2)}, u32[]{:S(2)}) %collective-permute-start.1) | collective-permute-done | bytes 4128 | tf_op jit(solution)/shard_map/ppermute | solution.py:409
  8.1 2.0 %collective-permute-start.2 = (f32[8,128]{1,0:T(8,128)S(1)}, f32[8,128]{1,0:T(8,128)S(1)}, u32[]{:S(2)}, u32[]{:S(2)}) collective-permute-start(f32[8,128]{1,0:T(8,128)S(1)} %add.36), channel_id=1, source_target_pairs={{0,4},{2,6},{4,0},{6,2},{8,12},{10,14},{12,8},{14,10},{16,20},{18,... | collective-permute-start | bytes 12296 | tf_op jit(solution)/shard_map/ppermute | solution.py:409
  10.2 1.6 %collective-permute-done.2 = f32[8,128]{1,0:T(8,128)S(1)} collective-permute-done((f32[8,128]{1,0:T(8,128)S(1)}, f32[8,128]{1,0:T(8,128)S(1)}, u32[]{:S(2)}, u32[]{:S(2)}) %collective-permute-start.2) | collective-permute-done | bytes 4128 | tf_op jit(solution)/shard_map/ppermute | solution.py:409
  11.8 2.1 %collective-permute-start.3 = (f32[8,128]{1,0:T(8,128)S(1)}, f32[8,128]{1,0:T(8,128)S(1)}, u32[]{:S(2)}, u32[]{:S(2)}) collective-permute-start(f32[8,128]{1,0:T(8,128)S(1)} %add.37), channel_id=1, source_target_pairs={{0,8},{2,10},{4,12},{6,14},{8,0},{10,2},{12,4},{14,6},{16,24},{18,... | collective-permute-start | bytes 12296 | tf_op jit(solution)/shard_map/ppermute | solution.py:409
  13.8 0.0 collective-permute-start
  13.9 1.6 %collective-permute-done.3 = f32[8,128]{1,0:T(8,128)S(1)} collective-permute-done((f32[8,128]{1,0:T(8,128)S(1)}, f32[8,128]{1,0:T(8,128)S(1)}, u32[]{:S(2)}, u32[]{:S(2)}) %collective-permute-start.3) | collective-permute-done | bytes 4128 | tf_op jit(solution)/shard_map/ppermute | solution.py:409
  15.4 3.0 %collective-permute-start.4 = (f32[8,128]{1,0:T(8,128)S(1)}, f32[8,128]{1,0:T(8,128)S(1)}, u32[]{:S(2)}, u32[]{:S(2)}) collective-permute-start(f32[8,128]{1,0:T(8,128)S(1)} %add.38), channel_id=1, source_target_pairs={{0,16},{2,18},{4,20},{6,22},{8,24},{10,26},{12,28},{14,30},{16,0},... | collective-permute-start | bytes 12296 | tf_op jit(solution)/shard_map/ppermute | solution.py:409
  18.5 0.0 collective-permute-done
  18.5 0.0 copy-start.8
  18.5 1.6 %collective-permute-done.4 = f32[8,128]{1,0:T(8,128)S(1)} collective-permute-done((f32[8,128]{1,0:T(8,128)S(1)}, f32[8,128]{1,0:T(8,128)S(1)}, u32[]{:S(2)}, u32[]{:S(2)}) %collective-permute-start.4) | collective-permute-done | bytes 4128 | tf_op jit(solution)/shard_map/ppermute | solution.py:409
  20.1 0.0 copy-done.4
  20.1 0.0 copy-done.6
  20.1 0.0 copy-done.8
  20.1 5.2 %solve.1 = (f32[2,128,256]{2,1,0:T(8,128)S(1)}, f32[2,128,256]{2,1,0:T(8,128)S(1)}, f32[2,128,256]{2,1,0:T(8,128)S(1)}, f32[2,128,256]{2,1,0:T(8,128)S(1)}, f32[...) custom-call(s32[1]{0:T(128)} %bitcast.rank_ref, bf16[1024,128]{1,0:T(8,128)(2,1)S(1)} %bitcast.15, ...), custom_call_target="tpu_custom_call" | custom-call | flops 1073741824 | bytes 1048576 | tf_op jit(solution)/shard_map/solve/pallas_call | solution.py:413
  25.2 1.9 %collective-permute-start.5 = (f32[2,128,256]{2,1,0:T(8,128)S(1)}, f32[2,128,256]{2,1,0:T(8,128)S(1)}, u32[]{:S(2)}, u32[]{:S(2)}) collective-permute-start(f32[2,128,256]{2,1,0:T(8,128)S(1)} %get-tuple-element.23), channel_id=1, source_target_pairs={{0,2},{2,0},{4,6},{6,4},{8,10},{10,8},{12,14},{14,12},{16,18},{18,... | collective-permute-start | bytes 786440 | tf_op jit(solution)/shard_map/ppermute | solution.py:424
  27.1 1.5 %collective-permute-start.6 = (f32[2,128,256]{2,1,0:T(8,128)S(1)}, f32[2,128,256]{2,1,0:T(8,128)S(1)}, u32[]{:S(2)}, u32[]{:S(2)}) collective-permute-start(f32[2,128,256]{2,1,0:T(8,128)S(1)} %get-tuple-element.24), channel_id=1, source_target_pairs={{0,4},{2,6},{4,0},{6,2},{8,12},{10,14},{12,8},{14,10},{16,20},{18,... | collective-permute-start | bytes 786440 | tf_op jit(solution)/shard_map/ppermute | solution.py:424
  28.6 0.1 collective-permute-start.7
  28.8 5.2 %collective-permute-done.5.refs_1_ = f32[2,128,256]{2,1,0:T(8,128)S(1)} collective-permute-done((f32[2,128,256]{2,1,0:T(8,128)S(1)}, f32[2,128,256]{2,1,0:T(8,128)S(1)}, u32[]{:S(2)}, u32[]{:S(2)}) %collective-permute-start.5) | collective-permute-done | bytes 262176 | tf_op jit(solution)/shard_map/ppermute | solution.py:424
  34.0 4.0 %collective-permute-done.6.refs_2_ = f32[2,128,256]{2,1,0:T(8,128)S(1)} collective-permute-done((f32[2,128,256]{2,1,0:T(8,128)S(1)}, f32[2,128,256]{2,1,0:T(8,128)S(1)}, u32[]{:S(2)}, u32[]{:S(2)}) %collective-permute-start.6) | collective-permute-done | bytes 262176 | tf_op jit(solution)/shard_map/ppermute | solution.py:424
  38.0 0.0 collective-permute-done.7.refs_3_
  38.0 0.7 %compose.1 = (f32[3,2,128,256]{3,2,1,0:T(8,128)S(1)}, f32[2,128,256]{2,1,0:T(8,128)S(1)}) custom-call(s32[1]{0:T(128)} %bitcast.rank_ref, f32[2,128,256]{2,1,0:T(8,128)S(1)} %get-tuple-element.22.refs_0_, f32[2,128,256]{2,1,0:T(8,128)S(1)} %collective-permute-done.5.refs_1_, f32[2,128,256]{2,1,0:T(8,128)S(1)} %collective-permute-done.6.refs_2_, ...), custom_call_target="tpu_custom_call" | custom-call | flops 134217728 | bytes 1048576 | tf_op jit(solution)/shard_map/compose/pallas_call | solution.py:436
  38.8 0.6 collective-permute-start.8
  39.3 0.0 copy-done
  39.3 5.9 %collective-permute-done.8.other_ref.before_ref = f32[2,128,256]{2,1,0:T(8,128)S(1)} collective-permute-done((f32[2,128,256]{2,1,0:T(8,128)S(1)}, f32[2,128,256]{2,1,0:T(8,128)S(1)}, u32[]{:S(2)}, u32[]{:S(2)}) %collective-permute-start.8) | collective-permute-done | bytes 262176 | tf_op jit(solution)/shard_map/ppermute | solution.py:449
  45.2 0.4 middle.1
  45.6 4.5 %collective-permute-start.9 = (f32[2,128,128]{2,1,0:T(8,128)S(1)}, f32[2,128,128]{2,1,0:T(8,128)S(1)}, u32[]{:S(2)}, u32[]{:S(2)}) collective-permute-start(f32[2,128,128]{2,1,0:T(8,128)S(1)} %middle.1), channel_id=1, source_target_pairs={{0,16},{2,18},{4,20},{6,22},{8,24},{10,26},{12,28},{14,30},{1,17},... | collective-permute-start | bytes 393224 | tf_op jit(solution)/shard_map/ppermute | solution.py:470
  50.1 2.5 %collective-permute-done.9.came_ref = f32[2,128,128]{2,1,0:T(8,128)S(1)} collective-permute-done((f32[2,128,128]{2,1,0:T(8,128)S(1)}, f32[2,128,128]{2,1,0:T(8,128)S(1)}, u32[]{:S(2)}, u32[]{:S(2)}) %collective-permute-start.9) | collective-permute-done | bytes 131104 | tf_op jit(solution)/shard_map/ppermute | solution.py:470
  52.6 0.0 copy-start.7
  52.6 0.7 %enter.1 = (f32[2,128,128]{2,1,0:T(8,128)S(1)}, f32[2,128,128]{2,1,0:T(8,128)S(1)}, f32[2,128,128]{2,1,0:T(8,128)S(1)}, f32[2,128,128]{2,1,0:T(8,128)S(1)}) custom-call(s32[1]{0:T(128)} %bitcast.rank_ref, s32[1]{0:T(128)} %bitcast.1.upper_ref, s32[1]{0:T(128)} %bitcast.2.later_ref, f32[3,2,128,256]{3,2,1,0:T(8,128)S(1)} %get-tuple-element.26.prefix_ref, ...), custom_call_target="tpu_custom_call" | custom-call | flops 134217728 | bytes 1048576 | tf_op jit(solution)/shard_map/enter/pallas_call | solution.py:472
  53.3 1.3 %collective-permute-start.10 = (f32[2,128,128]{2,1,0:T(8,128)S(1)}, f32[2,128,128]{2,1,0:T(8,128)S(1)}, u32[]{:S(2)}, u32[]{:S(2)}) collective-permute-start(f32[2,128,128]{2,1,0:T(8,128)S(1)} %get-tuple-element.29), channel_id=1, source_target_pairs={{0,2},{2,0},{4,6},{6,4},{8,10},{10,8},{12,14},{14,12},{16,18},{18,... | collective-permute-start | bytes 393224 | tf_op jit(solution)/shard_map/ppermute | solution.py:483
  54.6 0.8 %collective-permute-start.11 = (f32[2,128,128]{2,1,0:T(8,128)S(1)}, f32[2,128,128]{2,1,0:T(8,128)S(1)}, u32[]{:S(2)}, u32[]{:S(2)}) collective-permute-start(f32[2,128,128]{2,1,0:T(8,128)S(1)} %get-tuple-element.30), channel_id=1, source_target_pairs={{0,4},{2,6},{4,0},{6,2},{8,12},{10,14},{12,8},{14,10},{16,20},{18,... | collective-permute-start | bytes 393224 | tf_op jit(solution)/shard_map/ppermute | solution.py:483
  55.5 1.4 %collective-permute-start.12 = (f32[2,128,128]{2,1,0:T(8,128)S(1)}, f32[2,128,128]{2,1,0:T(8,128)S(1)}, u32[]{:S(2)}, u32[]{:S(2)}) collective-permute-start(f32[2,128,128]{2,1,0:T(8,128)S(1)} %get-tuple-element.31), channel_id=1, source_target_pairs={{0,6},{2,4},{4,2},{6,0},{8,14},{10,12},{12,10},{14,8},{16,22},{18,... | collective-permute-start | bytes 393224 | tf_op jit(solution)/shard_map/ppermute | solution.py:483
  56.9 0.0 copy-done.7
  56.9 0.0 copy-start.1
  56.9 2.1 %outputs.1 = (bf16[8,256,256]{2,1,0:T(8,128)(2,1)S(1)}, f32[8,256,128]{2,1,0:T(8,128)S(1)}) custom-call(s32[1]{0:T(128)} %bitcast.rank_ref, bf16[1024,128]{1,0:T(8,128)(2,1)S(1)} %bitcast.20, bf16[1024,128]{1,0:T(8,128)(2,1)S(1)} %bitcast.16, f32[8,128]{1,0:T(8,128)S(1)} %add.39.total_ref, f32[8,128]{1,0:T(8,128)S(1)} %get-tuple-element.32.cum_ref, ...), custom_call_target="tpu_custom_call" | custom-call | flops 1073741824 | bytes 1048576 | tf_op jit(solution)/shard_map/outputs/pallas_call | solution.py:426
  59.0 0.0 collective-permute-done.10.refs_1_
  59.0 0.6 collective-permute-done.11.refs_2_
  59.6 1.7 %collective-permute-done.12.refs_3_ = f32[2,128,128]{2,1,0:T(8,128)S(1)} collective-permute-done((f32[2,128,128]{2,1,0:T(8,128)S(1)}, f32[2,128,128]{2,1,0:T(8,128)S(1)}, u32[]{:S(2)}, u32[]{:S(2)}) %collective-permute-start.12) | collective-permute-done | bytes 131104 | tf_op jit(solution)/shard_map/ppermute | solution.py:483
  61.3 0.0 copy-done.1
  61.3 1.9 %finish.1 = (bf16[1024,128]{1,0:T(8,128)(2,1)}, f32[2,8,128,128]{3,2,1,0:T(8,128)}) custom-call(s32[1]{0:T(128)} %bitcast.rank_ref, f32[2,128,128]{2,1,0:T(8,128)S(1)} %get-tuple-element.28.refs_0_, f32[2,128,128]{2,1,0:T(8,128)S(1)} %collective-permute-done.10.refs_1_, f32[2,128,128]{2,1,0:T(8,128)S(1)} %collective-permute-done.11.refs_2_, ...), custom_call_target="tpu_custom_call" | custom-call | flops 268435456 | bytes 1048576 | tf_op jit(solution)/shard_map/finish/pallas_call | solution.py:485
  (7 shorter events, 0.0 us)
Async XLA Ops:
  0.6 38.7 %copy-start = (f32[8,128,128]{2,1,0:T(8,128)S(1)}, f32[8,128,128]{2,1,0:T(8,128)}, u32[]{:S(2)}) copy-start(f32[8,128,128]{2,1,0:T(8,128)} %param.15) | copy-start | bytes 1572868
  0.6 1.0 %copy-start.2 = (bf16[128,1024]{1,0:T(8,128)(2,1)S(1)}, bf16[128,1024]{1,0:T(8,128)(2,1)}, u32[]{:S(2)}) copy-start(bf16[128,1024]{1,0:T(8,128)(2,1)} %inputs_ref.1) | copy-start | bytes 786436
  1.7 0.9 %copy-start.3 = (bf16[128,8,128]{2,1,0:T(8,128)(2,1)S(1)}, bf16[128,8,128]{2,1,0:T(8,128)(2,1)}, u32[]{:S(2)}) copy-start(bf16[128,8,128]{2,1,0:T(8,128)(2,1)} %param.9) | copy-start | bytes 786436
  2.6 0.8 %copy-start.5 = (bf16[16,1024]{1,0:T(8,128)(2,1)S(1)}, bf16[16,1024]{1,0:T(8,128)(2,1)}, u32[]{:S(2)}) copy-start(bf16[16,1024]{1,0:T(8,128)(2,1)} %weight_ref.1) | copy-start | bytes 98308
  3.4 16.7 %copy-start.4 = (bf16[128,8,128]{2,1,0:T(8,128)(2,1)S(1)}, bf16[128,8,128]{2,1,0:T(8,128)(2,1)}, u32[]{:S(2)}) copy-start(bf16[128,8,128]{2,1,0:T(8,128)(2,1)} %param.9) | copy-start | bytes 786436
  3.4 16.7 %copy-start.6 = (bf16[128,8,128]{2,1,0:T(8,128)(2,1)S(1)}, bf16[128,8,128]{2,1,0:T(8,128)(2,1)}, u32[]{:S(2)}) copy-start(bf16[128,8,128]{2,1,0:T(8,128)(2,1)} %param.10) | copy-start | bytes 786436
  3.6 4.6 %collective-permute-start.1 = (f32[8,128]{1,0:T(8,128)S(1)}, f32[8,128]{1,0:T(8,128)S(1)}, u32[]{:S(2)}, u32[]{:S(2)}) collective-permute-start(f32[8,128]{1,0:T(8,128)S(1)} %get-tuple-element.21), channel_id=1, source_target_pairs={{0,2},{2,0},{4,6},{6,4},{8,10},{10,8},{12,14},{14,12},{16,18},{18,... | collective-permute-start | bytes 12296 | tf_op jit(solution)/shard_map/ppermute | solution.py:409
  8.1 3.6 %collective-permute-start.2 = (f32[8,128]{1,0:T(8,128)S(1)}, f32[8,128]{1,0:T(8,128)S(1)}, u32[]{:S(2)}, u32[]{:S(2)}) collective-permute-start(f32[8,128]{1,0:T(8,128)S(1)} %add.36), channel_id=1, source_target_pairs={{0,4},{2,6},{4,0},{6,2},{8,12},{10,14},{12,8},{14,10},{16,20},{18,... | collective-permute-start | bytes 12296 | tf_op jit(solution)/shard_map/ppermute | solution.py:409
  11.8 3.7 %collective-permute-start.3 = (f32[8,128]{1,0:T(8,128)S(1)}, f32[8,128]{1,0:T(8,128)S(1)}, u32[]{:S(2)}, u32[]{:S(2)}) collective-permute-start(f32[8,128]{1,0:T(8,128)S(1)} %add.37), channel_id=1, source_target_pairs={{0,8},{2,10},{4,12},{6,14},{8,0},{10,2},{12,4},{14,6},{16,24},{18,... | collective-permute-start | bytes 12296 | tf_op jit(solution)/shard_map/ppermute | solution.py:409
  13.8 4.6 %collective-permute-start = (f32[8,128]{1,0:T(8,128)S(1)}, f32[8,128]{1,0:T(8,128)S(1)}, u32[]{:S(2)}, u32[]{:S(2)}) collective-permute-start(f32[8,128]{1,0:T(8,128)S(1)} %dynamic-slice_bitcast_fusion), channel_id=1, source_target_pairs={{0,1},{1,0},{2,3},{3,2},{4,5},{5,4},{6,7},{7,6},{8,9},{9,8},{10,11... | collective-permute-start | bytes 12296 | tf_op jit(solution)/shard_map/ppermute | solution.py:404
  15.4 4.6 %collective-permute-start.4 = (f32[8,128]{1,0:T(8,128)S(1)}, f32[8,128]{1,0:T(8,128)S(1)}, u32[]{:S(2)}, u32[]{:S(2)}) collective-permute-start(f32[8,128]{1,0:T(8,128)S(1)} %add.38), channel_id=1, source_target_pairs={{0,16},{2,18},{4,20},{6,22},{8,24},{10,26},{12,28},{14,30},{16,0},... | collective-permute-start | bytes 12296 | tf_op jit(solution)/shard_map/ppermute | solution.py:409
  18.5 1.6 %copy-start.8 = (f32[8,128]{1,0:T(8,128)S(1)}, f32[8,128]{1,0:T(8,128)}, u32[]{:S(2)}) copy-start(f32[8,128]{1,0:T(8,128)} %decay_ref.1) | copy-start | bytes 12292
  25.2 8.7 %collective-permute-start.5 = (f32[2,128,256]{2,1,0:T(8,128)S(1)}, f32[2,128,256]{2,1,0:T(8,128)S(1)}, u32[]{:S(2)}, u32[]{:S(2)}) collective-permute-start(f32[2,128,256]{2,1,0:T(8,128)S(1)} %get-tuple-element.23), channel_id=1, source_target_pairs={{0,2},{2,0},{4,6},{6,4},{8,10},{10,8},{12,14},{14,12},{16,18},{18,... | collective-permute-start | bytes 786440 | tf_op jit(solution)/shard_map/ppermute | solution.py:424
  27.1 10.9 %collective-permute-start.6 = (f32[2,128,256]{2,1,0:T(8,128)S(1)}, f32[2,128,256]{2,1,0:T(8,128)S(1)}, u32[]{:S(2)}, u32[]{:S(2)}) collective-permute-start(f32[2,128,256]{2,1,0:T(8,128)S(1)} %get-tuple-element.24), channel_id=1, source_target_pairs={{0,4},{2,6},{4,0},{6,2},{8,12},{10,14},{12,8},{14,10},{16,20},{18,... | collective-permute-start | bytes 786440 | tf_op jit(solution)/shard_map/ppermute | solution.py:424
  28.6 9.4 %collective-permute-start.7 = (f32[2,128,256]{2,1,0:T(8,128)S(1)}, f32[2,128,256]{2,1,0:T(8,128)S(1)}, u32[]{:S(2)}, u32[]{:S(2)}) collective-permute-start(f32[2,128,256]{2,1,0:T(8,128)S(1)} %get-tuple-element.25), channel_id=1, source_target_pairs={{0,6},{2,4},{4,2},{6,0},{8,14},{10,12},{12,10},{14,8},{16,22},{18,... | collective-permute-start | bytes 786440 | tf_op jit(solution)/shard_map/ppermute | solution.py:424
  38.8 6.4 %collective-permute-start.8 = (f32[2,128,256]{2,1,0:T(8,128)S(1)}, f32[2,128,256]{2,1,0:T(8,128)S(1)}, u32[]{:S(2)}, u32[]{:S(2)}) collective-permute-start(f32[2,128,256]{2,1,0:T(8,128)S(1)} %get-tuple-element.27.mine_ref), channel_id=1, source_target_pairs={{0,8},{2,10},{4,12},{6,14},{8,0},{10,2},{12,4},{14,6},{16,24},{18,... | collective-permute-start | bytes 786440 | tf_op jit(solution)/shard_map/ppermute | solution.py:449
  45.6 7.0 %collective-permute-start.9 = (f32[2,128,128]{2,1,0:T(8,128)S(1)}, f32[2,128,128]{2,1,0:T(8,128)S(1)}, u32[]{:S(2)}, u32[]{:S(2)}) collective-permute-start(f32[2,128,128]{2,1,0:T(8,128)S(1)} %middle.1), channel_id=1, source_target_pairs={{0,16},{2,18},{4,20},{6,22},{8,24},{10,26},{12,28},{14,30},{1,17},... | collective-permute-start | bytes 393224 | tf_op jit(solution)/shard_map/ppermute | solution.py:470
  52.6 4.3 %copy-start.7 = (bf16[128,8,128]{2,1,0:T(8,128)(2,1)S(1)}, bf16[128,8,128]{2,1,0:T(8,128)(2,1)}, u32[]{:S(2)}) copy-start(bf16[128,8,128]{2,1,0:T(8,128)(2,1)} %param.8) | copy-start | bytes 786436
  53.3 5.7 %collective-permute-start.10 = (f32[2,128,128]{2,1,0:T(8,128)S(1)}, f32[2,128,128]{2,1,0:T(8,128)S(1)}, u32[]{:S(2)}, u32[]{:S(2)}) collective-permute-start(f32[2,128,128]{2,1,0:T(8,128)S(1)} %get-tuple-element.29), channel_id=1, source_target_pairs={{0,2},{2,0},{4,6},{6,4},{8,10},{10,8},{12,14},{14,12},{16,18},{18,... | collective-permute-start | bytes 393224 | tf_op jit(solution)/shard_map/ppermute | solution.py:483
  54.6 5.0 %collective-permute-start.11 = (f32[2,128,128]{2,1,0:T(8,128)S(1)}, f32[2,128,128]{2,1,0:T(8,128)S(1)}, u32[]{:S(2)}, u32[]{:S(2)}) collective-permute-start(f32[2,128,128]{2,1,0:T(8,128)S(1)} %get-tuple-element.30), channel_id=1, source_target_pairs={{0,4},{2,6},{4,0},{6,2},{8,12},{10,14},{12,8},{14,10},{16,20},{18,... | collective-permute-start | bytes 393224 | tf_op jit(solution)/shard_map/ppermute | solution.py:483
  55.5 5.9 %collective-permute-start.12 = (f32[2,128,128]{2,1,0:T(8,128)S(1)}, f32[2,128,128]{2,1,0:T(8,128)S(1)}, u32[]{:S(2)}, u32[]{:S(2)}) collective-permute-start(f32[2,128,128]{2,1,0:T(8,128)S(1)} %get-tuple-element.31), channel_id=1, source_target_pairs={{0,6},{2,4},{4,2},{6,0},{8,14},{10,12},{12,10},{14,8},{16,22},{18,... | collective-permute-start | bytes 393224 | tf_op jit(solution)/shard_map/ppermute | solution.py:483
  56.9 4.4 %copy-start.1 = (bf16[128,8,128]{2,1,0:T(8,128)(2,1)S(1)}, bf16[128,8,128]{2,1,0:T(8,128)(2,1)}, u32[]{:S(2)}) copy-start(bf16[128,8,128]{2,1,0:T(8,128)(2,1)} %param.11) | copy-start | bytes 786436

commit v3 on v2

v3 whole, which is shorter than its diff:
```python
import functools
import math

import jax
import jax.numpy as jnp
from jax import lax
from jax.experimental import pallas as pl
from jax.experimental.pallas import tpu as pltpu
from jax.sharding import PartitionSpec as P


BLOCK = 64
EPSILON = 1e-06
F32 = jnp.float32
BF16 = jnp.bfloat16
VMEM_LIMIT = 20 * 1024 * 1024


def split(x):
    high = x.astype(BF16)
    return high, (x - high.astype(F32)).astype(BF16)


def mm(a, b):
    return jnp.dot(a, b, preferred_element_type=F32)


def dot_split(left, right):
    (lh, ll), (rh, rl) = left, right
    return mm(jnp.concatenate([lh, ll], 1), jnp.concatenate([rh, rh], 0)) + mm(lh, rl)


def dot_square(left, right):
    (lh, ll), (rh, rl) = left, right
    n = rh.shape[1]
    wide = mm(
        jnp.concatenate([lh, ll], 1),
        jnp.concatenate(
            [jnp.concatenate([rh, rl], 1), jnp.concatenate([rh, jnp.zeros_like(rl)], 1)], 0
        ),
    )
    return wide[:, :n] + wide[:, n:]


def iotas(n, m):
    return (
        lax.broadcasted_iota(jnp.int32, (n, m), 0),
        lax.broadcasted_iota(jnp.int32, (n, m), 1),
    )


def vmem(count):
    return [pl.BlockSpec(memory_space=pltpu.VMEM)] * count


def smem():
    return pl.BlockSpec(memory_space=pltpu.SMEM)


def call(kernel, out_shape, scratch=(), scalars=0, operands=0, anywhere=0, flops=0, grant=VMEM_LIMIT):
    single = not isinstance(out_shape, (list, tuple))
    return pl.pallas_call(
        kernel,
        out_shape=out_shape,
        in_specs=[smem()] * scalars
        + [pl.BlockSpec(memory_space=pltpu.HBM)] * anywhere
        + vmem(operands),
        out_specs=vmem(1)[0] if single else vmem(len(out_shape)),
        scratch_shapes=list(scratch),
        compiler_params=pltpu.CompilerParams(vmem_limit_bytes=grant),
        cost_estimate=pl.CostEstimate(flops=flops, bytes_accessed=1 << 20, transcendentals=0),
    )


def shape(*dims, dtype=F32):
    return jax.ShapeDtypeStruct(dims, dtype)


def norms_kernel(heads, key_ref, total_ref):
    keys = key_ref[...].astype(F32)
    squares = keys * keys
    rows = squares.shape[0]
    total_ref[...] = squares.reshape(rows // heads, heads, squares.shape[1]).sum(0)


def logits_kernel(heads, pair, side_ref, weight_ref, inputs_ref, *refs):
    logits = lax.dot_general(
        weight_ref[...], inputs_ref[...], (((1,), (1,)), ((), ())), preferred_element_type=F32
    )
    if pair:
        own_ref, theirs_ref, full_ref = refs
        full_ref[...] = logits
        mine = pl.multiple_of(side_ref[0] * heads, heads)
        own_ref[...] = full_ref[pl.ds(mine, heads), :]
        theirs_ref[...] = full_ref[pl.ds(heads - mine, heads), :]
    else:
        refs[0][...] = logits


def pack_kernel(
    groups, per, rank_ref, key_ref, value_ref, decay_ref, own_ref, came_ref, *refs
):
    out_refs, (flat_ref, logit_ref) = refs[:groups], refs[groups:]
    heads, n = decay_ref.shape
    logit_ref[...] = own_ref[...] + came_ref[...]
    for at, source in enumerate((key_ref, value_ref)):
        flat_ref[...] = source[...].astype(F32)
        for slot in range(groups):
            for i in range(per):
                head = (slot ^ rank_ref[0]) * per + i
                out_refs[slot][i, at * n : (at + 1) * n] = flat_ref[
                    pl.ds(head, n, stride=heads), :
                ]
    for slot in range(groups):
        for i in range(per):
            head = (slot ^ rank_ref[0]) * per + i
            out_refs[slot][i, 2 * n : 2 * n + 1] = decay_ref[pl.ds(head, 1), :]
            out_refs[slot][i, 2 * n + 1 : 2 * n + 2] = logit_ref[pl.ds(head, 1), :]
            out_refs[slot][i, 2 * n + 2 :] = jnp.zeros((6, n), F32)


def sums_along(decay):
    lane = lax.broadcasted_iota(jnp.int32, decay.shape, 1)
    step = 1
    while step < decay.shape[1]:
        decay = decay + jnp.where(lane >= step, pltpu.roll(decay, step, 1), 0.0)
        step *= 2
    return decay


def limits(total, tokens_all):
    return jnp.sqrt(jnp.sum(total, 1, keepdims=True) / tokens_all + EPSILON)


def solve(keys, values, decay, logits, limit, rows_ref):
    items, n = decay.shape
    row, col = iotas(n, n)
    cum = sums_along(decay)
    beta = 1.0 / (1.0 + jnp.exp(-logits))
    keys_t = [key.T for key in keys]
    grams = [mm(key, key_t) for key, key_t in zip(keys, keys_t)]
    norm = jnp.concatenate(
        [jnp.sum(jnp.where(row == col, gram, 0.0), 0, keepdims=True) for gram in grams], 0
    )
    inverse = 1.0 / jnp.maximum(jnp.sqrt(norm), limit)
    for at, kind in enumerate((cum, beta * inverse, inverse)):
        rows_ref[at * items : (at + 1) * items, :] = kind
    columns = rows_ref[...].T

    def column(kind, item):
        at = kind * items + item
        return columns[:, at : at + 1]

    systems, inverses = [], []
    for item in range(items):
        spread = column(0, item) - cum[item : item + 1, :]
        damping = jnp.exp(jnp.where(row > col, spread, 0.0))
        system = jnp.where(
            row > col,
            grams[item] * damping * column(1, item) * inverse[item : item + 1, :],
            0.0,
        )
        systems.append(split(system))
        inverses.append(
            jnp.where(row == col, 1.0, jnp.where((row ^ col) == 1, -system, 0.0))
        )
    size = 2
    while size < n:
        joins = ((row ^ col) & ~(2 * size - 1)) == 0
        joins = joins & ((row & size) != 0) & ((col & size) == 0)
        parts = [split(x) for x in inverses]
        mids = [split(dot_square(a, x)) for a, x in zip(systems, parts)]
        ends = [dot_square(x, t) for x, t in zip(parts, mids)]
        inverses = [x - jnp.where(joins, e, 0.0) for x, e in zip(inverses, ends)]
        size *= 2
    write_scale = beta * jnp.exp(cum) * inverse
    writes = []
    for item in range(items):
        x, key, value = inverses[item], keys[item], values[item]
        w = mm(
            jnp.concatenate(split(x * write_scale[item : item + 1, :]), 1),
            jnp.concatenate([key, key], 0),
        )
        u = mm(
            jnp.concatenate(split(x * beta[item : item + 1, :]), 1),
            jnp.concatenate([value, value], 0),
        )
        writes.append(jnp.concatenate([w, u], 1) * column(2, item))
    return writes, keys_t, cum, [column(0, item) for item in range(items)]


def read_map(write, key_t, carry, lift, row, col):
    d = key_t.shape[0]
    both = mm(
        jnp.concatenate([key_t, key_t], 1), jnp.concatenate(split(write * carry), 0)
    )
    ends = jnp.where(row == col, lift, 0.0)
    return jnp.concatenate([ends - both[:, :d], both[:, d:]], 1)


def run_kernel(groups, per, tokens_all, rank_ref, total_ref, *refs):
    packs, (prefix_ref, run_ref, rows_ref, held_ref) = refs[:groups], refs[groups:]
    n = total_ref.shape[1]
    row, col = iotas(n, n)
    items = [(slot, i) for slot in range(groups) for i in range(per)]
    limit = limits(total_ref[...], tokens_all)
    rows_ref[0 : limit.shape[0], :] = jnp.broadcast_to(limit, (limit.shape[0], n))
    limit = jnp.concatenate(
        [rows_ref[pl.ds(rank_ref[0] * per + i, 1), :] for _, i in items], 0
    )
    keys = [packs[slot][i, 0:n].astype(BF16) for slot, i in items]
    values = [packs[slot][i, n : 2 * n].astype(BF16) for slot, i in items]
    decay = jnp.concatenate([packs[slot][i, 2 * n : 2 * n + 1] for slot, i in items], 0)
    logits = jnp.concatenate([packs[slot][i, 2 * n + 1 : 2 * n + 2] for slot, i in items], 0)
    writes, keys_t, cum, cum_columns = solve(keys, values, decay, logits, limit, rows_ref)
    for item, (slot, i) in enumerate(items):
        last = cum[item : item + 1, n - 1 : n]
        held_ref[slot ^ rank_ref[0], i] = read_map(
            writes[item], keys_t[item], jnp.exp(last - cum_columns[item]), jnp.exp(last), row, col
        )
    so_far = [held_ref[0, i] for i in range(per)]
    for place in range(1, groups):
        for i in range(per):
            prefix_ref[place - 1, i] = so_far[i]
        so_far = [join(held_ref[place, i], so_far[i]) for i in range(per)]
    for i in range(per):
        run_ref[i] = so_far[i]


def own_kernel(
    tokens_all,
    key_ref,
    value_ref,
    own_ref,
    came_ref,
    total_ref,
    decay_ref,
    wu_ref,
    cum_ref,
    flat_ref,
    rows_ref,
):
    heads, n = decay_ref.shape
    flat_ref[...] = key_ref[...].astype(F32)
    keys = [flat_ref[pl.ds(h, n, stride=heads), :].astype(BF16) for h in range(heads)]
    flat_ref[...] = value_ref[...].astype(F32)
    values = [flat_ref[pl.ds(h, n, stride=heads), :].astype(BF16) for h in range(heads)]
    writes, _, cum, _ = solve(
        keys,
        values,
        decay_ref[...],
        own_ref[...] + came_ref[...],
        limits(total_ref[...], tokens_all),
        rows_ref,
    )
    cum_ref[...] = cum
    for h in range(heads):
        wu_ref[h] = writes[h]


def output_kernel(
    query_ref, key_ref, cum_ref, wu_ref, left_ref, right_ref, flat_ref, rows_ref
):
    heads, n = cum_ref.shape
    d = key_ref.shape[1]
    blocks = n // BLOCK
    row, col = iotas(n, n)
    cum = cum_ref[...]
    flat_ref[...] = key_ref[...].astype(F32)
    keys = [flat_ref[pl.ds(h, n, stride=heads), :].astype(BF16) for h in range(heads)]
    flat_ref[...] = query_ref[...].astype(F32)
    queries = [flat_ref[pl.ds(h, n, stride=heads), :] for h in range(heads)]
    position = lax.broadcasted_iota(jnp.int32, (heads, n), 1)
    kinds = [cum]
    for b in range(1, blocks):
        end = b * BLOCK
        fall = jnp.exp(jnp.minimum(cum[:, end - 1 : end] - cum, 0.0))
        kinds.append(jnp.where(position < end, fall, 0.0))
    for at, kind in enumerate(kinds):
        rows_ref[at * heads : (at + 1) * heads, :] = kind
    columns = rows_ref[...].T
    for h in range(heads):
        write, key_t, query = wu_ref[h], keys[h].T, queries[h]
        cum_column = columns[:, h : h + 1]
        reach = (
            1.0 / jnp.sqrt(jnp.sum(query * query, 1, keepdims=True) + EPSILON) * (d**-0.5)
        )
        scores = mm(query.astype(BF16), key_t)
        spread = jnp.where(row >= col, cum_column - cum[h : h + 1, :], 0.0)
        scores = jnp.where(row >= col, scores * jnp.exp(spread), 0.0) * reach
        both = dot_split(split(scores), split(write))
        rest = [query * (reach * jnp.exp(cum_column)) - both[:, :d]]
        outs = [both[:, d:]]
        for b in range(1, blocks):
            at = b * BLOCK - 1
            carry = columns[:, b * heads + h : b * heads + h + 1]
            inner = read_map(
                write, key_t, carry, jnp.exp(cum[h : h + 1, at : at + 1]), row, col
            )
            rest.append(inner[:, :d])
            outs.append(inner[:, d:])
        left_ref[h] = jnp.concatenate(split(jnp.concatenate(rest, 0)), 1)
        right_ref[h] = jnp.concatenate(outs, 0)


def join(latter, earlier):
    d = latter.shape[0]
    both = dot_split(split(latter[:, :d]), split(earlier))
    return jnp.concatenate([both[:, :d], both[:, d:] + latter[:, d:]], 1)


def apply(step, state):
    d = state.shape[0]
    return dot_split(split(step[:, :d]), split(state)) + step[:, d:]


def middle_kernel(per, upper_ref, mine_ref, other_ref, start_ref, state_ref):
    for i in range(per):
        mine, other = mine_ref[i], other_ref[i]
        upper = upper_ref[0] != 0
        earlier = jnp.where(upper, other, mine)
        latter = jnp.where(upper, mine, other)
        state_ref[i] = apply(latter, apply(earlier, start_ref[i]))


def enter_kernel(
    groups, per, rank_ref, upper_ref, later_ref, prefix_ref, before_ref, start_ref, came_ref, *refs
):
    out_refs, out_ref = refs[:groups], refs[groups]
    for i in range(per):
        state = jnp.where(later_ref[0] != 0, came_ref[i], start_ref[i])
        moved = apply(before_ref[i], state)
        state = jnp.where(upper_ref[0] != 0, moved, state)
        out_ref[rank_ref[0], i] = state
        for place in range(1, groups):
            out_ref[place ^ rank_ref[0], i] = apply(prefix_ref[place - 1, i], state)
    for slot in range(groups):
        out_refs[slot][...] = out_ref[slot]


def finish_kernel(groups, per, rank_ref, *refs):
    states = refs[:groups]
    left_ref, right_ref, gate_ref, out_ref, block_ref, flat_ref, gates_ref = refs[groups:]
    heads = groups * per
    order = [(slot ^ rank_ref[0]) * per + i for slot in range(groups) for i in range(per)]
    d = gate_ref.shape[1]
    n = gate_ref.shape[0] // heads
    blocks = block_ref.shape[0]
    gates_ref[...] = gate_ref[...].astype(F32)
    for item, head in enumerate(order):
        state = states[item // per][item % per]
        high, low = split(state)
        left = left_ref[head]
        both = mm(left, jnp.concatenate([high, high], 0)) + mm(left[:, :d], low) + right_ref[head]
        raw = both[:n]
        block_ref[0, head] = state
        for b in range(1, blocks):
            block_ref[b, head] = both[n + (b - 1) * d : n + b * d]
        gate = gates_ref[pl.ds(head, n, stride=heads), :]
        scale = 1.0 / jnp.sqrt(jnp.mean(raw * raw, 1, keepdims=True) + EPSILON)
        flat_ref[pl.ds(head, n, stride=heads), :] = raw * scale * (gate / (1.0 + jnp.exp(-gate)))
    out_ref[...] = flat_ref[...].astype(BF16)


def exact(matrix, operand):
    return jnp.einsum("...ij,...jk->...ik", matrix, operand, precision=lax.Precision.HIGHEST)


def chain(latter, earlier):
    d = latter.shape[-2]
    both = exact(latter[..., :d], earlier)
    return jnp.concatenate([both[..., :d], both[..., d:] + latter[..., d:]], -1)


def flag(value):
    return jnp.reshape(value, (1,)).astype(jnp.int32)


def on_device(
    queries, key_vectors, values, out_gate, inputs, beta_weight, log_decay, initial_state
):
    n, heads, d = queries.shape
    blocks = n // BLOCK
    count, place = lax.axis_size("seq"), lax.axis_index("seq")
    groups = math.gcd(math.gcd(4, heads), count)
    per = heads // groups
    runs = count // groups
    rounds = runs.bit_length() - 1
    assert runs == 1 << rounds
    rank = flag(place % groups)
    run = place // groups

    def flipped(mask):
        return [(i, i ^ mask) for i in range(count)]

    def flat(tensor):
        return tensor.reshape(n * heads, d)

    pair = lax.axis_size("head") == 2
    all_heads = beta_weight.shape[0]
    total = call(
        functools.partial(norms_kernel, heads), shape(heads, d), operands=1, flops=1 << 31
    )(flat(key_vectors))
    logits = call(
        functools.partial(logits_kernel, heads, pair),
        [shape(heads, n)] * 2 if pair else [shape(all_heads, n)],
        scratch=(pltpu.VMEM((all_heads, n), F32),) if pair else (),
        scalars=1,
        operands=2,
        flops=1 << 24,
    )(flag(lax.axis_index("head")), beta_weight, inputs)
    if pair:
        own, theirs = logits
        came = lax.ppermute(theirs, "head", [(0, 1), (1, 0)])
    else:
        own = lax.psum_scatter(logits[0], "head", scatter_dimension=0, tiled=True)
        came = jnp.zeros_like(own)
    packs = call(
        functools.partial(pack_kernel, groups, per),
        [shape(per, 2 * n + 8, d)] * groups,
        scratch=(pltpu.VMEM((n * heads, d), F32), pltpu.VMEM((heads, n), F32)),
        scalars=1,
        operands=5,
        flops=1 << 24,
    )(rank, flat(key_vectors), flat(values), log_decay, own, came)

    def summed(total, mask):
        return total + lax.ppermute(total, "seq", flipped(mask))

    for slot in range(1, groups):
        if slot & (slot - 1) == 0:
            total = summed(total, slot)
            if slot == 1:
                total, packs = lax.optimization_barrier((total, packs))
    exchanged = []
    for slot in range(1, groups):
        exchanged.append(lax.ppermute(packs[slot], "seq", flipped(slot)))
    packs = [packs[0]] + exchanged
    mask = groups
    while mask < count:
        total = summed(total, mask)
        mask *= 2

    tokens_all = n * count
    prefix, run_map = call(
        functools.partial(run_kernel, groups, per, tokens_all),
        (shape(max(groups - 1, 1), per, d, 2 * d), shape(per, d, 2 * d)),
        scratch=(pltpu.VMEM((128, n), F32), pltpu.VMEM((groups, per, d, 2 * d), F32)),
        scalars=1,
        operands=1 + groups,
        flops=1 << 30,
    )(rank, total, *packs)

    wu, cum = call(
        functools.partial(own_kernel, tokens_all),
        (shape(heads, n, 2 * d), shape(heads, n)),
        scratch=(pltpu.VMEM((n * heads, d), F32), pltpu.VMEM((128, n), F32)),
        operands=6,
        flops=1 << 31,
    )(flat(key_vectors), flat(values), own, came, total, log_decay)
    start = lax.dynamic_slice_in_dim(initial_state, (place % groups) * per, per, 0)

    before, upper, came, later = run_map, flag(0), start, flag(0)
    if rounds == 2:
        other = lax.ppermute(run_map, "seq", flipped(groups))
        other, wu = lax.optimization_barrier((other, wu))
        upper = flag(run & 1)
        before = other
        middle = call(
            functools.partial(middle_kernel, per), shape(per, d, d), scalars=1, operands=3
        )(upper, run_map, other, start)
    elif rounds:
        eye = jnp.broadcast_to(jnp.eye(d, 2 * d, dtype=F32), run_map.shape)
        before, upper, window = eye, flag(1), run_map
        for r in range(rounds - 1):
            other = lax.ppermute(window, "seq", flipped(groups << r))
            high = (run >> r) & 1 == 1
            before = jnp.where(high, chain(before, other), before)
            window = chain(jnp.where(high, window, other), jnp.where(high, other, window))
        middle = exact(window[..., :d], start) + window[..., d:]
    if rounds:
        mirror = [(i, (runs - 1 - i // groups) * groups + i % groups) for i in range(count)]
        came = lax.ppermute(middle, "seq", mirror)
        later = flag(run >= runs // 2)
    rows = n + (blocks - 1) * d
    left, right = call(
        output_kernel,
        (shape(heads, rows, 2 * d, dtype=BF16), shape(heads, rows, d)),
        scratch=(pltpu.VMEM((n * heads, d), F32), pltpu.VMEM((128, n), F32)),
        operands=4,
        flops=1 << 30,
    )(flat(queries), flat(key_vectors), cum, wu)
    came, left = lax.optimization_barrier((came, left))
    entries = call(
        functools.partial(enter_kernel, groups, per),
        [shape(per, d, d)] * groups,
        scratch=(pltpu.VMEM((groups, per, d, d), F32),),
        scalars=3,
        operands=4,
        flops=1 << 27,
    )(rank, upper, later, prefix, before, start, came)

    states = [entries[0]] + [
        lax.ppermute(entries[slot], "seq", flipped(slot)) for slot in range(1, groups)
    ]
    gated, block_states = call(
        functools.partial(finish_kernel, groups, per),
        (shape(n * heads, d, dtype=BF16), shape(blocks, heads, d, d)),
        scratch=(pltpu.VMEM((n * heads, d), F32), pltpu.VMEM((n * heads, d), F32)),
        scalars=1,
        operands=groups + 3,
        flops=1 << 28,
    )(rank, *states, left, right, flat(out_gate))
    return (gated.reshape(n, heads, d), block_states)


def solution(mesh):
    return jax.shard_map(
        on_device,
        mesh=mesh,
        in_specs=(
            P("seq", "head", None),
            P("seq", "head", None),
            P("seq", "head", None),
            P("seq", "head", None),
            P("seq", "head"),
            P(None, "head"),
            P("head", "seq"),
            P("head", None, None),
        ),
        out_specs=(P("seq", "head", None), P("seq", "head", None, None)),
        check_vma=False,
    )
```

time: 64 us -> 59.5 us (0.930); the launches traced: 63.2 us -> 59.3 us
  waiting for transfers between devices: 26.2 us -> 21.9 us
  Pallas kernels: 11.2 us -> 13.4 us
  local copies, waits for them, and re-layouts: 2.75 us -> 1.7 us
  starting transfers between devices: 22.3 us -> 21.6 us
    ppermute x1, waiting for transfers between devices: 5.86 us -> 1.16 us  [on_device(): other = lax.ppermute(run_map, 'seq', flipped(groups))]
    pallas_call x4 -> x6, Pallas kernels: 8.18 us -> 10.4 us  [the longest x1 4.51 us: on_device(): call(functools.partial(run_kernel, groups, per, tokens_all), (shape(max(g...]
    ppermute x3, waiting for transfers between devices: 2.29 us -> 4.48 us  [on_device(): lax.ppermute(entries[slot], 'seq', flipped(slot))]
    ppermute x9, waiting for transfers between devices: 18.1 us -> 16.2 us  [the longest x4 14.6 us: summed(): return total + lax.ppermute(total, 'seq', flipped(mask))]
    ppermute x9, starting transfers between devices: 18.2 us -> 16.5 us  [the longest x4 9.17 us: summed(): return total + lax.ppermute(total, 'seq', flipped(mask))]
    unnamed x18, local copies, waits for them, and re-layouts: 2.73 us -> 1.69 us
    ppermute x1, starting transfers between devices: 0.56 us -> 1.59 us  [on_device(): other = lax.ppermute(run_map, 'seq', flipped(groups))]
  transfers between devices with their start and end apart: 13 -> 13, of which waited for: 10 -> 9; matrix products, arithmetic and copies ran while one was open for 0% -> 0% of each run, Pallas kernels for 3% -> 9%
where the time goes in v3:
time: 59.5 us; the launch traced here: 59.3 us
  waiting for transfers between devices  21.9 us (37%)
  starting transfers between devices  21.6 us (36%)
  Pallas kernels  13.4 us (23%)
  local copies, waits for them, and re-layouts  1.7 us (3%)
  between operations  0.74 us (1%)
    ppermute x4, waiting for transfers between devices, summed(): return total + lax.ppermute(total, 'seq', flipped(mask))  14.6 us
    ppermute x4, starting transfers between devices, summed(): return total + lax.ppermute(total, 'seq', flipped(mask))  9.17 us
    pallas_call x1, Pallas kernels, on_device(): call(functools.partial(run_kernel, groups, per, tokens_all), (shape(max(g...  4.51 us
    ppermute x3, waiting for transfers between devices, on_device(): lax.ppermute(entries[slot], 'seq', flipped(slot))  4.48 us
    ppermute x1, starting transfers between devices, on_device(): came = lax.ppermute(middle, 'seq', mirror)  3.67 us
    pallas_call x1, Pallas kernels, on_device(): call(functools.partial(own_kernel, tokens_all), (shape(heads, n, 2 * d),...  3.67 us
    ppermute x3, starting transfers between devices, on_device(): exchanged.append(lax.ppermute(packs[slot], 'seq', flipped(slot)))  3.63 us
    ppermute x3, starting transfers between devices, on_device(): lax.ppermute(entries[slot], 'seq', flipped(slot))  3.55 us
  transfers between devices with their start and end apart: 13, of which 9 were waited for; matrix products, arithmetic and copies ran while one was open for 0% of the time, Pallas kernels for 9%

profile of v3, /device:TPU:0, one launch (start us, length us, event | category | flops | bytes accessed | tf_op | source)
XLA Modules:
  0.0 59.3 jit_solution(5492404020961929211)
XLA Ops:
  0.6 0.0 copy-start
  0.6 0.0 copy-start.3
  0.7 1.0 %copy-done.3 = bf16[128,8,128]{2,1,0:T(8,128)(2,1)S(1)} copy-done((bf16[128,8,128]{2,1,0:T(8,128)(2,1)S(1)}, bf16[128,8,128]{2,1,0:T(8,128)(2,1)}, u32[]{:S(2)}) %copy-start.3) | copy-done | bytes 262168
  1.7 0.0 copy-start.5
  1.7 0.0 copy-start.6
  1.7 0.0 copy-start.4
  1.7 0.1 shard_map.95
  1.8 0.0 copy-start.2
  1.8 3.0 %collective-permute-start = (f32[8,128]{1,0:T(8,128)S(1)}, f32[8,128]{1,0:T(8,128)S(1)}, u32[]{:S(2)}, u32[]{:S(2)}) collective-permute-start(f32[8,128]{1,0:T(8,128)S(1)} %shard_map.95), channel_id=1, source_target_pairs={{0,2},{2,0},{4,6},{6,4},{8,10},{10,8},{12,14},{14,12},{16,18},{18,... | collective-permute-start | bytes 12296 | tf_op jit(solution)/shard_map/ppermute | solution.py:428
  4.8 0.0 copy-done.5
  4.8 0.0 copy-done.6
  4.8 0.2 shard_map.96
  5.0 0.0 collective-permute-start.1
  5.0 1.4 %collective-permute-done = f32[8,128]{1,0:T(8,128)S(1)} collective-permute-done((f32[8,128]{1,0:T(8,128)S(1)}, f32[8,128]{1,0:T(8,128)S(1)}, u32[]{:S(2)}, u32[]{:S(2)}) %collective-permute-start) | collective-permute-done | bytes 4128 | tf_op jit(solution)/shard_map/ppermute | solution.py:428
  6.4 0.0 copy-start.7
  6.4 0.0 collective-permute-done.1.came_ref
  6.4 0.0 copy-done.4
  6.4 0.0 copy-done.2
  6.5 0.7 %copy-done.7 = f32[8,128]{1,0:T(8,128)S(1)} copy-done((f32[8,128]{1,0:T(8,128)S(1)}, f32[8,128]{1,0:T(8,128)}, u32[]{:S(2)}) %copy-start.7) | copy-done | bytes 4120
  7.1 0.3 shard_map.97
  7.4 2.1 %collective-permute-start.5 = (f32[2,264,128]{2,1,0:T(8,128)S(1)}, f32[2,264,128]{2,1,0:T(8,128)S(1)}, u32[]{:S(2)}, u32[]{:S(2)}) collective-permute-start(f32[2,264,128]{2,1,0:T(8,128)S(1)} %get-tuple-element.37), channel_id=1, source_target_pairs={{0,2},{2,0},{4,6},{6,4},{8,10},{10,8},{12,14},{14,12},{16,18},{18,... | collective-permute-start | bytes 811016 | tf_op jit(solution)/shard_map/ppermute | solution.py:437
  9.5 1.5 %collective-permute-start.6 = (f32[2,264,128]{2,1,0:T(8,128)S(1)}, f32[2,264,128]{2,1,0:T(8,128)S(1)}, u32[]{:S(2)}, u32[]{:S(2)}) collective-permute-start(f32[2,264,128]{2,1,0:T(8,128)S(1)} %get-tuple-element.38), channel_id=1, source_target_pairs={{0,4},{2,6},{4,0},{6,2},{8,12},{10,14},{12,8},{14,10},{16,20},{18,... | collective-permute-start | bytes 811016 | tf_op jit(solution)/shard_map/ppermute | solution.py:437
  11.0 0.0 collective-permute-start.7
  11.0 2.0 %collective-permute-start.2 = (f32[8,128]{1,0:T(8,128)S(1)}, f32[8,128]{1,0:T(8,128)S(1)}, u32[]{:S(2)}, u32[]{:S(2)}) collective-permute-start(f32[8,128]{1,0:T(8,128)S(1)} %add.22), channel_id=1, source_target_pairs={{0,4},{2,6},{4,0},{6,2},{8,12},{10,14},{12,8},{14,10},{16,20},{18,... | collective-permute-start | bytes 12296 | tf_op jit(solution)/shard_map/ppermute | solution.py:428
  13.0 9.2 %collective-permute-done.2 = f32[8,128]{1,0:T(8,128)S(1)} collective-permute-done((f32[8,128]{1,0:T(8,128)S(1)}, f32[8,128]{1,0:T(8,128)S(1)}, u32[]{:S(2)}, u32[]{:S(2)}) %collective-permute-start.2) | collective-permute-done | bytes 4128 | tf_op jit(solution)/shard_map/ppermute | solution.py:428
  22.1 1.6 %collective-permute-start.3 = (f32[8,128]{1,0:T(8,128)S(1)}, f32[8,128]{1,0:T(8,128)S(1)}, u32[]{:S(2)}, u32[]{:S(2)}) collective-permute-start(f32[8,128]{1,0:T(8,128)S(1)} %add.23), channel_id=1, source_target_pairs={{0,8},{2,10},{4,12},{6,14},{8,0},{10,2},{12,4},{14,6},{16,24},{18,... | collective-permute-start | bytes 12296 | tf_op jit(solution)/shard_map/ppermute | solution.py:428
  23.7 2.0 %collective-permute-done.3 = f32[8,128]{1,0:T(8,128)S(1)} collective-permute-done((f32[8,128]{1,0:T(8,128)S(1)}, f32[8,128]{1,0:T(8,128)S(1)}, u32[]{:S(2)}, u32[]{:S(2)}) %collective-permute-start.3) | collective-permute-done | bytes 4128 | tf_op jit(solution)/shard_map/ppermute | solution.py:428
  25.8 2.6 %collective-permute-start.4 = (f32[8,128]{1,0:T(8,128)S(1)}, f32[8,128]{1,0:T(8,128)S(1)}, u32[]{:S(2)}, u32[]{:S(2)}) collective-permute-start(f32[8,128]{1,0:T(8,128)S(1)} %add.24), channel_id=1, source_target_pairs={{0,16},{2,18},{4,20},{6,22},{8,24},{10,26},{12,28},{14,30},{16,0},... | collective-permute-start | bytes 12296 | tf_op jit(solution)/shard_map/ppermute | solution.py:428
  28.3 2.0 %collective-permute-done.4 = f32[8,128]{1,0:T(8,128)S(1)} collective-permute-done((f32[8,128]{1,0:T(8,128)S(1)}, f32[8,128]{1,0:T(8,128)S(1)}, u32[]{:S(2)}, u32[]{:S(2)}) %collective-permute-start.4) | collective-permute-done | bytes 4128 | tf_op jit(solution)/shard_map/ppermute | solution.py:428
  30.4 0.0 collective-permute-done.5.refs_1_
  30.4 0.0 collective-permute-done.6.refs_2_
  30.4 0.0 collective-permute-done.7.refs_3_
  30.4 4.5 %shard_map.98 = (f32[3,2,128,256]{3,2,1,0:T(8,128)S(1)}, f32[2,128,256]{2,1,0:T(8,128)S(1)}) custom-call(s32[1]{0:T(128)} %bitcast.rank_ref, f32[8,128]{1,0:T(8,128)S(1)} %add.25.total_ref, f32[2,264,128]{2,1,0:T(8,128)S(1)} %get-tuple-element.36.refs_0_, f32[2,264,128]{2,1,0:T(8,128)S(1)} %collective-permute-done.5.refs_1_, ...), custom_call_target="tpu_custom_call" | custom-call | flops 1073741824 | bytes 1048576 | tf_op jit(solution)/shard_map/pallas_call | solution.py:445
  34.9 1.6 %collective-permute-start.8 = (f32[2,128,256]{2,1,0:T(8,128)S(1)}, f32[2,128,256]{2,1,0:T(8,128)S(1)}, u32[]{:S(2)}, u32[]{:S(2)}) collective-permute-start(f32[2,128,256]{2,1,0:T(8,128)S(1)} %get-tuple-element.41.mine_ref), channel_id=1, source_target_pairs={{0,8},{2,10},{4,12},{6,14},{8,0},{10,2},{12,4},{14,6},{16,24},{18,... | collective-permute-start | bytes 786440 | tf_op jit(solution)/shard_map/ppermute | solution.py:465
  36.5 0.0 copy-done
  36.5 3.7 %shard_map.99 = (f32[8,128,256]{2,1,0:T(8,128)S(1)}, f32[8,128]{1,0:T(8,128)S(1)}) custom-call(bf16[1024,128]{1,0:T(8,128)(2,1)S(1)} %bitcast.14, bf16[1024,128]{1,0:T(8,128)(2,1)S(1)} %bitcast.11, f32[8,128]{1,0:T(8,128)S(1)} %get-tuple-element.29.own_ref, f32[8,128]{1,0:T(8,128)S(1)} %collective-permute-done.1.came_ref, f32[8,128]{1,0:T(8,128)S(1)} %add.25.total_ref, ...), custom_call_target="tpu_custom_call" | custom-call | flops 2147483648 | bytes 1048576 | tf_op jit(solution)/shard_map/pallas_call | solution.py:454
  40.2 1.2 %collective-permute-done.8.other_ref.before_ref = f32[2,128,256]{2,1,0:T(8,128)S(1)} collective-permute-done((f32[2,128,256]{2,1,0:T(8,128)S(1)}, f32[2,128,256]{2,1,0:T(8,128)S(1)}, u32[]{:S(2)}, u32[]{:S(2)}) %collective-permute-start.8) | collective-permute-done | bytes 262176 | tf_op jit(solution)/shard_map/ppermute | solution.py:465
  41.3 0.0 copy-start.8
  41.3 0.4 shard_map.100
  41.7 3.7 %collective-permute-start.9 = (f32[2,128,128]{2,1,0:T(8,128)S(1)}, f32[2,128,128]{2,1,0:T(8,128)S(1)}, u32[]{:S(2)}, u32[]{:S(2)}) collective-permute-start(f32[2,128,128]{2,1,0:T(8,128)S(1)} %shard_map.100), channel_id=1, source_target_pairs={{0,24},{2,26},{4,28},{6,30},{8,16},{10,18},{12,20},{14,22},{16,8},... | collective-permute-start | bytes 393224 | tf_op jit(solution)/shard_map/ppermute | solution.py:483
  45.4 0.0 copy-done.8
  45.4 1.7 %shard_map.101 = (bf16[8,256,256]{2,1,0:T(8,128)(2,1)S(1)}, f32[8,256,128]{2,1,0:T(8,128)S(1)}) custom-call(bf16[1024,128]{1,0:T(8,128)(2,1)S(1)} %bitcast.16, bf16[1024,128]{1,0:T(8,128)(2,1)S(1)} %bitcast.15, f32[8,128]{1,0:T(8,128)S(1)} %get-tuple-element.44.cum_ref, f32[8,128,256]{2,1,0:T(8,128)S(1)} %get-tuple-element.45.wu_ref), custom_call_target="tpu_custom_call" | custom-call | flops 1073741824 | bytes 1048576 | tf_op jit(solution)/shard_map/pallas_call | solution.py:486
  47.1 1.6 %collective-permute-done.9.came_ref = f32[2,128,128]{2,1,0:T(8,128)S(1)} collective-permute-done((f32[2,128,128]{2,1,0:T(8,128)S(1)}, f32[2,128,128]{2,1,0:T(8,128)S(1)}, u32[]{:S(2)}, u32[]{:S(2)}) %collective-permute-start.9) | collective-permute-done | bytes 131104 | tf_op jit(solution)/shard_map/ppermute | solution.py:483
  48.7 0.0 copy-start.1
  48.7 0.7 %shard_map.102 = (f32[2,128,128]{2,1,0:T(8,128)S(1)}, f32[2,128,128]{2,1,0:T(8,128)S(1)}, f32[2,128,128]{2,1,0:T(8,128)S(1)}, f32[2,128,128]{2,1,0:T(8,128)S(1)}) custom-call(s32[1]{0:T(128)} %bitcast.rank_ref, s32[1]{0:T(128)} %bitcast.1.upper_ref, s32[1]{0:T(128)} %bitcast.2.later_ref, f32[3,2,128,256]{3,2,1,0:T(8,128)S(1)} %get-tuple-element.40.prefix_ref, ...), custom_call_target="tpu_custom_call" | custom-call | flops 134217728 | bytes 1048576 | tf_op jit(solution)/shard_map/pallas_call | solution.py:494
  49.4 0.1 collective-permute-start.10
  49.5 2.1 %collective-permute-start.11 = (f32[2,128,128]{2,1,0:T(8,128)S(1)}, f32[2,128,128]{2,1,0:T(8,128)S(1)}, u32[]{:S(2)}, u32[]{:S(2)}) collective-permute-start(f32[2,128,128]{2,1,0:T(8,128)S(1)} %get-tuple-element.50), channel_id=1, source_target_pairs={{0,4},{2,6},{4,0},{6,2},{8,12},{10,14},{12,8},{14,10},{16,20},{18,... | collective-permute-start | bytes 393224 | tf_op jit(solution)/shard_map/ppermute | solution.py:504
  51.6 1.4 %collective-permute-start.12 = (f32[2,128,128]{2,1,0:T(8,128)S(1)}, f32[2,128,128]{2,1,0:T(8,128)S(1)}, u32[]{:S(2)}, u32[]{:S(2)}) collective-permute-start(f32[2,128,128]{2,1,0:T(8,128)S(1)} %get-tuple-element.51), channel_id=1, source_target_pairs={{0,6},{2,4},{4,2},{6,0},{8,14},{10,12},{12,10},{14,8},{16,22},{18,... | collective-permute-start | bytes 393224 | tf_op jit(solution)/shard_map/ppermute | solution.py:504
  53.0 1.5 %collective-permute-done.10.refs_1_ = f32[2,128,128]{2,1,0:T(8,128)S(1)} collective-permute-done((f32[2,128,128]{2,1,0:T(8,128)S(1)}, f32[2,128,128]{2,1,0:T(8,128)S(1)}, u32[]{:S(2)}, u32[]{:S(2)}) %collective-permute-start.10) | collective-permute-done | bytes 131104 | tf_op jit(solution)/shard_map/ppermute | solution.py:504
  54.4 1.1 %collective-permute-done.11.refs_2_ = f32[2,128,128]{2,1,0:T(8,128)S(1)} collective-permute-done((f32[2,128,128]{2,1,0:T(8,128)S(1)}, f32[2,128,128]{2,1,0:T(8,128)S(1)}, u32[]{:S(2)}, u32[]{:S(2)}) %collective-permute-start.11) | collective-permute-done | bytes 131104 | tf_op jit(solution)/shard_map/ppermute | solution.py:504
  55.5 1.9 %collective-permute-done.12.refs_3_ = f32[2,128,128]{2,1,0:T(8,128)S(1)} collective-permute-done((f32[2,128,128]{2,1,0:T(8,128)S(1)}, f32[2,128,128]{2,1,0:T(8,128)S(1)}, u32[]{:S(2)}, u32[]{:S(2)}) %collective-permute-start.12) | collective-permute-done | bytes 131104 | tf_op jit(solution)/shard_map/ppermute | solution.py:504
  57.4 0.0 copy-done.1
  57.5 1.9 %shard_map.103 = (bf16[1024,128]{1,0:T(8,128)(2,1)}, f32[2,8,128,128]{3,2,1,0:T(8,128)}) custom-call(s32[1]{0:T(128)} %bitcast.rank_ref, f32[2,128,128]{2,1,0:T(8,128)S(1)} %get-tuple-element.48.refs_0_, f32[2,128,128]{2,1,0:T(8,128)S(1)} %collective-permute-done.10.refs_1_, f32[2,128,128]{2,1,0:T(8,128)S(1)} %collective-permute-done.11.refs_2_, ...), custom_call_target="tpu_custom_call" | custom-call | flops 268435456 | bytes 1048576 | tf_op jit(solution)/shard_map/pallas_call | solution.py:506
  (5 shorter events, 0.0 us)
Async XLA Ops:
  0.6 35.9 %copy-start = (f32[8,128,128]{2,1,0:T(8,128)S(1)}, f32[8,128,128]{2,1,0:T(8,128)}, u32[]{:S(2)}) copy-start(f32[8,128,128]{2,1,0:T(8,128)} %param.15) | copy-start | bytes 1572868
  0.6 1.0 %copy-start.3 = (bf16[128,8,128]{2,1,0:T(8,128)(2,1)S(1)}, bf16[128,8,128]{2,1,0:T(8,128)(2,1)}, u32[]{:S(2)}) copy-start(bf16[128,8,128]{2,1,0:T(8,128)(2,1)} %param.9) | copy-start | bytes 786436
  1.7 3.2 %copy-start.5 = (bf16[128,1024]{1,0:T(8,128)(2,1)S(1)}, bf16[128,1024]{1,0:T(8,128)(2,1)}, u32[]{:S(2)}) copy-start(bf16[128,1024]{1,0:T(8,128)(2,1)} %inputs_ref.1) | copy-start | bytes 786436
  1.7 3.2 %copy-start.6 = (bf16[16,1024]{1,0:T(8,128)(2,1)S(1)}, bf16[16,1024]{1,0:T(8,128)(2,1)}, u32[]{:S(2)}) copy-start(bf16[16,1024]{1,0:T(8,128)(2,1)} %weight_ref.1) | copy-start | bytes 98308
  1.7 4.8 %copy-start.4 = (bf16[128,8,128]{2,1,0:T(8,128)(2,1)S(1)}, bf16[128,8,128]{2,1,0:T(8,128)(2,1)}, u32[]{:S(2)}) copy-start(bf16[128,8,128]{2,1,0:T(8,128)(2,1)} %param.9) | copy-start | bytes 786436
  1.8 4.6 %copy-start.2 = (bf16[128,8,128]{2,1,0:T(8,128)(2,1)S(1)}, bf16[128,8,128]{2,1,0:T(8,128)(2,1)}, u32[]{:S(2)}) copy-start(bf16[128,8,128]{2,1,0:T(8,128)(2,1)} %param.10) | copy-start | bytes 786436
  1.8 4.6 %collective-permute-start = (f32[8,128]{1,0:T(8,128)S(1)}, f32[8,128]{1,0:T(8,128)S(1)}, u32[]{:S(2)}, u32[]{:S(2)}) collective-permute-start(f32[8,128]{1,0:T(8,128)S(1)} %shard_map.95), channel_id=1, source_target_pairs={{0,2},{2,0},{4,6},{6,4},{8,10},{10,8},{12,14},{14,12},{16,18},{18,... | collective-permute-start | bytes 12296 | tf_op jit(solution)/shard_map/ppermute | solution.py:428
  5.0 1.4 %collective-permute-start.1 = (f32[8,128]{1,0:T(8,128)S(1)}, f32[8,128]{1,0:T(8,128)S(1)}, u32[]{:S(2)}, u32[]{:S(2)}) collective-permute-start(f32[8,128]{1,0:T(8,128)S(1)} %get-tuple-element.30), channel_id=1, source_target_pairs={{0,1},{1,0},{2,3},{3,2},{4,5},{5,4},{6,7},{7,6},{8,9},{9,8},{10,11... | collective-permute-start | bytes 12296 | tf_op jit(solution)/shard_map/ppermute | solution.py:414
  6.4 0.7 %copy-start.7 = (f32[8,128]{1,0:T(8,128)S(1)}, f32[8,128]{1,0:T(8,128)}, u32[]{:S(2)}) copy-start(f32[8,128]{1,0:T(8,128)} %decay_ref.3) | copy-start | bytes 12292
  7.4 23.0 %collective-permute-start.5 = (f32[2,264,128]{2,1,0:T(8,128)S(1)}, f32[2,264,128]{2,1,0:T(8,128)S(1)}, u32[]{:S(2)}, u32[]{:S(2)}) collective-permute-start(f32[2,264,128]{2,1,0:T(8,128)S(1)} %get-tuple-element.37), channel_id=1, source_target_pairs={{0,2},{2,0},{4,6},{6,4},{8,10},{10,8},{12,14},{14,12},{16,18},{18,... | collective-permute-start | bytes 811016 | tf_op jit(solution)/shard_map/ppermute | solution.py:437
  9.5 20.9 %collective-permute-start.6 = (f32[2,264,128]{2,1,0:T(8,128)S(1)}, f32[2,264,128]{2,1,0:T(8,128)S(1)}, u32[]{:S(2)}, u32[]{:S(2)}) collective-permute-start(f32[2,264,128]{2,1,0:T(8,128)S(1)} %get-tuple-element.38), channel_id=1, source_target_pairs={{0,4},{2,6},{4,0},{6,2},{8,12},{10,14},{12,8},{14,10},{16,20},{18,... | collective-permute-start | bytes 811016 | tf_op jit(solution)/shard_map/ppermute | solution.py:437
  11.0 19.4 %collective-permute-start.7 = (f32[2,264,128]{2,1,0:T(8,128)S(1)}, f32[2,264,128]{2,1,0:T(8,128)S(1)}, u32[]{:S(2)}, u32[]{:S(2)}) collective-permute-start(f32[2,264,128]{2,1,0:T(8,128)S(1)} %get-tuple-element.39), channel_id=1, source_target_pairs={{0,6},{2,4},{4,2},{6,0},{8,14},{10,12},{12,10},{14,8},{16,22},{18,... | collective-permute-start | bytes 811016 | tf_op jit(solution)/shard_map/ppermute | solution.py:437
  11.0 11.1 %collective-permute-start.2 = (f32[8,128]{1,0:T(8,128)S(1)}, f32[8,128]{1,0:T(8,128)S(1)}, u32[]{:S(2)}, u32[]{:S(2)}) collective-permute-start(f32[8,128]{1,0:T(8,128)S(1)} %add.22), channel_id=1, source_target_pairs={{0,4},{2,6},{4,0},{6,2},{8,12},{10,14},{12,8},{14,10},{16,20},{18,... | collective-permute-start | bytes 12296 | tf_op jit(solution)/shard_map/ppermute | solution.py:428
  22.1 3.6 %collective-permute-start.3 = (f32[8,128]{1,0:T(8,128)S(1)}, f32[8,128]{1,0:T(8,128)S(1)}, u32[]{:S(2)}, u32[]{:S(2)}) collective-permute-start(f32[8,128]{1,0:T(8,128)S(1)} %add.23), channel_id=1, source_target_pairs={{0,8},{2,10},{4,12},{6,14},{8,0},{10,2},{12,4},{14,6},{16,24},{18,... | collective-permute-start | bytes 12296 | tf_op jit(solution)/shard_map/ppermute | solution.py:428
  25.8 4.6 %collective-permute-start.4 = (f32[8,128]{1,0:T(8,128)S(1)}, f32[8,128]{1,0:T(8,128)S(1)}, u32[]{:S(2)}, u32[]{:S(2)}) collective-permute-start(f32[8,128]{1,0:T(8,128)S(1)} %add.24), channel_id=1, source_target_pairs={{0,16},{2,18},{4,20},{6,22},{8,24},{10,26},{12,28},{14,30},{16,0},... | collective-permute-start | bytes 12296 | tf_op jit(solution)/shard_map/ppermute | solution.py:428
  34.9 6.4 %collective-permute-start.8 = (f32[2,128,256]{2,1,0:T(8,128)S(1)}, f32[2,128,256]{2,1,0:T(8,128)S(1)}, u32[]{:S(2)}, u32[]{:S(2)}) collective-permute-start(f32[2,128,256]{2,1,0:T(8,128)S(1)} %get-tuple-element.41.mine_ref), channel_id=1, source_target_pairs={{0,8},{2,10},{4,12},{6,14},{8,0},{10,2},{12,4},{14,6},{16,24},{18,... | collective-permute-start | bytes 786440 | tf_op jit(solution)/shard_map/ppermute | solution.py:465
  41.3 4.1 %copy-start.8 = (bf16[128,8,128]{2,1,0:T(8,128)(2,1)S(1)}, bf16[128,8,128]{2,1,0:T(8,128)(2,1)}, u32[]{:S(2)}) copy-start(bf16[128,8,128]{2,1,0:T(8,128)(2,1)} %param.8) | copy-start | bytes 786436
  41.7 6.9 %collective-permute-start.9 = (f32[2,128,128]{2,1,0:T(8,128)S(1)}, f32[2,128,128]{2,1,0:T(8,128)S(1)}, u32[]{:S(2)}, u32[]{:S(2)}) collective-permute-start(f32[2,128,128]{2,1,0:T(8,128)S(1)} %shard_map.100), channel_id=1, source_target_pairs={{0,24},{2,26},{4,28},{6,30},{8,16},{10,18},{12,20},{14,22},{16,8},... | collective-permute-start | bytes 393224 | tf_op jit(solution)/shard_map/ppermute | solution.py:483
  48.7 8.8 %copy-start.1 = (bf16[128,8,128]{2,1,0:T(8,128)(2,1)S(1)}, bf16[128,8,128]{2,1,0:T(8,128)(2,1)}, u32[]{:S(2)}) copy-start(bf16[128,8,128]{2,1,0:T(8,128)(2,1)} %param.11) | copy-start | bytes 786436
  49.4 5.0 %collective-permute-start.10 = (f32[2,128,128]{2,1,0:T(8,128)S(1)}, f32[2,128,128]{2,1,0:T(8,128)S(1)}, u32[]{:S(2)}, u32[]{:S(2)}) collective-permute-start(f32[2,128,128]{2,1,0:T(8,128)S(1)} %get-tuple-element.49), channel_id=1, source_target_pairs={{0,2},{2,0},{4,6},{6,4},{8,10},{10,8},{12,14},{14,12},{16,18},{18,... | collective-permute-start | bytes 393224 | tf_op jit(solution)/shard_map/ppermute | solution.py:504
  49.5 6.0 %collective-permute-start.11 = (f32[2,128,128]{2,1,0:T(8,128)S(1)}, f32[2,128,128]{2,1,0:T(8,128)S(1)}, u32[]{:S(2)}, u32[]{:S(2)}) collective-permute-start(f32[2,128,128]{2,1,0:T(8,128)S(1)} %get-tuple-element.50), channel_id=1, source_target_pairs={{0,4},{2,6},{4,0},{6,2},{8,12},{10,14},{12,8},{14,10},{16,20},{18,... | collective-permute-start | bytes 393224 | tf_op jit(solution)/shard_map/ppermute | solution.py:504
  51.6 5.9 %collective-permute-start.12 = (f32[2,128,128]{2,1,0:T(8,128)S(1)}, f32[2,128,128]{2,1,0:T(8,128)S(1)}, u32[]{:S(2)}, u32[]{:S(2)}) collective-permute-start(f32[2,128,128]{2,1,0:T(8,128)S(1)} %get-tuple-element.51), channel_id=1, source_target_pairs={{0,6},{2,4},{4,2},{6,0},{8,14},{10,12},{12,10},{14,8},{16,22},{18,... | collective-permute-start | bytes 393224 | tf_op jit(solution)/shard_map/ppermute | solution.py:504

commit v4 on v3

--- a/solution.py
+++ b/solution.py
@@ -76,14 +76,13 @@
     return jax.ShapeDtypeStruct(dims, dtype)
 
 
-def norms_kernel(heads, key_ref, total_ref):
-    keys = key_ref[...].astype(F32)
-    squares = keys * keys
-    rows = squares.shape[0]
-    total_ref[...] = squares.reshape(rows // heads, heads, squares.shape[1]).sum(0)
-
-
-def logits_kernel(heads, pair, side_ref, weight_ref, inputs_ref, *refs):
+def zeros_kernel(out_ref):
+    out_ref[...] = jnp.zeros_like(out_ref)
+
+
+def stats_kernel(
+    heads, pair, side_ref, zeros_ref, key_ref, weight_ref, inputs_ref, decay_ref, total_ref, cum_ref, *refs
+):
     logits = lax.dot_general(
         weight_ref[...], inputs_ref[...], (((1,), (1,)), ((), ())), preferred_element_type=F32
     )
@@ -95,14 +94,25 @@
         theirs_ref[...] = full_ref[pl.ds(heads - mine, heads), :]
     else:
         refs[0][...] = logits
+    cum = decay_ref[...]
+    lane = lax.broadcasted_iota(jnp.int32, cum.shape, 1)
+    step = 1
+    while step < cum.shape[1]:
+        cum = cum + jnp.where(lane >= step, pltpu.roll(cum, step, 1), 0.0)
+        step *= 2
+    cum_ref[...] = cum
+    keys = key_ref[...].astype(F32)
+    squares = keys * keys
+    rows = squares.shape[0]
+    total_ref[...] = zeros_ref[...] + squares.reshape(rows // heads, heads, squares.shape[1]).sum(0)
 
 
 def pack_kernel(
-    groups, per, rank_ref, key_ref, value_ref, decay_ref, own_ref, came_ref, *refs
+    groups, per, rank_ref, key_ref, value_ref, cum_ref, own_ref, came_ref, *refs
 ):
-    out_refs, (flat_ref, logit_ref) = refs[:groups], refs[groups:]
-    heads, n = decay_ref.shape
-    logit_ref[...] = own_ref[...] + came_ref[...]
+    out_refs, (beta_ref, flat_ref) = refs[:groups], refs[groups:]
+    heads, n = cum_ref.shape
+    beta_ref[...] = 1.0 / (1.0 + jnp.exp(-(own_ref[...] + came_ref[...])))
     for at, source in enumerate((key_ref, value_ref)):
         flat_ref[...] = source[...].astype(F32)
         for slot in range(groups):
@@ -114,29 +124,18 @@
     for slot in range(groups):
         for i in range(per):
             head = (slot ^ rank_ref[0]) * per + i
-            out_refs[slot][i, 2 * n : 2 * n + 1] = decay_ref[pl.ds(head, 1), :]
-            out_refs[slot][i, 2 * n + 1 : 2 * n + 2] = logit_ref[pl.ds(head, 1), :]
+            out_refs[slot][i, 2 * n : 2 * n + 1] = cum_ref[pl.ds(head, 1), :]
+            out_refs[slot][i, 2 * n + 1 : 2 * n + 2] = beta_ref[pl.ds(head, 1), :]
             out_refs[slot][i, 2 * n + 2 :] = jnp.zeros((6, n), F32)
-
-
-def sums_along(decay):
-    lane = lax.broadcasted_iota(jnp.int32, decay.shape, 1)
-    step = 1
-    while step < decay.shape[1]:
-        decay = decay + jnp.where(lane >= step, pltpu.roll(decay, step, 1), 0.0)
-        step *= 2
-    return decay
 
 
 def limits(total, tokens_all):
     return jnp.sqrt(jnp.sum(total, 1, keepdims=True) / tokens_all + EPSILON)
 
 
-def solve(keys, values, decay, logits, limit, rows_ref):
-    items, n = decay.shape
+def solve(keys, values, cum, beta, limit, rows_ref):
+    items, n = cum.shape
     row, col = iotas(n, n)
-    cum = sums_along(decay)
-    beta = 1.0 / (1.0 + jnp.exp(-logits))
     keys_t = [key.T for key in keys]
     grams = [mm(key, key_t) for key, key_t in zip(keys, keys_t)]
     norm = jnp.concatenate(
@@ -186,7 +185,7 @@
             jnp.concatenate([value, value], 0),
         )
         writes.append(jnp.concatenate([w, u], 1) * column(2, item))
-    return writes, keys_t, cum, [column(0, item) for item in range(items)]
+    return writes, keys_t, [column(0, item) for item in range(items)]
 
 
 def read_map(write, key_t, carry, lift, row, col):
@@ -198,26 +197,35 @@
     return jnp.concatenate([ends - both[:, :d], both[:, d:]], 1)
 
 
-def run_kernel(groups, per, tokens_all, rank_ref, total_ref, *refs):
-    packs, (prefix_ref, run_ref, rows_ref, held_ref) = refs[:groups], refs[groups:]
+def chunk_maps(packs, per, tokens_all, rank_ref, total_ref, rows_ref):
     n = total_ref.shape[1]
     row, col = iotas(n, n)
-    items = [(slot, i) for slot in range(groups) for i in range(per)]
+    items = [(pack, i) for pack in packs for i in range(per)]
     limit = limits(total_ref[...], tokens_all)
     rows_ref[0 : limit.shape[0], :] = jnp.broadcast_to(limit, (limit.shape[0], n))
     limit = jnp.concatenate(
         [rows_ref[pl.ds(rank_ref[0] * per + i, 1), :] for _, i in items], 0
     )
-    keys = [packs[slot][i, 0:n].astype(BF16) for slot, i in items]
-    values = [packs[slot][i, n : 2 * n].astype(BF16) for slot, i in items]
-    decay = jnp.concatenate([packs[slot][i, 2 * n : 2 * n + 1] for slot, i in items], 0)
-    logits = jnp.concatenate([packs[slot][i, 2 * n + 1 : 2 * n + 2] for slot, i in items], 0)
-    writes, keys_t, cum, cum_columns = solve(keys, values, decay, logits, limit, rows_ref)
-    for item, (slot, i) in enumerate(items):
+    keys = [pack[i, 0:n].astype(BF16) for pack, i in items]
+    values = [pack[i, n : 2 * n].astype(BF16) for pack, i in items]
+    cum = jnp.concatenate([pack[i, 2 * n : 2 * n + 1] for pack, i in items], 0)
+    beta = jnp.concatenate([pack[i, 2 * n + 1 : 2 * n + 2] for pack, i in items], 0)
+    writes, keys_t, cum_columns = solve(keys, values, cum, beta, limit, rows_ref)
+    maps = []
+    for item in range(len(items)):
         last = cum[item : item + 1, n - 1 : n]
-        held_ref[slot ^ rank_ref[0], i] = read_map(
-            writes[item], keys_t[item], jnp.exp(last - cum_columns[item]), jnp.exp(last), row, col
+        maps.append(
+            read_map(
+                writes[item], keys_t[item], jnp.exp(last - cum_columns[item]), jnp.exp(last), row, col
+            )
         )
+    return maps
+
+
+def run_kernel(groups, per, tokens_all, rank_ref, total_ref, *refs):
+    packs, (prefix_ref, run_ref, rows_ref, held_ref) = refs[:groups], refs[groups:]
+    for item, found in enumerate(chunk_maps(packs, per, tokens_all, rank_ref, total_ref, rows_ref)):
+        held_ref[(item // per) ^ rank_ref[0], item % per] = found
     so_far = [held_ref[0, i] for i in range(per)]
     for place in range(1, groups):
         for i in range(per):
@@ -228,32 +236,15 @@
 
 
 def own_kernel(
-    tokens_all,
-    key_ref,
-    value_ref,
-    own_ref,
-    came_ref,
-    total_ref,
-    decay_ref,
-    wu_ref,
-    cum_ref,
-    flat_ref,
-    rows_ref,
+    tokens_all, key_ref, value_ref, beta_ref, total_ref, cum_ref, wu_ref, flat_ref, rows_ref
 ):
-    heads, n = decay_ref.shape
+    heads, n = cum_ref.shape
     flat_ref[...] = key_ref[...].astype(F32)
     keys = [flat_ref[pl.ds(h, n, stride=heads), :].astype(BF16) for h in range(heads)]
     flat_ref[...] = value_ref[...].astype(F32)
     values = [flat_ref[pl.ds(h, n, stride=heads), :].astype(BF16) for h in range(heads)]
-    writes, _, cum, _ = solve(
-        keys,
-        values,
-        decay_ref[...],
-        own_ref[...] + came_ref[...],
-        limits(total_ref[...], tokens_all),
-        rows_ref,
-    )
-    cum_ref[...] = cum
+    limit = limits(total_ref[...], tokens_all)
+    writes, _, _ = solve(keys, values, cum_ref[...], beta_ref[...], limit, rows_ref)
     for h in range(heads):
         wu_ref[h] = writes[h]
 
@@ -323,19 +314,33 @@
         state_ref[i] = apply(latter, apply(earlier, start_ref[i]))
 
 
-def enter_kernel(
-    groups, per, rank_ref, upper_ref, later_ref, prefix_ref, before_ref, start_ref, came_ref, *refs
-):
-    out_refs, out_ref = refs[:groups], refs[groups]
+def reach_kernel(groups, per, upper_ref, prefix_ref, before_ref, step_ref, offset_ref):
+    d = before_ref.shape[1]
+    row, col = iotas(d, 2 * d)
+    upper = upper_ref[0] != 0
     for i in range(per):
-        state = jnp.where(later_ref[0] != 0, came_ref[i], start_ref[i])
-        moved = apply(before_ref[i], state)
-        state = jnp.where(upper_ref[0] != 0, moved, state)
-        out_ref[rank_ref[0], i] = state
+        before = before_ref[i]
+        found = [jnp.where(upper, before, jnp.where(row == col, 1.0, 0.0))]
         for place in range(1, groups):
-            out_ref[place ^ rank_ref[0], i] = apply(prefix_ref[place - 1, i], state)
+            prefix = prefix_ref[place - 1, i]
+            found.append(jnp.where(upper, join(prefix, before), prefix))
+        for place in range(groups):
+            step_ref[place, i] = jnp.concatenate(split(found[place][:, :d]), 1)
+            offset_ref[place, i] = found[place][:, d:]
+
+
+def enter_kernel(groups, per, rank_ref, later_ref, step_ref, offset_ref, start_ref, came_ref, *refs):
+    out_refs, (held_ref,) = refs[:groups], refs[groups:]
+    d = start_ref.shape[1]
+    for i in range(per):
+        high, low = split(jnp.where(later_ref[0] != 0, came_ref[i], start_ref[i]))
+        for place in range(groups):
+            step = step_ref[place, i]
+            held_ref[place ^ rank_ref[0], i] = (
+                mm(step, jnp.concatenate([high, high], 0)) + mm(step[:, :d], low) + offset_ref[place, i]
+            )
     for slot in range(groups):
-        out_refs[slot][...] = out_ref[slot]
+        out_refs[slot][...] = held_ref[slot]
 
 
 def finish_kernel(groups, per, rank_ref, *refs):
@@ -398,47 +403,45 @@
 
     pair = lax.axis_size("head") == 2
     all_heads = beta_weight.shape[0]
-    total = call(
-        functools.partial(norms_kernel, heads), shape(heads, d), operands=1, flops=1 << 31
-    )(flat(key_vectors))
-    logits = call(
-        functools.partial(logits_kernel, heads, pair),
-        [shape(heads, n)] * 2 if pair else [shape(all_heads, n)],
+    zeros = call(zeros_kernel, shape(heads, d), flops=1 << 31)()
+    total, cum, *logits = call(
+        functools.partial(stats_kernel, heads, pair),
+        [shape(heads, d), shape(heads, n)]
+        + ([shape(heads, n)] * 2 if pair else [shape(all_heads, n)]),
         scratch=(pltpu.VMEM((all_heads, n), F32),) if pair else (),
         scalars=1,
-        operands=2,
-        flops=1 << 24,
-    )(flag(lax.axis_index("head")), beta_weight, inputs)
+        operands=5,
+        flops=1 << 31,
+    )(flag(lax.axis_index("head")), zeros, flat(key_vectors), beta_weight, inputs, log_decay)
     if pair:
         own, theirs = logits
         came = lax.ppermute(theirs, "head", [(0, 1), (1, 0)])
     else:
         own = lax.psum_scatter(logits[0], "head", scatter_dimension=0, tiled=True)
         came = jnp.zeros_like(own)
-    packs = call(
+    packing = call(
         functools.partial(pack_kernel, groups, per),
-        [shape(per, 2 * n + 8, d)] * groups,
-        scratch=(pltpu.VMEM((n * heads, d), F32), pltpu.VMEM((heads, n), F32)),
+        [shape(per, 2 * n + 8, d)] * groups + [shape(heads, n)],
+        scratch=(pltpu.VMEM((n * heads, d), F32),),
         scalars=1,
         operands=5,
         flops=1 << 24,
-    )(rank, flat(key_vectors), flat(values), log_decay, own, came)
-
-    def summed(total, mask):
-        return total + lax.ppermute(total, "seq", flipped(mask))
+    )
+    *packs, beta = packing(rank, flat(key_vectors), flat(values), cum, own, came)
+
+    def shared(total, mask):
+        return lax.ppermute(total, "seq", flipped(mask))
 
     for slot in range(1, groups):
         if slot & (slot - 1) == 0:
-            total = summed(total, slot)
-            if slot == 1:
-                total, packs = lax.optimization_barrier((total, packs))
+            total = total + shared(total, slot)
     exchanged = []
     for slot in range(1, groups):
         exchanged.append(lax.ppermute(packs[slot], "seq", flipped(slot)))
     packs = [packs[0]] + exchanged
     mask = groups
     while mask < count:
-        total = summed(total, mask)
+        total = total + shared(total, mask)
         mask *= 2
 
     tokens_all = n * count
@@ -451,13 +454,14 @@
         flops=1 << 30,
     )(rank, total, *packs)
 
-    wu, cum = call(
+    wu = call(
         functools.partial(own_kernel, tokens_all),
-        (shape(heads, n, 2 * d), shape(heads, n)),
+        shape(heads, n, 2 * d),
         scratch=(pltpu.VMEM((n * heads, d), F32), pltpu.VMEM((128, n), F32)),
-        operands=6,
+        operands=5,
         flops=1 << 31,
-    )(flat(key_vectors), flat(values), own, came, total, log_decay)
+    )(flat(key_vectors), flat(values), beta, total, cum)
+
     start = lax.dynamic_slice_in_dim(initial_state, (place % groups) * per, per, 0)
 
     before, upper, came, later = run_map, flag(0), start, flag(0)
@@ -490,15 +494,22 @@
         operands=4,
         flops=1 << 30,
     )(flat(queries), flat(key_vectors), cum, wu)
-    came, left = lax.optimization_barrier((came, left))
+    step, offset = call(
+        functools.partial(reach_kernel, groups, per),
+        (shape(groups, per, d, 2 * d, dtype=BF16), shape(groups, per, d, d)),
+        scalars=1,
+        operands=2,
+        flops=1 << 28,
+    )(upper, prefix, before)
+    came, left, step = lax.optimization_barrier((came, left, step))
     entries = call(
         functools.partial(enter_kernel, groups, per),
         [shape(per, d, d)] * groups,
         scratch=(pltpu.VMEM((groups, per, d, d), F32),),
-        scalars=3,
+        scalars=2,
         operands=4,
         flops=1 << 27,
-    )(rank, upper, later, prefix, before, start, came)
+    )(rank, later, step, offset, start, came)
 
     states = [entries[0]] + [
         lax.ppermute(entries[slot], "seq", flipped(slot)) for slot in range(1, groups)

time: 59.5 us -> 62.2 us (1.045)
  starting transfers between devices: 21.6 us -> 24 us
  local copies, waits for them, and re-layouts: 1.7 us -> 2.59 us
  waiting for transfers between devices: 21.9 us -> 21.1 us
    ppermute x1, starting transfers between devices: 3.67 us -> 5.31 us  [on_device(): came = lax.ppermute(middle, 'seq', mirror)]
    ppermute x1, waiting for transfers between devices: 1.59 us -> 0.41 us  [on_device(): came = lax.ppermute(middle, 'seq', mirror)]
    ppermute x1, waiting for transfers between devices: 1.16 us -> 0.01 us  [on_device(): other = lax.ppermute(run_map, 'seq', flipped(groups))]
    unnamed x18 -> x20, local copies, waits for them, and re-layouts: 1.69 us -> 2.58 us
    ppermute x3, waiting for transfers between devices: 4.48 us -> 5.33 us  [on_device(): lax.ppermute(entries[slot], 'seq', flipped(slot))]
    ppermute x1, waiting for transfers between devices: 0.01 us -> 0.82 us  [on_device(): came = lax.ppermute(theirs, 'head', [(0, 1), (1, 0)])]
    ppermute x4, starting transfers between devices: 9.17 us -> 8.37 us  [shared(): return lax.ppermute(total, 'seq', flipped(mask))]
    ppermute x3, starting transfers between devices: 3.63 us -> 4.42 us  [on_device(): exchanged.append(lax.ppermute(packs[slot], 'seq', flipped(slot)))]
where the time goes in v4:
time: 62.2 us; the launch traced here: 62 us
  starting transfers between devices  24 us (39%)
  waiting for transfers between devices  21.1 us (34%)
  Pallas kernels  13.5 us (22%)
  local copies, waits for them, and re-layouts  2.59 us (4%)
  between operations  0.78 us (1%)
    ppermute x4, waiting for transfers between devices, shared(): return lax.ppermute(total, 'seq', flipped(mask))  14.5 us
    ppermute x4, starting transfers between devices, shared(): return lax.ppermute(total, 'seq', flipped(mask))  8.37 us
    ppermute x3, waiting for transfers between devices, on_device(): lax.ppermute(entries[slot], 'seq', flipped(slot))  5.33 us
    ppermute x1, starting transfers between devices, on_device(): came = lax.ppermute(middle, 'seq', mirror)  5.31 us
    ppermute x3, starting transfers between devices, on_device(): exchanged.append(lax.ppermute(packs[slot], 'seq', flipped(slot)))  4.42 us
    pallas_call x1, Pallas kernels, on_device(): call(functools.partial(run_kernel, groups, per, tokens_all), (shape(max(g...  4.39 us
    pallas_call x1, Pallas kernels, on_device(): call(functools.partial(own_kernel, tokens_all), shape(heads, n, 2 * d), s...  3.57 us
    ppermute x3, starting transfers between devices, on_device(): lax.ppermute(entries[slot], 'seq', flipped(slot))  3.55 us
  transfers between devices with their start and end apart: 13, of which 9 were waited for; matrix products, arithmetic and copies ran while one was open for 0% of the time, Pallas kernels for 9%

profile of v4, /device:TPU:0, one launch (start us, length us, event | category | flops | bytes accessed | tf_op | source)
XLA Modules:
  0.0 62.0 jit_solution(9724574145689377105)
XLA Ops:
  0.6 0.0 copy-start
  0.6 0.0 copy-start.3
  0.7 0.0 copy-start.4
  0.7 0.0 copy-start.6
  0.7 0.0 copy-start.7
  0.7 1.0 %copy-done.3 = bf16[128,8,128]{2,1,0:T(8,128)(2,1)S(1)} copy-done((bf16[128,8,128]{2,1,0:T(8,128)(2,1)S(1)}, bf16[128,8,128]{2,1,0:T(8,128)(2,1)}, u32[]{:S(2)}) %copy-start.3) | copy-done | bytes 262168
  1.7 0.1 copy-done.4
  1.7 0.0 copy-done.6
  1.7 0.0 copy-done.7
  1.7 0.0 copy-start.2
  1.7 0.5 shard_map.96
  2.2 0.5 collective-permute-start.4
  2.7 0.8 %collective-permute-done.4.came_ref = f32[8,128]{1,0:T(8,128)S(1)} collective-permute-done((f32[8,128]{1,0:T(8,128)S(1)}, f32[8,128]{1,0:T(8,128)S(1)}, u32[]{:S(2)}, u32[]{:S(2)}) %collective-permute-start.4) | collective-permute-done | bytes 4128 | tf_op jit(solution)/shard_map/ppermute | solution.py:418
  3.5 0.0 copy-done.2
  3.6 0.3 shard_map.97
  3.8 2.9 %collective-permute-start.5 = (f32[2,264,128]{2,1,0:T(8,128)S(1)}, f32[2,264,128]{2,1,0:T(8,128)S(1)}, u32[]{:S(2)}, u32[]{:S(2)}) collective-permute-start(f32[2,264,128]{2,1,0:T(8,128)S(1)} %get-tuple-element.33), channel_id=1, source_target_pairs={{0,2},{2,0},{4,6},{6,4},{8,10},{10,8},{12,14},{14,12},{16,18},{18,... | collective-permute-start | bytes 811016 | tf_op jit(solution)/shard_map/ppermute | solution.py:440
  6.7 1.5 %collective-permute-start.6 = (f32[2,264,128]{2,1,0:T(8,128)S(1)}, f32[2,264,128]{2,1,0:T(8,128)S(1)}, u32[]{:S(2)}, u32[]{:S(2)}) collective-permute-start(f32[2,264,128]{2,1,0:T(8,128)S(1)} %get-tuple-element.34), channel_id=1, source_target_pairs={{0,4},{2,6},{4,0},{6,2},{8,12},{10,14},{12,8},{14,10},{16,20},{18,... | collective-permute-start | bytes 811016 | tf_op jit(solution)/shard_map/ppermute | solution.py:440
  8.2 0.0 collective-permute-start.7
  8.2 1.9 %collective-permute-start = (f32[8,128]{1,0:T(8,128)S(1)}, f32[8,128]{1,0:T(8,128)S(1)}, u32[]{:S(2)}, u32[]{:S(2)}) collective-permute-start(f32[8,128]{1,0:T(8,128)S(1)} %get-tuple-element.28), channel_id=1, source_target_pairs={{0,2},{2,0},{4,6},{6,4},{8,10},{10,8},{12,14},{14,12},{16,18},{18,... | collective-permute-start | bytes 12296 | tf_op jit(solution)/shard_map/ppermute | solution.py:433
  10.2 9.3 %collective-permute-done = f32[8,128]{1,0:T(8,128)S(1)} collective-permute-done((f32[8,128]{1,0:T(8,128)S(1)}, f32[8,128]{1,0:T(8,128)S(1)}, u32[]{:S(2)}, u32[]{:S(2)}) %collective-permute-start) | collective-permute-done | bytes 4128 | tf_op jit(solution)/shard_map/ppermute | solution.py:433
  19.4 1.8 %collective-permute-start.1 = (f32[8,128]{1,0:T(8,128)S(1)}, f32[8,128]{1,0:T(8,128)S(1)}, u32[]{:S(2)}, u32[]{:S(2)}) collective-permute-start(f32[8,128]{1,0:T(8,128)S(1)} %add.22), channel_id=1, source_target_pairs={{0,4},{2,6},{4,0},{6,2},{8,12},{10,14},{12,8},{14,10},{16,20},{18,... | collective-permute-start | bytes 12296 | tf_op jit(solution)/shard_map/ppermute | solution.py:433
  21.2 1.8 %collective-permute-done.1 = f32[8,128]{1,0:T(8,128)S(1)} collective-permute-done((f32[8,128]{1,0:T(8,128)S(1)}, f32[8,128]{1,0:T(8,128)S(1)}, u32[]{:S(2)}, u32[]{:S(2)}) %collective-permute-start.1) | collective-permute-done | bytes 4128 | tf_op jit(solution)/shard_map/ppermute | solution.py:433
  23.1 1.8 %collective-permute-start.2 = (f32[8,128]{1,0:T(8,128)S(1)}, f32[8,128]{1,0:T(8,128)S(1)}, u32[]{:S(2)}, u32[]{:S(2)}) collective-permute-start(f32[8,128]{1,0:T(8,128)S(1)} %add.23), channel_id=1, source_target_pairs={{0,8},{2,10},{4,12},{6,14},{8,0},{10,2},{12,4},{14,6},{16,24},{18,... | collective-permute-start | bytes 12296 | tf_op jit(solution)/shard_map/ppermute | solution.py:433
  24.9 1.8 %collective-permute-done.2 = f32[8,128]{1,0:T(8,128)S(1)} collective-permute-done((f32[8,128]{1,0:T(8,128)S(1)}, f32[8,128]{1,0:T(8,128)S(1)}, u32[]{:S(2)}, u32[]{:S(2)}) %collective-permute-start.2) | collective-permute-done | bytes 4128 | tf_op jit(solution)/shard_map/ppermute | solution.py:433
  26.7 2.8 %collective-permute-start.3 = (f32[8,128]{1,0:T(8,128)S(1)}, f32[8,128]{1,0:T(8,128)S(1)}, u32[]{:S(2)}, u32[]{:S(2)}) collective-permute-start(f32[8,128]{1,0:T(8,128)S(1)} %add.24), channel_id=1, source_target_pairs={{0,16},{2,18},{4,20},{6,22},{8,24},{10,26},{12,28},{14,30},{16,0},... | collective-permute-start | bytes 12296 | tf_op jit(solution)/shard_map/ppermute | solution.py:433
  29.5 1.7 %collective-permute-done.3 = f32[8,128]{1,0:T(8,128)S(1)} collective-permute-done((f32[8,128]{1,0:T(8,128)S(1)}, f32[8,128]{1,0:T(8,128)S(1)}, u32[]{:S(2)}, u32[]{:S(2)}) %collective-permute-start.3) | collective-permute-done | bytes 4128 | tf_op jit(solution)/shard_map/ppermute | solution.py:433
  31.2 0.0 collective-permute-done.5.refs_1_
  31.2 0.0 collective-permute-done.6.refs_2_
  31.2 0.0 collective-permute-done.7.refs_3_
  31.2 4.4 %shard_map.98 = (f32[3,2,128,256]{3,2,1,0:T(8,128)S(1)}, f32[2,128,256]{2,1,0:T(8,128)S(1)}) custom-call(s32[1]{0:T(128)} %bitcast.rank_ref, f32[8,128]{1,0:T(8,128)S(1)} %add.25.total_ref, f32[2,264,128]{2,1,0:T(8,128)S(1)} %get-tuple-element.32.refs_0_, f32[2,264,128]{2,1,0:T(8,128)S(1)} %collective-permute-done.5.refs_1_, ...), custom_call_target="tpu_custom_call" | custom-call | flops 1073741824 | bytes 1048576 | tf_op jit(solution)/shard_map/pallas_call | solution.py:448
  35.6 1.9 %collective-permute-start.8 = (f32[2,128,256]{2,1,0:T(8,128)S(1)}, f32[2,128,256]{2,1,0:T(8,128)S(1)}, u32[]{:S(2)}, u32[]{:S(2)}) collective-permute-start(f32[2,128,256]{2,1,0:T(8,128)S(1)} %get-tuple-element.36.mine_ref), channel_id=1, source_target_pairs={{0,8},{2,10},{4,12},{6,14},{8,0},{10,2},{12,4},{14,6},{16,24},{18,... | collective-permute-start | bytes 786440 | tf_op jit(solution)/shard_map/ppermute | solution.py:469
  37.5 0.0 copy-done
  37.5 3.6 %shard_map.99.wu_ref = f32[8,128,256]{2,1,0:T(8,128)S(1)} custom-call(bf16[1024,128]{1,0:T(8,128)(2,1)S(1)} %bitcast.14, bf16[1024,128]{1,0:T(8,128)(2,1)S(1)} %bitcast.11, f32[8,128]{1,0:T(8,128)S(1)} %get-tuple-element.37.beta_ref, f32[8,128]{1,0:T(8,128)S(1)} %add.25.total_ref, f32[8,128]{1,0:T(8,128)S(1)} %get-tuple-element.29.cum_ref), custom_call_target="tpu_custom_call" | custom-call | flops 2147483648 | bytes 1048576 | tf_op jit(solution)/shard_map/pallas_call | solution.py:457
  41.1 0.0 copy-start.8
  41.1 1.0 %copy-done.8 = f32[8,128,256]{2,1,0:T(8,128)} copy-done((f32[8,128,256]{2,1,0:T(8,128)}, f32[8,128,256]{2,1,0:T(8,128)S(1)}, u32[]{:S(2)}) %copy-start.8) | copy-done | bytes 1048600
  42.0 0.0 collective-permute-done.8.other_ref.before_ref
  42.0 0.0 copy-start.9
  42.0 0.4 shard_map.100
  42.5 5.3 %collective-permute-start.9 = (f32[2,128,128]{2,1,0:T(8,128)S(1)}, f32[2,128,128]{2,1,0:T(8,128)S(1)}, u32[]{:S(2)}, u32[]{:S(2)}) collective-permute-start(f32[2,128,128]{2,1,0:T(8,128)S(1)} %shard_map.100), channel_id=1, source_target_pairs={{0,24},{2,26},{4,28},{6,30},{8,16},{10,18},{12,20},{14,22},{16,8},... | collective-permute-start | bytes 393224 | tf_op jit(solution)/shard_map/ppermute | solution.py:487
  47.8 0.0 copy-start.5
  47.8 0.4 shard_map.102
  48.2 0.0 copy-done.9
  48.2 0.6 copy-done.5
  48.7 1.7 %shard_map.101 = (bf16[8,256,256]{2,1,0:T(8,128)(2,1)S(1)}, f32[8,256,128]{2,1,0:T(8,128)S(1)}) custom-call(bf16[1024,128]{1,0:T(8,128)(2,1)S(1)} %bitcast.16, bf16[1024,128]{1,0:T(8,128)(2,1)S(1)} %bitcast.15, f32[8,128]{1,0:T(8,128)S(1)} %get-tuple-element.29.cum_ref, f32[8,128,256]{2,1,0:T(8,128)S(1)} %copy-done.9), custom_call_target="tpu_custom_call" | custom-call | flops 1073741824 | bytes 1048576 | tf_op jit(solution)/shard_map/pallas_call | solution.py:490
  50.4 0.4 collective-permute-done.9.came_ref
  50.8 0.0 copy-start.1
  50.8 0.4 shard_map.103
  51.3 1.5 %collective-permute-start.10 = (f32[2,128,128]{2,1,0:T(8,128)S(1)}, f32[2,128,128]{2,1,0:T(8,128)S(1)}, u32[]{:S(2)}, u32[]{:S(2)}) collective-permute-start(f32[2,128,128]{2,1,0:T(8,128)S(1)} %get-tuple-element.47), channel_id=1, source_target_pairs={{0,2},{2,0},{4,6},{6,4},{8,10},{10,8},{12,14},{14,12},{16,18},{18,... | collective-permute-start | bytes 393224 | tf_op jit(solution)/shard_map/ppermute | solution.py:515
  52.8 1.5 %collective-permute-start.11 = (f32[2,128,128]{2,1,0:T(8,128)S(1)}, f32[2,128,128]{2,1,0:T(8,128)S(1)}, u32[]{:S(2)}, u32[]{:S(2)}) collective-permute-start(f32[2,128,128]{2,1,0:T(8,128)S(1)} %get-tuple-element.48), channel_id=1, source_target_pairs={{0,4},{2,6},{4,0},{6,2},{8,12},{10,14},{12,8},{14,10},{16,20},{18,... | collective-permute-start | bytes 393224 | tf_op jit(solution)/shard_map/ppermute | solution.py:515
  54.3 0.5 collective-permute-start.12
  54.8 1.5 %collective-permute-done.10.refs_1_ = f32[2,128,128]{2,1,0:T(8,128)S(1)} collective-permute-done((f32[2,128,128]{2,1,0:T(8,128)S(1)}, f32[2,128,128]{2,1,0:T(8,128)S(1)}, u32[]{:S(2)}, u32[]{:S(2)}) %collective-permute-start.10) | collective-permute-done | bytes 131104 | tf_op jit(solution)/shard_map/ppermute | solution.py:515
  56.3 1.5 %collective-permute-done.11.refs_2_ = f32[2,128,128]{2,1,0:T(8,128)S(1)} collective-permute-done((f32[2,128,128]{2,1,0:T(8,128)S(1)}, f32[2,128,128]{2,1,0:T(8,128)S(1)}, u32[]{:S(2)}, u32[]{:S(2)}) %collective-permute-start.11) | collective-permute-done | bytes 131104 | tf_op jit(solution)/shard_map/ppermute | solution.py:515
  57.8 2.4 %collective-permute-done.12.refs_3_ = f32[2,128,128]{2,1,0:T(8,128)S(1)} collective-permute-done((f32[2,128,128]{2,1,0:T(8,128)S(1)}, f32[2,128,128]{2,1,0:T(8,128)S(1)}, u32[]{:S(2)}, u32[]{:S(2)}) %collective-permute-start.12) | collective-permute-done | bytes 131104 | tf_op jit(solution)/shard_map/ppermute | solution.py:515
  60.1 0.0 copy-done.1
  60.1 1.9 %shard_map.104 = (bf16[1024,128]{1,0:T(8,128)(2,1)}, f32[2,8,128,128]{3,2,1,0:T(8,128)}) custom-call(s32[1]{0:T(128)} %bitcast.rank_ref, f32[2,128,128]{2,1,0:T(8,128)S(1)} %get-tuple-element.46.refs_0_, f32[2,128,128]{2,1,0:T(8,128)S(1)} %collective-permute-done.10.refs_1_, f32[2,128,128]{2,1,0:T(8,128)S(1)} %collective-permute-done.11.refs_2_, ...), custom_call_target="tpu_custom_call" | custom-call | flops 268435456 | bytes 1048576 | tf_op jit(solution)/shard_map/pallas_call | solution.py:517
  (6 shorter events, 0.0 us)
Async XLA Ops:
  0.6 36.9 %copy-start = (f32[8,128,128]{2,1,0:T(8,128)S(1)}, f32[8,128,128]{2,1,0:T(8,128)}, u32[]{:S(2)}) copy-start(f32[8,128,128]{2,1,0:T(8,128)} %param.15) | copy-start | bytes 1572868
  0.6 1.0 %copy-start.3 = (bf16[128,8,128]{2,1,0:T(8,128)(2,1)S(1)}, bf16[128,8,128]{2,1,0:T(8,128)(2,1)}, u32[]{:S(2)}) copy-start(bf16[128,8,128]{2,1,0:T(8,128)(2,1)} %param.9) | copy-start | bytes 786436
  0.7 1.1 %copy-start.4 = (bf16[128,1024]{1,0:T(8,128)(2,1)S(1)}, bf16[128,1024]{1,0:T(8,128)(2,1)}, u32[]{:S(2)}) copy-start(bf16[128,1024]{1,0:T(8,128)(2,1)} %inputs_ref.1) | copy-start | bytes 786436
  0.7 1.1 %copy-start.6 = (bf16[16,1024]{1,0:T(8,128)(2,1)S(1)}, bf16[16,1024]{1,0:T(8,128)(2,1)}, u32[]{:S(2)}) copy-start(bf16[16,1024]{1,0:T(8,128)(2,1)} %weight_ref.1) | copy-start | bytes 98308
  0.7 1.1 %copy-start.7 = (f32[8,128]{1,0:T(8,128)S(1)}, f32[8,128]{1,0:T(8,128)}, u32[]{:S(2)}) copy-start(f32[8,128]{1,0:T(8,128)} %decay_ref.1) | copy-start | bytes 12292
  1.7 1.8 %copy-start.2 = (bf16[128,8,128]{2,1,0:T(8,128)(2,1)S(1)}, bf16[128,8,128]{2,1,0:T(8,128)(2,1)}, u32[]{:S(2)}) copy-start(bf16[128,8,128]{2,1,0:T(8,128)(2,1)} %param.10) | copy-start | bytes 786436
  2.2 1.3 %collective-permute-start.4 = (f32[8,128]{1,0:T(8,128)S(1)}, f32[8,128]{1,0:T(8,128)S(1)}, u32[]{:S(2)}, u32[]{:S(2)}) collective-permute-start(f32[8,128]{1,0:T(8,128)S(1)} %get-tuple-element.31), channel_id=1, source_target_pairs={{0,1},{1,0},{2,3},{3,2},{4,5},{5,4},{6,7},{7,6},{8,9},{9,8},{10,11... | collective-permute-start | bytes 12296 | tf_op jit(solution)/shard_map/ppermute | solution.py:418
  3.8 27.4 %collective-permute-start.5 = (f32[2,264,128]{2,1,0:T(8,128)S(1)}, f32[2,264,128]{2,1,0:T(8,128)S(1)}, u32[]{:S(2)}, u32[]{:S(2)}) collective-permute-start(f32[2,264,128]{2,1,0:T(8,128)S(1)} %get-tuple-element.33), channel_id=1, source_target_pairs={{0,2},{2,0},{4,6},{6,4},{8,10},{10,8},{12,14},{14,12},{16,18},{18,... | collective-permute-start | bytes 811016 | tf_op jit(solution)/shard_map/ppermute | solution.py:440
  6.7 24.5 %collective-permute-start.6 = (f32[2,264,128]{2,1,0:T(8,128)S(1)}, f32[2,264,128]{2,1,0:T(8,128)S(1)}, u32[]{:S(2)}, u32[]{:S(2)}) collective-permute-start(f32[2,264,128]{2,1,0:T(8,128)S(1)} %get-tuple-element.34), channel_id=1, source_target_pairs={{0,4},{2,6},{4,0},{6,2},{8,12},{10,14},{12,8},{14,10},{16,20},{18,... | collective-permute-start | bytes 811016 | tf_op jit(solution)/shard_map/ppermute | solution.py:440
  8.2 23.0 %collective-permute-start.7 = (f32[2,264,128]{2,1,0:T(8,128)S(1)}, f32[2,264,128]{2,1,0:T(8,128)S(1)}, u32[]{:S(2)}, u32[]{:S(2)}) collective-permute-start(f32[2,264,128]{2,1,0:T(8,128)S(1)} %get-tuple-element.35), channel_id=1, source_target_pairs={{0,6},{2,4},{4,2},{6,0},{8,14},{10,12},{12,10},{14,8},{16,22},{18,... | collective-permute-start | bytes 811016 | tf_op jit(solution)/shard_map/ppermute | solution.py:440
  8.2 11.2 %collective-permute-start = (f32[8,128]{1,0:T(8,128)S(1)}, f32[8,128]{1,0:T(8,128)S(1)}, u32[]{:S(2)}, u32[]{:S(2)}) collective-permute-start(f32[8,128]{1,0:T(8,128)S(1)} %get-tuple-element.28), channel_id=1, source_target_pairs={{0,2},{2,0},{4,6},{6,4},{8,10},{10,8},{12,14},{14,12},{16,18},{18,... | collective-permute-start | bytes 12296 | tf_op jit(solution)/shard_map/ppermute | solution.py:433
  19.4 3.6 %collective-permute-start.1 = (f32[8,128]{1,0:T(8,128)S(1)}, f32[8,128]{1,0:T(8,128)S(1)}, u32[]{:S(2)}, u32[]{:S(2)}) collective-permute-start(f32[8,128]{1,0:T(8,128)S(1)} %add.22), channel_id=1, source_target_pairs={{0,4},{2,6},{4,0},{6,2},{8,12},{10,14},{12,8},{14,10},{16,20},{18,... | collective-permute-start | bytes 12296 | tf_op jit(solution)/shard_map/ppermute | solution.py:433
  23.1 3.6 %collective-permute-start.2 = (f32[8,128]{1,0:T(8,128)S(1)}, f32[8,128]{1,0:T(8,128)S(1)}, u32[]{:S(2)}, u32[]{:S(2)}) collective-permute-start(f32[8,128]{1,0:T(8,128)S(1)} %add.23), channel_id=1, source_target_pairs={{0,8},{2,10},{4,12},{6,14},{8,0},{10,2},{12,4},{14,6},{16,24},{18,... | collective-permute-start | bytes 12296 | tf_op jit(solution)/shard_map/ppermute | solution.py:433
  26.7 4.5 %collective-permute-start.3 = (f32[8,128]{1,0:T(8,128)S(1)}, f32[8,128]{1,0:T(8,128)S(1)}, u32[]{:S(2)}, u32[]{:S(2)}) collective-permute-start(f32[8,128]{1,0:T(8,128)S(1)} %add.24), channel_id=1, source_target_pairs={{0,16},{2,18},{4,20},{6,22},{8,24},{10,26},{12,28},{14,30},{16,0},... | collective-permute-start | bytes 12296 | tf_op jit(solution)/shard_map/ppermute | solution.py:433
  35.6 6.5 %collective-permute-start.8 = (f32[2,128,256]{2,1,0:T(8,128)S(1)}, f32[2,128,256]{2,1,0:T(8,128)S(1)}, u32[]{:S(2)}, u32[]{:S(2)}) collective-permute-start(f32[2,128,256]{2,1,0:T(8,128)S(1)} %get-tuple-element.36.mine_ref), channel_id=1, source_target_pairs={{0,8},{2,10},{4,12},{6,14},{8,0},{10,2},{12,4},{14,6},{16,24},{18,... | collective-permute-start | bytes 786440 | tf_op jit(solution)/shard_map/ppermute | solution.py:469
  41.1 1.0 %copy-start.8 = (f32[8,128,256]{2,1,0:T(8,128)}, f32[8,128,256]{2,1,0:T(8,128)S(1)}, u32[]{:S(2)}) copy-start(f32[8,128,256]{2,1,0:T(8,128)S(1)} %shard_map.99.wu_ref) | copy-start | bytes 3145732
  42.0 6.1 %copy-start.9 = (f32[8,128,256]{2,1,0:T(8,128)S(1)}, f32[8,128,256]{2,1,0:T(8,128)}, u32[]{:S(2)}) copy-start(f32[8,128,256]{2,1,0:T(8,128)} %copy-done.8) | copy-start | bytes 3145732
  42.5 8.4 %collective-permute-start.9 = (f32[2,128,128]{2,1,0:T(8,128)S(1)}, f32[2,128,128]{2,1,0:T(8,128)S(1)}, u32[]{:S(2)}, u32[]{:S(2)}) collective-permute-start(f32[2,128,128]{2,1,0:T(8,128)S(1)} %shard_map.100), channel_id=1, source_target_pairs={{0,24},{2,26},{4,28},{6,30},{8,16},{10,18},{12,20},{14,22},{16,8},... | collective-permute-start | bytes 393224 | tf_op jit(solution)/shard_map/ppermute | solution.py:487
  47.8 0.9 %copy-start.5 = (bf16[128,8,128]{2,1,0:T(8,128)(2,1)S(1)}, bf16[128,8,128]{2,1,0:T(8,128)(2,1)}, u32[]{:S(2)}) copy-start(bf16[128,8,128]{2,1,0:T(8,128)(2,1)} %param.8) | copy-start | bytes 786436
  50.8 9.3 %copy-start.1 = (bf16[128,8,128]{2,1,0:T(8,128)(2,1)S(1)}, bf16[128,8,128]{2,1,0:T(8,128)(2,1)}, u32[]{:S(2)}) copy-start(bf16[128,8,128]{2,1,0:T(8,128)(2,1)} %param.11) | copy-start | bytes 786436
  51.3 5.0 %collective-permute-start.10 = (f32[2,128,128]{2,1,0:T(8,128)S(1)}, f32[2,128,128]{2,1,0:T(8,128)S(1)}, u32[]{:S(2)}, u32[]{:S(2)}) collective-permute-start(f32[2,128,128]{2,1,0:T(8,128)S(1)} %get-tuple-element.47), channel_id=1, source_target_pairs={{0,2},{2,0},{4,6},{6,4},{8,10},{10,8},{12,14},{14,12},{16,18},{18,... | collective-permute-start | bytes 393224 | tf_op jit(solution)/shard_map/ppermute | solution.py:515
  52.8 5.0 %collective-permute-start.11 = (f32[2,128,128]{2,1,0:T(8,128)S(1)}, f32[2,128,128]{2,1,0:T(8,128)S(1)}, u32[]{:S(2)}, u32[]{:S(2)}) collective-permute-start(f32[2,128,128]{2,1,0:T(8,128)S(1)} %get-tuple-element.48), channel_id=1, source_target_pairs={{0,4},{2,6},{4,0},{6,2},{8,12},{10,14},{12,8},{14,10},{16,20},{18,... | collective-permute-start | bytes 393224 | tf_op jit(solution)/shard_map/ppermute | solution.py:515
  54.3 5.9 %collective-permute-start.12 = (f32[2,128,128]{2,1,0:T(8,128)S(1)}, f32[2,128,128]{2,1,0:T(8,128)S(1)}, u32[]{:S(2)}, u32[]{:S(2)}) collective-permute-start(f32[2,128,128]{2,1,0:T(8,128)S(1)} %get-tuple-element.49), channel_id=1, source_target_pairs={{0,6},{2,4},{4,2},{6,0},{8,14},{10,12},{12,10},{14,8},{16,22},{18,... | collective-permute-start | bytes 393224 | tf_op jit(solution)/shard_map/ppermute | solution.py:515

commit v5 on v4

--- a/solution.py
+++ b/solution.py
@@ -165,13 +165,16 @@
         )
     size = 2
     while size < n:
-        joins = ((row ^ col) & ~(2 * size - 1)) == 0
-        joins = joins & ((row & size) != 0) & ((col & size) == 0)
+        grown = 4 * size if 4 * size <= n else 2 * size
+        joins = (((row ^ col) & ~(grown - 1)) == 0) & (((row ^ col) & ~(size - 1)) != 0)
         parts = [split(x) for x in inverses]
-        mids = [split(dot_square(a, x)) for a, x in zip(systems, parts)]
-        ends = [dot_square(x, t) for x, t in zip(parts, mids)]
-        inverses = [x - jnp.where(joins, e, 0.0) for x, e in zip(inverses, ends)]
-        size *= 2
+        mixes = [jnp.where(joins, dot_square(x, a), 0.0) for x, a in zip(parts, systems)]
+        mixes = [split(mix) for mix in mixes]
+        inverses = [x - dot_square(mix, part) for x, mix, part in zip(inverses, mixes, parts)]
+        if grown == 4 * size:
+            squares = [split(dot_square(mix, mix)) for mix in mixes]
+            inverses = [x + dot_square(sq, split(x)) for x, sq in zip(inverses, squares)]
+        size = grown
     write_scale = beta * jnp.exp(cum) * inverse
     writes = []
     for item in range(items):

time: 62.2 us -> 61.7 us (level)
  Pallas kernels: 13.5 us -> 12.5 us
  transfers between devices with their start and end apart: 13 -> 13, of which waited for: 9 -> 10; matrix products, arithmetic and copies ran while one was open for 0% -> 0% of each run, Pallas kernels for 9% -> 8%
where the time goes in v5:
time: 61.7 us; the launch traced here: 61.5 us
  starting transfers between devices  24 us (39%)
  waiting for transfers between devices  21.6 us (35%)
  Pallas kernels  12.5 us (20%)
  local copies, waits for them, and re-layouts  2.59 us (4%)
  between operations  0.78 us (1%)
    ppermute x4, waiting for transfers between devices, shared(): return lax.ppermute(total, 'seq', flipped(mask))  14.5 us
    ppermute x4, starting transfers between devices, shared(): return lax.ppermute(total, 'seq', flipped(mask))  8.37 us
    ppermute x3, waiting for transfers between devices, on_device(): lax.ppermute(entries[slot], 'seq', flipped(slot))  5.35 us
    ppermute x1, starting transfers between devices, on_device(): came = lax.ppermute(middle, 'seq', mirror)  5.31 us
    ppermute x3, starting transfers between devices, on_device(): exchanged.append(lax.ppermute(packs[slot], 'seq', flipped(slot)))  4.42 us
    pallas_call x1, Pallas kernels, on_device(): call(functools.partial(run_kernel, groups, per, tokens_all), (shape(max(g...  3.89 us
    ppermute x3, starting transfers between devices, on_device(): lax.ppermute(entries[slot], 'seq', flipped(slot))  3.55 us
    pallas_call x1, Pallas kernels, on_device(): call(functools.partial(own_kernel, tokens_all), shape(heads, n, 2 * d), s...  3.09 us
  transfers between devices with their start and end apart: 13, of which 10 were waited for; matrix products, arithmetic and copies ran while one was open for 0% of the time, Pallas kernels for 8%

profile of v5, /device:TPU:0, one launch (start us, length us, event | category | flops | bytes accessed | tf_op | source)
XLA Modules:
  0.0 61.5 jit_solution(16073554423715029589)
XLA Ops:
  0.6 0.0 copy-start
  0.6 0.0 copy-start.3
  0.7 0.0 copy-start.4
  0.7 0.0 copy-start.6
  0.7 0.0 copy-start.7
  0.7 1.0 %copy-done.3 = bf16[128,8,128]{2,1,0:T(8,128)(2,1)S(1)} copy-done((bf16[128,8,128]{2,1,0:T(8,128)(2,1)S(1)}, bf16[128,8,128]{2,1,0:T(8,128)(2,1)}, u32[]{:S(2)}) %copy-start.3) | copy-done | bytes 262168
  1.7 0.1 copy-done.4
  1.7 0.0 copy-done.6
  1.7 0.0 copy-done.7
  1.7 0.0 copy-start.2
  1.7 0.5 shard_map.96
  2.2 0.5 collective-permute-start.4
  2.7 0.8 %collective-permute-done.4.came_ref = f32[8,128]{1,0:T(8,128)S(1)} collective-permute-done((f32[8,128]{1,0:T(8,128)S(1)}, f32[8,128]{1,0:T(8,128)S(1)}, u32[]{:S(2)}, u32[]{:S(2)}) %collective-permute-start.4) | collective-permute-done | bytes 4128 | tf_op jit(solution)/shard_map/ppermute | solution.py:421
  3.5 0.0 copy-done.2
  3.6 0.3 shard_map.97
  3.8 2.9 %collective-permute-start.5 = (f32[2,264,128]{2,1,0:T(8,128)S(1)}, f32[2,264,128]{2,1,0:T(8,128)S(1)}, u32[]{:S(2)}, u32[]{:S(2)}) collective-permute-start(f32[2,264,128]{2,1,0:T(8,128)S(1)} %get-tuple-element.33), channel_id=1, source_target_pairs={{0,2},{2,0},{4,6},{6,4},{8,10},{10,8},{12,14},{14,12},{16,18},{18,... | collective-permute-start | bytes 811016 | tf_op jit(solution)/shard_map/ppermute | solution.py:443
  6.7 1.5 %collective-permute-start.6 = (f32[2,264,128]{2,1,0:T(8,128)S(1)}, f32[2,264,128]{2,1,0:T(8,128)S(1)}, u32[]{:S(2)}, u32[]{:S(2)}) collective-permute-start(f32[2,264,128]{2,1,0:T(8,128)S(1)} %get-tuple-element.34), channel_id=1, source_target_pairs={{0,4},{2,6},{4,0},{6,2},{8,12},{10,14},{12,8},{14,10},{16,20},{18,... | collective-permute-start | bytes 811016 | tf_op jit(solution)/shard_map/ppermute | solution.py:443
  8.2 0.0 collective-permute-start.7
  8.2 1.9 %collective-permute-start = (f32[8,128]{1,0:T(8,128)S(1)}, f32[8,128]{1,0:T(8,128)S(1)}, u32[]{:S(2)}, u32[]{:S(2)}) collective-permute-start(f32[8,128]{1,0:T(8,128)S(1)} %get-tuple-element.28), channel_id=1, source_target_pairs={{0,2},{2,0},{4,6},{6,4},{8,10},{10,8},{12,14},{14,12},{16,18},{18,... | collective-permute-start | bytes 12296 | tf_op jit(solution)/shard_map/ppermute | solution.py:436
  10.2 9.3 %collective-permute-done = f32[8,128]{1,0:T(8,128)S(1)} collective-permute-done((f32[8,128]{1,0:T(8,128)S(1)}, f32[8,128]{1,0:T(8,128)S(1)}, u32[]{:S(2)}, u32[]{:S(2)}) %collective-permute-start) | collective-permute-done | bytes 4128 | tf_op jit(solution)/shard_map/ppermute | solution.py:436
  19.4 1.8 %collective-permute-start.1 = (f32[8,128]{1,0:T(8,128)S(1)}, f32[8,128]{1,0:T(8,128)S(1)}, u32[]{:S(2)}, u32[]{:S(2)}) collective-permute-start(f32[8,128]{1,0:T(8,128)S(1)} %add.22), channel_id=1, source_target_pairs={{0,4},{2,6},{4,0},{6,2},{8,12},{10,14},{12,8},{14,10},{16,20},{18,... | collective-permute-start | bytes 12296 | tf_op jit(solution)/shard_map/ppermute | solution.py:436
  21.2 1.8 %collective-permute-done.1 = f32[8,128]{1,0:T(8,128)S(1)} collective-permute-done((f32[8,128]{1,0:T(8,128)S(1)}, f32[8,128]{1,0:T(8,128)S(1)}, u32[]{:S(2)}, u32[]{:S(2)}) %collective-permute-start.1) | collective-permute-done | bytes 4128 | tf_op jit(solution)/shard_map/ppermute | solution.py:436
  23.1 1.8 %collective-permute-start.2 = (f32[8,128]{1,0:T(8,128)S(1)}, f32[8,128]{1,0:T(8,128)S(1)}, u32[]{:S(2)}, u32[]{:S(2)}) collective-permute-start(f32[8,128]{1,0:T(8,128)S(1)} %add.23), channel_id=1, source_target_pairs={{0,8},{2,10},{4,12},{6,14},{8,0},{10,2},{12,4},{14,6},{16,24},{18,... | collective-permute-start | bytes 12296 | tf_op jit(solution)/shard_map/ppermute | solution.py:436
  24.9 1.8 %collective-permute-done.2 = f32[8,128]{1,0:T(8,128)S(1)} collective-permute-done((f32[8,128]{1,0:T(8,128)S(1)}, f32[8,128]{1,0:T(8,128)S(1)}, u32[]{:S(2)}, u32[]{:S(2)}) %collective-permute-start.2) | collective-permute-done | bytes 4128 | tf_op jit(solution)/shard_map/ppermute | solution.py:436
  26.7 2.8 %collective-permute-start.3 = (f32[8,128]{1,0:T(8,128)S(1)}, f32[8,128]{1,0:T(8,128)S(1)}, u32[]{:S(2)}, u32[]{:S(2)}) collective-permute-start(f32[8,128]{1,0:T(8,128)S(1)} %add.24), channel_id=1, source_target_pairs={{0,16},{2,18},{4,20},{6,22},{8,24},{10,26},{12,28},{14,30},{16,0},... | collective-permute-start | bytes 12296 | tf_op jit(solution)/shard_map/ppermute | solution.py:436
  29.5 1.7 %collective-permute-done.3 = f32[8,128]{1,0:T(8,128)S(1)} collective-permute-done((f32[8,128]{1,0:T(8,128)S(1)}, f32[8,128]{1,0:T(8,128)S(1)}, u32[]{:S(2)}, u32[]{:S(2)}) %collective-permute-start.3) | collective-permute-done | bytes 4128 | tf_op jit(solution)/shard_map/ppermute | solution.py:436
  31.2 0.0 collective-permute-done.5.refs_1_
  31.2 0.0 collective-permute-done.6.refs_2_
  31.2 0.0 collective-permute-done.7.refs_3_
  31.2 3.9 %shard_map.98 = (f32[3,2,128,256]{3,2,1,0:T(8,128)S(1)}, f32[2,128,256]{2,1,0:T(8,128)S(1)}) custom-call(s32[1]{0:T(128)} %bitcast.rank_ref, f32[8,128]{1,0:T(8,128)S(1)} %add.25.total_ref, f32[2,264,128]{2,1,0:T(8,128)S(1)} %get-tuple-element.32.refs_0_, f32[2,264,128]{2,1,0:T(8,128)S(1)} %collective-permute-done.5.refs_1_, ...), custom_call_target="tpu_custom_call" | custom-call | flops 1073741824 | bytes 1048576 | tf_op jit(solution)/shard_map/pallas_call | solution.py:451
  35.1 1.9 %collective-permute-start.8 = (f32[2,128,256]{2,1,0:T(8,128)S(1)}, f32[2,128,256]{2,1,0:T(8,128)S(1)}, u32[]{:S(2)}, u32[]{:S(2)}) collective-permute-start(f32[2,128,256]{2,1,0:T(8,128)S(1)} %get-tuple-element.36.mine_ref), channel_id=1, source_target_pairs={{0,8},{2,10},{4,12},{6,14},{8,0},{10,2},{12,4},{14,6},{16,24},{18,... | collective-permute-start | bytes 786440 | tf_op jit(solution)/shard_map/ppermute | solution.py:472
  37.0 0.0 copy-done
  37.0 3.1 %shard_map.99.wu_ref = f32[8,128,256]{2,1,0:T(8,128)S(1)} custom-call(bf16[1024,128]{1,0:T(8,128)(2,1)S(1)} %bitcast.14, bf16[1024,128]{1,0:T(8,128)(2,1)S(1)} %bitcast.11, f32[8,128]{1,0:T(8,128)S(1)} %get-tuple-element.37.beta_ref, f32[8,128]{1,0:T(8,128)S(1)} %add.25.total_ref, f32[8,128]{1,0:T(8,128)S(1)} %get-tuple-element.29.cum_ref), custom_call_target="tpu_custom_call" | custom-call | flops 2147483648 | bytes 1048576 | tf_op jit(solution)/shard_map/pallas_call | solution.py:460
  40.1 0.0 copy-start.8
  40.1 1.0 %copy-done.8 = f32[8,128,256]{2,1,0:T(8,128)} copy-done((f32[8,128,256]{2,1,0:T(8,128)}, f32[8,128,256]{2,1,0:T(8,128)S(1)}, u32[]{:S(2)}) %copy-start.8) | copy-done | bytes 1048600
  41.1 0.5 collective-permute-done.8.other_ref.before_ref
  41.5 0.0 copy-start.9
  41.5 0.4 shard_map.100
  42.0 5.3 %collective-permute-start.9 = (f32[2,128,128]{2,1,0:T(8,128)S(1)}, f32[2,128,128]{2,1,0:T(8,128)S(1)}, u32[]{:S(2)}, u32[]{:S(2)}) collective-permute-start(f32[2,128,128]{2,1,0:T(8,128)S(1)} %shard_map.100), channel_id=1, source_target_pairs={{0,24},{2,26},{4,28},{6,30},{8,16},{10,18},{12,20},{14,22},{16,8},... | collective-permute-start | bytes 393224 | tf_op jit(solution)/shard_map/ppermute | solution.py:490
  47.3 0.0 copy-start.5
  47.3 0.4 shard_map.102
  47.7 0.0 copy-done.9
  47.7 0.6 copy-done.5
  48.2 1.7 %shard_map.101 = (bf16[8,256,256]{2,1,0:T(8,128)(2,1)S(1)}, f32[8,256,128]{2,1,0:T(8,128)S(1)}) custom-call(bf16[1024,128]{1,0:T(8,128)(2,1)S(1)} %bitcast.16, bf16[1024,128]{1,0:T(8,128)(2,1)S(1)} %bitcast.15, f32[8,128]{1,0:T(8,128)S(1)} %get-tuple-element.29.cum_ref, f32[8,128,256]{2,1,0:T(8,128)S(1)} %copy-done.9), custom_call_target="tpu_custom_call" | custom-call | flops 1073741824 | bytes 1048576 | tf_op jit(solution)/shard_map/pallas_call | solution.py:493
  49.9 0.4 collective-permute-done.9.came_ref
  50.3 0.0 copy-start.1
  50.3 0.4 shard_map.103
  50.7 1.6 %collective-permute-start.10 = (f32[2,128,128]{2,1,0:T(8,128)S(1)}, f32[2,128,128]{2,1,0:T(8,128)S(1)}, u32[]{:S(2)}, u32[]{:S(2)}) collective-permute-start(f32[2,128,128]{2,1,0:T(8,128)S(1)} %get-tuple-element.47), channel_id=1, source_target_pairs={{0,2},{2,0},{4,6},{6,4},{8,10},{10,8},{12,14},{14,12},{16,18},{18,... | collective-permute-start | bytes 393224 | tf_op jit(solution)/shard_map/ppermute | solution.py:518
  52.3 1.5 %collective-permute-start.11 = (f32[2,128,128]{2,1,0:T(8,128)S(1)}, f32[2,128,128]{2,1,0:T(8,128)S(1)}, u32[]{:S(2)}, u32[]{:S(2)}) collective-permute-start(f32[2,128,128]{2,1,0:T(8,128)S(1)} %get-tuple-element.48), channel_id=1, source_target_pairs={{0,4},{2,6},{4,0},{6,2},{8,12},{10,14},{12,8},{14,10},{16,20},{18,... | collective-permute-start | bytes 393224 | tf_op jit(solution)/shard_map/ppermute | solution.py:518
  53.8 0.5 collective-permute-start.12
  54.3 1.5 %collective-permute-done.10.refs_1_ = f32[2,128,128]{2,1,0:T(8,128)S(1)} collective-permute-done((f32[2,128,128]{2,1,0:T(8,128)S(1)}, f32[2,128,128]{2,1,0:T(8,128)S(1)}, u32[]{:S(2)}, u32[]{:S(2)}) %collective-permute-start.10) | collective-permute-done | bytes 131104 | tf_op jit(solution)/shard_map/ppermute | solution.py:518
  55.8 1.5 %collective-permute-done.11.refs_2_ = f32[2,128,128]{2,1,0:T(8,128)S(1)} collective-permute-done((f32[2,128,128]{2,1,0:T(8,128)S(1)}, f32[2,128,128]{2,1,0:T(8,128)S(1)}, u32[]{:S(2)}, u32[]{:S(2)}) %collective-permute-start.11) | collective-permute-done | bytes 131104 | tf_op jit(solution)/shard_map/ppermute | solution.py:518
  57.3 2.4 %collective-permute-done.12.refs_3_ = f32[2,128,128]{2,1,0:T(8,128)S(1)} collective-permute-done((f32[2,128,128]{2,1,0:T(8,128)S(1)}, f32[2,128,128]{2,1,0:T(8,128)S(1)}, u32[]{:S(2)}, u32[]{:S(2)}) %collective-permute-start.12) | collective-permute-done | bytes 131104 | tf_op jit(solution)/shard_map/ppermute | solution.py:518
  59.6 0.0 copy-done.1
  59.6 1.9 %shard_map.104 = (bf16[1024,128]{1,0:T(8,128)(2,1)}, f32[2,8,128,128]{3,2,1,0:T(8,128)}) custom-call(s32[1]{0:T(128)} %bitcast.rank_ref, f32[2,128,128]{2,1,0:T(8,128)S(1)} %get-tuple-element.46.refs_0_, f32[2,128,128]{2,1,0:T(8,128)S(1)} %collective-permute-done.10.refs_1_, f32[2,128,128]{2,1,0:T(8,128)S(1)} %collective-permute-done.11.refs_2_, ...), custom_call_target="tpu_custom_call" | custom-call | flops 268435456 | bytes 1048576 | tf_op jit(solution)/shard_map/pallas_call | solution.py:520
  (6 shorter events, 0.0 us)
Async XLA Ops:
  0.6 36.4 %copy-start = (f32[8,128,128]{2,1,0:T(8,128)S(1)}, f32[8,128,128]{2,1,0:T(8,128)}, u32[]{:S(2)}) copy-start(f32[8,128,128]{2,1,0:T(8,128)} %param.15) | copy-start | bytes 1572868
  0.6 1.0 %copy-start.3 = (bf16[128,8,128]{2,1,0:T(8,128)(2,1)S(1)}, bf16[128,8,128]{2,1,0:T(8,128)(2,1)}, u32[]{:S(2)}) copy-start(bf16[128,8,128]{2,1,0:T(8,128)(2,1)} %param.9) | copy-start | bytes 786436
  0.7 1.1 %copy-start.4 = (bf16[128,1024]{1,0:T(8,128)(2,1)S(1)}, bf16[128,1024]{1,0:T(8,128)(2,1)}, u32[]{:S(2)}) copy-start(bf16[128,1024]{1,0:T(8,128)(2,1)} %inputs_ref.1) | copy-start | bytes 786436
  0.7 1.1 %copy-start.6 = (bf16[16,1024]{1,0:T(8,128)(2,1)S(1)}, bf16[16,1024]{1,0:T(8,128)(2,1)}, u32[]{:S(2)}) copy-start(bf16[16,1024]{1,0:T(8,128)(2,1)} %weight_ref.1) | copy-start | bytes 98308
  0.7 1.1 %copy-start.7 = (f32[8,128]{1,0:T(8,128)S(1)}, f32[8,128]{1,0:T(8,128)}, u32[]{:S(2)}) copy-start(f32[8,128]{1,0:T(8,128)} %decay_ref.1) | copy-start | bytes 12292
  1.7 1.8 %copy-start.2 = (bf16[128,8,128]{2,1,0:T(8,128)(2,1)S(1)}, bf16[128,8,128]{2,1,0:T(8,128)(2,1)}, u32[]{:S(2)}) copy-start(bf16[128,8,128]{2,1,0:T(8,128)(2,1)} %param.10) | copy-start | bytes 786436
  2.2 1.3 %collective-permute-start.4 = (f32[8,128]{1,0:T(8,128)S(1)}, f32[8,128]{1,0:T(8,128)S(1)}, u32[]{:S(2)}, u32[]{:S(2)}) collective-permute-start(f32[8,128]{1,0:T(8,128)S(1)} %get-tuple-element.31), channel_id=1, source_target_pairs={{0,1},{1,0},{2,3},{3,2},{4,5},{5,4},{6,7},{7,6},{8,9},{9,8},{10,11... | collective-permute-start | bytes 12296 | tf_op jit(solution)/shard_map/ppermute | solution.py:421
  3.8 27.4 %collective-permute-start.5 = (f32[2,264,128]{2,1,0:T(8,128)S(1)}, f32[2,264,128]{2,1,0:T(8,128)S(1)}, u32[]{:S(2)}, u32[]{:S(2)}) collective-permute-start(f32[2,264,128]{2,1,0:T(8,128)S(1)} %get-tuple-element.33), channel_id=1, source_target_pairs={{0,2},{2,0},{4,6},{6,4},{8,10},{10,8},{12,14},{14,12},{16,18},{18,... | collective-permute-start | bytes 811016 | tf_op jit(solution)/shard_map/ppermute | solution.py:443
  6.7 24.5 %collective-permute-start.6 = (f32[2,264,128]{2,1,0:T(8,128)S(1)}, f32[2,264,128]{2,1,0:T(8,128)S(1)}, u32[]{:S(2)}, u32[]{:S(2)}) collective-permute-start(f32[2,264,128]{2,1,0:T(8,128)S(1)} %get-tuple-element.34), channel_id=1, source_target_pairs={{0,4},{2,6},{4,0},{6,2},{8,12},{10,14},{12,8},{14,10},{16,20},{18,... | collective-permute-start | bytes 811016 | tf_op jit(solution)/shard_map/ppermute | solution.py:443
  8.2 23.0 %collective-permute-start.7 = (f32[2,264,128]{2,1,0:T(8,128)S(1)}, f32[2,264,128]{2,1,0:T(8,128)S(1)}, u32[]{:S(2)}, u32[]{:S(2)}) collective-permute-start(f32[2,264,128]{2,1,0:T(8,128)S(1)} %get-tuple-element.35), channel_id=1, source_target_pairs={{0,6},{2,4},{4,2},{6,0},{8,14},{10,12},{12,10},{14,8},{16,22},{18,... | collective-permute-start | bytes 811016 | tf_op jit(solution)/shard_map/ppermute | solution.py:443
  8.2 11.2 %collective-permute-start = (f32[8,128]{1,0:T(8,128)S(1)}, f32[8,128]{1,0:T(8,128)S(1)}, u32[]{:S(2)}, u32[]{:S(2)}) collective-permute-start(f32[8,128]{1,0:T(8,128)S(1)} %get-tuple-element.28), channel_id=1, source_target_pairs={{0,2},{2,0},{4,6},{6,4},{8,10},{10,8},{12,14},{14,12},{16,18},{18,... | collective-permute-start | bytes 12296 | tf_op jit(solution)/shard_map/ppermute | solution.py:436
  19.4 3.6 %collective-permute-start.1 = (f32[8,128]{1,0:T(8,128)S(1)}, f32[8,128]{1,0:T(8,128)S(1)}, u32[]{:S(2)}, u32[]{:S(2)}) collective-permute-start(f32[8,128]{1,0:T(8,128)S(1)} %add.22), channel_id=1, source_target_pairs={{0,4},{2,6},{4,0},{6,2},{8,12},{10,14},{12,8},{14,10},{16,20},{18,... | collective-permute-start | bytes 12296 | tf_op jit(solution)/shard_map/ppermute | solution.py:436
  23.1 3.6 %collective-permute-start.2 = (f32[8,128]{1,0:T(8,128)S(1)}, f32[8,128]{1,0:T(8,128)S(1)}, u32[]{:S(2)}, u32[]{:S(2)}) collective-permute-start(f32[8,128]{1,0:T(8,128)S(1)} %add.23), channel_id=1, source_target_pairs={{0,8},{2,10},{4,12},{6,14},{8,0},{10,2},{12,4},{14,6},{16,24},{18,... | collective-permute-start | bytes 12296 | tf_op jit(solution)/shard_map/ppermute | solution.py:436
  26.7 4.5 %collective-permute-start.3 = (f32[8,128]{1,0:T(8,128)S(1)}, f32[8,128]{1,0:T(8,128)S(1)}, u32[]{:S(2)}, u32[]{:S(2)}) collective-permute-start(f32[8,128]{1,0:T(8,128)S(1)} %add.24), channel_id=1, source_target_pairs={{0,16},{2,18},{4,20},{6,22},{8,24},{10,26},{12,28},{14,30},{16,0},... | collective-permute-start | bytes 12296 | tf_op jit(solution)/shard_map/ppermute | solution.py:436
  35.1 6.4 %collective-permute-start.8 = (f32[2,128,256]{2,1,0:T(8,128)S(1)}, f32[2,128,256]{2,1,0:T(8,128)S(1)}, u32[]{:S(2)}, u32[]{:S(2)}) collective-permute-start(f32[2,128,256]{2,1,0:T(8,128)S(1)} %get-tuple-element.36.mine_ref), channel_id=1, source_target_pairs={{0,8},{2,10},{4,12},{6,14},{8,0},{10,2},{12,4},{14,6},{16,24},{18,... | collective-permute-start | bytes 786440 | tf_op jit(solution)/shard_map/ppermute | solution.py:472
  40.1 1.0 %copy-start.8 = (f32[8,128,256]{2,1,0:T(8,128)}, f32[8,128,256]{2,1,0:T(8,128)S(1)}, u32[]{:S(2)}) copy-start(f32[8,128,256]{2,1,0:T(8,128)S(1)} %shard_map.99.wu_ref) | copy-start | bytes 3145732
  41.5 6.1 %copy-start.9 = (f32[8,128,256]{2,1,0:T(8,128)S(1)}, f32[8,128,256]{2,1,0:T(8,128)}, u32[]{:S(2)}) copy-start(f32[8,128,256]{2,1,0:T(8,128)} %copy-done.8) | copy-start | bytes 3145732
  42.0 8.4 %collective-permute-start.9 = (f32[2,128,128]{2,1,0:T(8,128)S(1)}, f32[2,128,128]{2,1,0:T(8,128)S(1)}, u32[]{:S(2)}, u32[]{:S(2)}) collective-permute-start(f32[2,128,128]{2,1,0:T(8,128)S(1)} %shard_map.100), channel_id=1, source_target_pairs={{0,24},{2,26},{4,28},{6,30},{8,16},{10,18},{12,20},{14,22},{16,8},... | collective-permute-start | bytes 393224 | tf_op jit(solution)/shard_map/ppermute | solution.py:490
  47.3 0.9 %copy-start.5 = (bf16[128,8,128]{2,1,0:T(8,128)(2,1)S(1)}, bf16[128,8,128]{2,1,0:T(8,128)(2,1)}, u32[]{:S(2)}) copy-start(bf16[128,8,128]{2,1,0:T(8,128)(2,1)} %param.8) | copy-start | bytes 786436
  50.3 9.3 %copy-start.1 = (bf16[128,8,128]{2,1,0:T(8,128)(2,1)S(1)}, bf16[128,8,128]{2,1,0:T(8,128)(2,1)}, u32[]{:S(2)}) copy-start(bf16[128,8,128]{2,1,0:T(8,128)(2,1)} %param.11) | copy-start | bytes 786436
  50.7 5.0 %collective-permute-start.10 = (f32[2,128,128]{2,1,0:T(8,128)S(1)}, f32[2,128,128]{2,1,0:T(8,128)S(1)}, u32[]{:S(2)}, u32[]{:S(2)}) collective-permute-start(f32[2,128,128]{2,1,0:T(8,128)S(1)} %get-tuple-element.47), channel_id=1, source_target_pairs={{0,2},{2,0},{4,6},{6,4},{8,10},{10,8},{12,14},{14,12},{16,18},{18,... | collective-permute-start | bytes 393224 | tf_op jit(solution)/shard_map/ppermute | solution.py:518
  52.3 5.0 %collective-permute-start.11 = (f32[2,128,128]{2,1,0:T(8,128)S(1)}, f32[2,128,128]{2,1,0:T(8,128)S(1)}, u32[]{:S(2)}, u32[]{:S(2)}) collective-permute-start(f32[2,128,128]{2,1,0:T(8,128)S(1)} %get-tuple-element.48), channel_id=1, source_target_pairs={{0,4},{2,6},{4,0},{6,2},{8,12},{10,14},{12,8},{14,10},{16,20},{18,... | collective-permute-start | bytes 393224 | tf_op jit(solution)/shard_map/ppermute | solution.py:518
  53.8 5.9 %collective-permute-start.12 = (f32[2,128,128]{2,1,0:T(8,128)S(1)}, f32[2,128,128]{2,1,0:T(8,128)S(1)}, u32[]{:S(2)}, u32[]{:S(2)}) collective-permute-start(f32[2,128,128]{2,1,0:T(8,128)S(1)} %get-tuple-element.49), channel_id=1, source_target_pairs={{0,6},{2,4},{4,2},{6,0},{8,14},{10,12},{12,10},{14,8},{16,22},{18,... | collective-permute-start | bytes 393224 | tf_op jit(solution)/shard_map/ppermute | solution.py:518

commit v6 on v5

--- a/solution.py
+++ b/solution.py
@@ -14,6 +14,8 @@
 F32 = jnp.float32
 BF16 = jnp.bfloat16
 VMEM_LIMIT = 20 * 1024 * 1024
+PIECES = 4
+EARLY = (0, 3)
 
 
 def split(x):
@@ -346,28 +348,85 @@
         out_refs[slot][...] = held_ref[slot]
 
 
-def finish_kernel(groups, per, rank_ref, *refs):
-    states = refs[:groups]
-    left_ref, right_ref, gate_ref, out_ref, block_ref, flat_ref, gates_ref = refs[groups:]
-    heads = groups * per
-    order = [(slot ^ rank_ref[0]) * per + i for slot in range(groups) for i in range(per)]
-    d = gate_ref.shape[1]
+def finish_heads(items, states, refs, block_hbm, flat_ref, gates_ref, inner_ref, sems):
+    left_ref, right_ref, gate_ref = refs
+    heads, d = left_ref.shape[0], gate_ref.shape[1]
     n = gate_ref.shape[0] // heads
-    blocks = block_ref.shape[0]
+    blocks = block_hbm.shape[0]
+    copies = []
+
+    def send(source, block, head, item):
+        copies.append(pltpu.make_async_copy(source, block_hbm.at[block, head], sems.at[block, item]))
+        copies[-1].start()
+
+    for item, (slot, i, head) in enumerate(items):
+        send(states[slot].at[i], 0, head, item)
     gates_ref[...] = gate_ref[...].astype(F32)
-    for item, head in enumerate(order):
-        state = states[item // per][item % per]
-        high, low = split(state)
+    for item, (slot, i, head) in enumerate(items):
+        high, low = split(states[slot][i])
         left = left_ref[head]
         both = mm(left, jnp.concatenate([high, high], 0)) + mm(left[:, :d], low) + right_ref[head]
+        for b in range(1, blocks):
+            inner_ref[item, b - 1] = both[n + (b - 1) * d : n + b * d]
+            send(inner_ref.at[item, b - 1], b, head, item)
         raw = both[:n]
-        block_ref[0, head] = state
-        for b in range(1, blocks):
-            block_ref[b, head] = both[n + (b - 1) * d : n + b * d]
         gate = gates_ref[pl.ds(head, n, stride=heads), :]
         scale = 1.0 / jnp.sqrt(jnp.mean(raw * raw, 1, keepdims=True) + EPSILON)
         flat_ref[pl.ds(head, n, stride=heads), :] = raw * scale * (gate / (1.0 + jnp.exp(-gate)))
-    out_ref[...] = flat_ref[...].astype(BF16)
+    return copies
+
+
+def slot_items(slots, per, rank):
+    return [(at, i, (slot ^ rank) * per + i) for at, slot in enumerate(slots) for i in range(per)]
+
+
+def first_kernel(slots, per, rank_ref, *refs):
+    early = len(slots)
+    states, left_ref, right_ref, gate_ref, flat_ref, block_hbm = refs[:early], *refs[early : early + 5]
+    copies = finish_heads(
+        slot_items(slots, per, rank_ref[0]),
+        states,
+        (left_ref, right_ref, gate_ref),
+        block_hbm,
+        flat_ref,
+        *refs[early + 5 :],
+    )
+    for copy in copies:
+        copy.wait()
+
+
+def finish_kernel(slots, groups, per, rank_ref, *refs):
+    states, refs = refs[: len(slots)], refs[len(slots) :]
+    left_ref, right_ref, gate_ref, done_ref, _, out_hbm, block_hbm, flat_ref, *rest = refs
+    *rest, rounded_ref, out_sems = rest
+    copies = finish_heads(
+        slot_items(slots, per, rank_ref[0]),
+        states,
+        (left_ref, right_ref, gate_ref),
+        block_hbm,
+        flat_ref,
+        *rest,
+    )
+    heads = groups * per
+    rows, d = flat_ref.shape
+    head = lax.broadcasted_iota(jnp.int32, (heads, d), 0)
+    slot = (head // per) ^ rank_ref[0]
+    was_done = functools.reduce(jnp.logical_and, [slot != mine for mine in slots])
+    size = rows // PIECES
+    for at in range(PIECES):
+        piece = pl.ds(at * size, size)
+        whole = jnp.where(
+            was_done[None],
+            done_ref[piece, :].reshape(size // heads, heads, d),
+            flat_ref[piece, :].reshape(size // heads, heads, d),
+        )
+        rounded_ref[piece, :] = whole.reshape(size, d).astype(BF16)
+        copies.append(
+            pltpu.make_async_copy(rounded_ref.at[piece], out_hbm.at[piece], out_sems.at[at])
+        )
+        copies[-1].start()
+    for copy in copies:
+        copy.wait()
 
 
 def exact(matrix, operand):
@@ -391,6 +450,7 @@
     blocks = n // BLOCK
     count, place = lax.axis_size("seq"), lax.axis_index("seq")
     groups = math.gcd(math.gcd(4, heads), count)
+    assert groups > 1
     per = heads // groups
     runs = count // groups
     rounds = runs.bit_length() - 1
@@ -514,17 +574,45 @@
         flops=1 << 27,
     )(rank, later, step, offset, start, came)
 
-    states = [entries[0]] + [
-        lax.ppermute(entries[slot], "seq", flipped(slot)) for slot in range(1, groups)
-    ]
-    gated, block_states = call(
-        functools.partial(finish_kernel, groups, per),
-        (shape(n * heads, d, dtype=BF16), shape(blocks, heads, d, d)),
-        scratch=(pltpu.VMEM((n * heads, d), F32), pltpu.VMEM((n * heads, d), F32)),
-        scalars=1,
-        operands=groups + 3,
-        flops=1 << 28,
-    )(rank, *states, left, right, flat(out_gate))
+    states = [entries[0]]
+    for slot in range(1, groups):
+        states.append(lax.ppermute(entries[slot], "seq", flipped(slot)))
+    early = [slot for slot in range(groups) if slot == 0 or slot in EARLY and groups > 2]
+    late = [slot for slot in range(groups) if slot not in early]
+
+    def room(slots):
+        return (
+            pltpu.VMEM((n * heads, d), F32),
+            pltpu.VMEM((slots * per, max(blocks - 1, 1), d, d), F32),
+            pltpu.SemaphoreType.DMA((blocks, slots * per)),
+        )
+
+    anywhere = pl.BlockSpec(memory_space=pl.ANY)
+    params = pltpu.CompilerParams(vmem_limit_bytes=VMEM_LIMIT)
+    cost = pl.CostEstimate(flops=1 << 28, bytes_accessed=1 << 20, transcendentals=0)
+    done, block_states = pl.pallas_call(
+        functools.partial(first_kernel, early, per),
+        out_shape=(shape(n * heads, d), shape(blocks, heads, d, d)),
+        in_specs=[smem()] + vmem(len(early) + 3),
+        out_specs=(vmem(1)[0], anywhere),
+        scratch_shapes=room(len(early)),
+        compiler_params=params,
+        cost_estimate=cost,
+        name="first",
+    )(rank, *(states[slot] for slot in early), left, right, flat(out_gate))
+    gated, block_states = pl.pallas_call(
+        functools.partial(finish_kernel, late, groups, per),
+        out_shape=(shape(n * heads, d, dtype=BF16), shape(blocks, heads, d, d)),
+        in_specs=[smem()] + vmem(len(late) + 4) + [anywhere],
+        out_specs=(anywhere, anywhere),
+        scratch_shapes=(pltpu.VMEM((n * heads, d), F32),)
+        + room(len(late))
+        + (pltpu.VMEM((n * heads, d), BF16), pltpu.SemaphoreType.DMA((PIECES,))),
+        input_output_aliases={len(late) + 5: 1},
+        compiler_params=params,
+        cost_estimate=cost,
+        name="finish",
+    )(rank, *(states[slot] for slot in late), left, right, flat(out_gate), done, block_states)
     return (gated.reshape(n, heads, d), block_states)
 
 

time: 61.7 us -> 60.2 us (0.976)
  waiting for transfers between devices: 21.6 us -> 19.6 us
    ppermute x3, waiting for transfers between devices: 5.35 us -> 3.34 us  [on_device(): states.append(lax.ppermute(entries[slot], 'seq', flipped(slot)))]
    pallas_call x1 -> x2, Pallas kernels: 1.85 us -> 2.42 us  [the longest x1 1.31 us: on_device(): pl.pallas_call(functools.partial(finish_kernel, late, groups, per), out_s...]
  transfers between devices with their start and end apart: 13 -> 13, of which waited for: 10 -> 10; matrix products, arithmetic and copies ran while one was open for 0% -> 0% of each run, Pallas kernels for 8% -> 10%
where the time goes in v6:
time: 60.2 us; the launch traced here: 60.1 us
  starting transfers between devices  24 us (40%)
  waiting for transfers between devices  19.6 us (33%)
  Pallas kernels  13 us (22%)
  local copies, waits for them, and re-layouts  2.59 us (4%)
  between operations  0.79 us (1%)
    ppermute x4, waiting for transfers between devices, shared(): return lax.ppermute(total, 'seq', flipped(mask))  14.5 us
    ppermute x4, starting transfers between devices, shared(): return lax.ppermute(total, 'seq', flipped(mask))  8.37 us
    ppermute x1, starting transfers between devices, on_device(): came = lax.ppermute(middle, 'seq', mirror)  5.31 us
    ppermute x3, starting transfers between devices, on_device(): exchanged.append(lax.ppermute(packs[slot], 'seq', flipped(slot)))  4.42 us
    pallas_call x1, Pallas kernels, on_device(): call(functools.partial(run_kernel, groups, per, tokens_all), (shape(max(g...  3.89 us
    ppermute x3, starting transfers between devices, on_device(): states.append(lax.ppermute(entries[slot], 'seq', flipped(slot)))  3.55 us
    ppermute x3, waiting for transfers between devices, on_device(): states.append(lax.ppermute(entries[slot], 'seq', flipped(slot)))  3.34 us
    pallas_call x1, Pallas kernels, on_device(): call(functools.partial(own_kernel, tokens_all), shape(heads, n, 2 * d), s...  3.09 us
  transfers between devices with their start and end apart: 13, of which 10 were waited for; matrix products, arithmetic and copies ran while one was open for 0% of the time, Pallas kernels for 10%

profile of v6, /device:TPU:0, one launch (start us, length us, event | category | flops | bytes accessed | tf_op | source)
XLA Modules:
  0.0 60.1 jit_solution(9091601786396911301)
XLA Ops:
  0.6 0.0 copy-start
  0.6 0.0 copy-start.3
  0.7 0.0 copy-start.4
  0.7 0.0 copy-start.6
  0.7 0.0 copy-start.7
  0.7 1.0 %copy-done.3 = bf16[128,8,128]{2,1,0:T(8,128)(2,1)S(1)} copy-done((bf16[128,8,128]{2,1,0:T(8,128)(2,1)S(1)}, bf16[128,8,128]{2,1,0:T(8,128)(2,1)}, u32[]{:S(2)}) %copy-start.3) | copy-done | bytes 262168
  1.7 0.1 copy-done.4
  1.7 0.0 copy-done.6
  1.7 0.0 copy-done.7
  1.7 0.0 copy-start.2
  1.7 0.5 shard_map.96
  2.2 0.5 collective-permute-start.4
  2.7 0.8 %collective-permute-done.4.came_ref = f32[8,128]{1,0:T(8,128)S(1)} collective-permute-done((f32[8,128]{1,0:T(8,128)S(1)}, f32[8,128]{1,0:T(8,128)S(1)}, u32[]{:S(2)}, u32[]{:S(2)}) %collective-permute-start.4) | collective-permute-done | bytes 4128 | tf_op jit(solution)/shard_map/ppermute | solution.py:481
  3.5 0.0 copy-done.2
  3.6 0.3 shard_map.97
  3.8 2.9 %collective-permute-start.5 = (f32[2,264,128]{2,1,0:T(8,128)S(1)}, f32[2,264,128]{2,1,0:T(8,128)S(1)}, u32[]{:S(2)}, u32[]{:S(2)}) collective-permute-start(f32[2,264,128]{2,1,0:T(8,128)S(1)} %get-tuple-element.35), channel_id=1, source_target_pairs={{0,2},{2,0},{4,6},{6,4},{8,10},{10,8},{12,14},{14,12},{16,18},{18,... | collective-permute-start | bytes 811016 | tf_op jit(solution)/shard_map/ppermute | solution.py:503
  6.7 1.5 %collective-permute-start.6 = (f32[2,264,128]{2,1,0:T(8,128)S(1)}, f32[2,264,128]{2,1,0:T(8,128)S(1)}, u32[]{:S(2)}, u32[]{:S(2)}) collective-permute-start(f32[2,264,128]{2,1,0:T(8,128)S(1)} %get-tuple-element.36), channel_id=1, source_target_pairs={{0,4},{2,6},{4,0},{6,2},{8,12},{10,14},{12,8},{14,10},{16,20},{18,... | collective-permute-start | bytes 811016 | tf_op jit(solution)/shard_map/ppermute | solution.py:503
  8.2 0.0 collective-permute-start.7
  8.2 1.9 %collective-permute-start = (f32[8,128]{1,0:T(8,128)S(1)}, f32[8,128]{1,0:T(8,128)S(1)}, u32[]{:S(2)}, u32[]{:S(2)}) collective-permute-start(f32[8,128]{1,0:T(8,128)S(1)} %get-tuple-element.30), channel_id=1, source_target_pairs={{0,2},{2,0},{4,6},{6,4},{8,10},{10,8},{12,14},{14,12},{16,18},{18,... | collective-permute-start | bytes 12296 | tf_op jit(solution)/shard_map/ppermute | solution.py:496
  10.2 9.3 %collective-permute-done = f32[8,128]{1,0:T(8,128)S(1)} collective-permute-done((f32[8,128]{1,0:T(8,128)S(1)}, f32[8,128]{1,0:T(8,128)S(1)}, u32[]{:S(2)}, u32[]{:S(2)}) %collective-permute-start) | collective-permute-done | bytes 4128 | tf_op jit(solution)/shard_map/ppermute | solution.py:496
  19.4 1.8 %collective-permute-start.1 = (f32[8,128]{1,0:T(8,128)S(1)}, f32[8,128]{1,0:T(8,128)S(1)}, u32[]{:S(2)}, u32[]{:S(2)}) collective-permute-start(f32[8,128]{1,0:T(8,128)S(1)} %add.22), channel_id=1, source_target_pairs={{0,4},{2,6},{4,0},{6,2},{8,12},{10,14},{12,8},{14,10},{16,20},{18,... | collective-permute-start | bytes 12296 | tf_op jit(solution)/shard_map/ppermute | solution.py:496
  21.2 1.8 %collective-permute-done.1 = f32[8,128]{1,0:T(8,128)S(1)} collective-permute-done((f32[8,128]{1,0:T(8,128)S(1)}, f32[8,128]{1,0:T(8,128)S(1)}, u32[]{:S(2)}, u32[]{:S(2)}) %collective-permute-start.1) | collective-permute-done | bytes 4128 | tf_op jit(solution)/shard_map/ppermute | solution.py:496
  23.1 1.8 %collective-permute-start.2 = (f32[8,128]{1,0:T(8,128)S(1)}, f32[8,128]{1,0:T(8,128)S(1)}, u32[]{:S(2)}, u32[]{:S(2)}) collective-permute-start(f32[8,128]{1,0:T(8,128)S(1)} %add.23), channel_id=1, source_target_pairs={{0,8},{2,10},{4,12},{6,14},{8,0},{10,2},{12,4},{14,6},{16,24},{18,... | collective-permute-start | bytes 12296 | tf_op jit(solution)/shard_map/ppermute | solution.py:496
  24.9 1.8 %collective-permute-done.2 = f32[8,128]{1,0:T(8,128)S(1)} collective-permute-done((f32[8,128]{1,0:T(8,128)S(1)}, f32[8,128]{1,0:T(8,128)S(1)}, u32[]{:S(2)}, u32[]{:S(2)}) %collective-permute-start.2) | collective-permute-done | bytes 4128 | tf_op jit(solution)/shard_map/ppermute | solution.py:496
  26.7 2.8 %collective-permute-start.3 = (f32[8,128]{1,0:T(8,128)S(1)}, f32[8,128]{1,0:T(8,128)S(1)}, u32[]{:S(2)}, u32[]{:S(2)}) collective-permute-start(f32[8,128]{1,0:T(8,128)S(1)} %add.24), channel_id=1, source_target_pairs={{0,16},{2,18},{4,20},{6,22},{8,24},{10,26},{12,28},{14,30},{16,0},... | collective-permute-start | bytes 12296 | tf_op jit(solution)/shard_map/ppermute | solution.py:496
  29.5 1.7 %collective-permute-done.3 = f32[8,128]{1,0:T(8,128)S(1)} collective-permute-done((f32[8,128]{1,0:T(8,128)S(1)}, f32[8,128]{1,0:T(8,128)S(1)}, u32[]{:S(2)}, u32[]{:S(2)}) %collective-permute-start.3) | collective-permute-done | bytes 4128 | tf_op jit(solution)/shard_map/ppermute | solution.py:496
  31.2 0.0 collective-permute-done.5.refs_1_
  31.2 0.0 collective-permute-done.6.refs_2_
  31.2 0.0 collective-permute-done.7.refs_3_
  31.2 3.9 %shard_map.98 = (f32[3,2,128,256]{3,2,1,0:T(8,128)S(1)}, f32[2,128,256]{2,1,0:T(8,128)S(1)}) custom-call(s32[1]{0:T(128)} %bitcast.rank_ref, f32[8,128]{1,0:T(8,128)S(1)} %add.25.total_ref, f32[2,264,128]{2,1,0:T(8,128)S(1)} %get-tuple-element.34.refs_0_, f32[2,264,128]{2,1,0:T(8,128)S(1)} %collective-permute-done.5.refs_1_, ...), custom_call_target="tpu_custom_call" | custom-call | flops 1073741824 | bytes 1048576 | tf_op jit(solution)/shard_map/pallas_call | solution.py:511
  35.1 1.9 %collective-permute-start.8 = (f32[2,128,256]{2,1,0:T(8,128)S(1)}, f32[2,128,256]{2,1,0:T(8,128)S(1)}, u32[]{:S(2)}, u32[]{:S(2)}) collective-permute-start(f32[2,128,256]{2,1,0:T(8,128)S(1)} %get-tuple-element.38.mine_ref), channel_id=1, source_target_pairs={{0,8},{2,10},{4,12},{6,14},{8,0},{10,2},{12,4},{14,6},{16,24},{18,... | collective-permute-start | bytes 786440 | tf_op jit(solution)/shard_map/ppermute | solution.py:532
  37.0 0.0 copy-done
  37.0 3.1 %shard_map.99.wu_ref = f32[8,128,256]{2,1,0:T(8,128)S(1)} custom-call(bf16[1024,128]{1,0:T(8,128)(2,1)S(1)} %bitcast.15, bf16[1024,128]{1,0:T(8,128)(2,1)S(1)} %bitcast.12, f32[8,128]{1,0:T(8,128)S(1)} %get-tuple-element.39.beta_ref, f32[8,128]{1,0:T(8,128)S(1)} %add.25.total_ref, f32[8,128]{1,0:T(8,128)S(1)} %get-tuple-element.31.cum_ref), custom_call_target="tpu_custom_call" | custom-call | flops 2147483648 | bytes 1048576 | tf_op jit(solution)/shard_map/pallas_call | solution.py:520
  40.1 0.0 copy-start.8
  40.1 1.0 %copy-done.8 = f32[8,128,256]{2,1,0:T(8,128)} copy-done((f32[8,128,256]{2,1,0:T(8,128)}, f32[8,128,256]{2,1,0:T(8,128)S(1)}, u32[]{:S(2)}) %copy-start.8) | copy-done | bytes 1048600
  41.1 0.5 collective-permute-done.8.other_ref.before_ref
  41.5 0.0 copy-start.9
  41.5 0.4 shard_map.100
  42.0 5.3 %collective-permute-start.9 = (f32[2,128,128]{2,1,0:T(8,128)S(1)}, f32[2,128,128]{2,1,0:T(8,128)S(1)}, u32[]{:S(2)}, u32[]{:S(2)}) collective-permute-start(f32[2,128,128]{2,1,0:T(8,128)S(1)} %shard_map.100), channel_id=1, source_target_pairs={{0,24},{2,26},{4,28},{6,30},{8,16},{10,18},{12,20},{14,22},{16,8},... | collective-permute-start | bytes 393224 | tf_op jit(solution)/shard_map/ppermute | solution.py:550
  47.3 0.0 copy-start.5
  47.3 0.4 shard_map.102
  47.7 0.0 copy-done.9
  47.7 0.6 copy-done.5
  48.2 1.7 %shard_map.101 = (bf16[8,256,256]{2,1,0:T(8,128)(2,1)S(1)}, f32[8,256,128]{2,1,0:T(8,128)S(1)}) custom-call(bf16[1024,128]{1,0:T(8,128)(2,1)S(1)} %bitcast.17, bf16[1024,128]{1,0:T(8,128)(2,1)S(1)} %bitcast.16, f32[8,128]{1,0:T(8,128)S(1)} %get-tuple-element.31.cum_ref, f32[8,128,256]{2,1,0:T(8,128)S(1)} %copy-done.9), custom_call_target="tpu_custom_call" | custom-call | flops 1073741824 | bytes 1048576 | tf_op jit(solution)/shard_map/pallas_call | solution.py:553
  49.9 0.4 collective-permute-done.9.came_ref
  50.3 0.0 copy-start.1
  50.3 0.4 shard_map.103
  50.7 2.5 %collective-permute-start.12 = (f32[2,128,128]{2,1,0:T(8,128)S(1)}, f32[2,128,128]{2,1,0:T(8,128)S(1)}, u32[]{:S(2)}, u32[]{:S(2)}) collective-permute-start(f32[2,128,128]{2,1,0:T(8,128)S(1)} %get-tuple-element.53), channel_id=1, source_target_pairs={{0,6},{2,4},{4,2},{6,0},{8,14},{10,12},{12,10},{14,8},{16,22},{18,... | collective-permute-start | bytes 393224 | tf_op jit(solution)/shard_map/ppermute | solution.py:579
  53.2 0.6 collective-permute-start.10
  53.8 0.5 collective-permute-start.11
  54.3 2.4 %collective-permute-done.12.refs_1_ = f32[2,128,128]{2,1,0:T(8,128)S(1)} collective-permute-done((f32[2,128,128]{2,1,0:T(8,128)S(1)}, f32[2,128,128]{2,1,0:T(8,128)S(1)}, u32[]{:S(2)}, u32[]{:S(2)}) %collective-permute-start.12) | collective-permute-done | bytes 131104 | tf_op jit(solution)/shard_map/ppermute | solution.py:579
  56.7 0.0 copy-done.1
  56.7 1.1 %first.1 = (f32[1024,128]{1,0:T(8,128)S(1)}, f32[2,8,128,128]{3,2,1,0:T(8,128)}) custom-call(s32[1]{0:T(128)} %bitcast.rank_ref, f32[2,128,128]{2,1,0:T(8,128)S(1)} %get-tuple-element.52.refs_0_, f32[2,128,128]{2,1,0:T(8,128)S(1)} %collective-permute-done.12.refs_1_, bf16[8,256,256]{2,1,0:T(8,128)(2,1)S(1)} %get-tuple-element.50.refs_2_, ...), custom_call_target="tpu_custom_call" | custom-call | flops 268435456 | bytes 1048576 | tf_op jit(solution)/shard_map/first/pallas_call | solution.py:593
  57.8 0.4 collective-permute-done.10.refs_0_
  58.2 0.6 collective-permute-done.11.refs_1_
  58.8 1.3 %finish.1 = (bf16[1024,128]{1,0:T(8,128)(2,1)}, f32[2,8,128,128]{3,2,1,0:T(8,128)}) custom-call(s32[1]{0:T(128)} %bitcast.rank_ref, f32[2,128,128]{2,1,0:T(8,128)S(1)} %collective-permute-done.10.refs_0_, f32[2,128,128]{2,1,0:T(8,128)S(1)} %collective-permute-done.11.refs_1_, ...), custom_call_target="tpu_custom_call", output_to_operand_aliasing={{1}: (7, {})} | custom-call | flops 268435456 | bytes 1048576 | tf_op jit(solution)/shard_map/finish/pallas_call | solution.py:603
  (6 shorter events, 0.0 us)
Async XLA Ops:
  0.6 36.4 %copy-start = (f32[8,128,128]{2,1,0:T(8,128)S(1)}, f32[8,128,128]{2,1,0:T(8,128)}, u32[]{:S(2)}) copy-start(f32[8,128,128]{2,1,0:T(8,128)} %param.15) | copy-start | bytes 1572868
  0.6 1.0 %copy-start.3 = (bf16[128,8,128]{2,1,0:T(8,128)(2,1)S(1)}, bf16[128,8,128]{2,1,0:T(8,128)(2,1)}, u32[]{:S(2)}) copy-start(bf16[128,8,128]{2,1,0:T(8,128)(2,1)} %param.9) | copy-start | bytes 786436
  0.7 1.1 %copy-start.4 = (bf16[128,1024]{1,0:T(8,128)(2,1)S(1)}, bf16[128,1024]{1,0:T(8,128)(2,1)}, u32[]{:S(2)}) copy-start(bf16[128,1024]{1,0:T(8,128)(2,1)} %inputs_ref.1) | copy-start | bytes 786436
  0.7 1.1 %copy-start.6 = (bf16[16,1024]{1,0:T(8,128)(2,1)S(1)}, bf16[16,1024]{1,0:T(8,128)(2,1)}, u32[]{:S(2)}) copy-start(bf16[16,1024]{1,0:T(8,128)(2,1)} %weight_ref.1) | copy-start | bytes 98308
  0.7 1.1 %copy-start.7 = (f32[8,128]{1,0:T(8,128)S(1)}, f32[8,128]{1,0:T(8,128)}, u32[]{:S(2)}) copy-start(f32[8,128]{1,0:T(8,128)} %decay_ref.1) | copy-start | bytes 12292
  1.7 1.8 %copy-start.2 = (bf16[128,8,128]{2,1,0:T(8,128)(2,1)S(1)}, bf16[128,8,128]{2,1,0:T(8,128)(2,1)}, u32[]{:S(2)}) copy-start(bf16[128,8,128]{2,1,0:T(8,128)(2,1)} %param.10) | copy-start | bytes 786436
  2.2 1.3 %collective-permute-start.4 = (f32[8,128]{1,0:T(8,128)S(1)}, f32[8,128]{1,0:T(8,128)S(1)}, u32[]{:S(2)}, u32[]{:S(2)}) collective-permute-start(f32[8,128]{1,0:T(8,128)S(1)} %get-tuple-element.33), channel_id=1, source_target_pairs={{0,1},{1,0},{2,3},{3,2},{4,5},{5,4},{6,7},{7,6},{8,9},{9,8},{10,11... | collective-permute-start | bytes 12296 | tf_op jit(solution)/shard_map/ppermute | solution.py:481
  3.8 27.4 %collective-permute-start.5 = (f32[2,264,128]{2,1,0:T(8,128)S(1)}, f32[2,264,128]{2,1,0:T(8,128)S(1)}, u32[]{:S(2)}, u32[]{:S(2)}) collective-permute-start(f32[2,264,128]{2,1,0:T(8,128)S(1)} %get-tuple-element.35), channel_id=1, source_target_pairs={{0,2},{2,0},{4,6},{6,4},{8,10},{10,8},{12,14},{14,12},{16,18},{18,... | collective-permute-start | bytes 811016 | tf_op jit(solution)/shard_map/ppermute | solution.py:503
  6.7 24.5 %collective-permute-start.6 = (f32[2,264,128]{2,1,0:T(8,128)S(1)}, f32[2,264,128]{2,1,0:T(8,128)S(1)}, u32[]{:S(2)}, u32[]{:S(2)}) collective-permute-start(f32[2,264,128]{2,1,0:T(8,128)S(1)} %get-tuple-element.36), channel_id=1, source_target_pairs={{0,4},{2,6},{4,0},{6,2},{8,12},{10,14},{12,8},{14,10},{16,20},{18,... | collective-permute-start | bytes 811016 | tf_op jit(solution)/shard_map/ppermute | solution.py:503
  8.2 23.0 %collective-permute-start.7 = (f32[2,264,128]{2,1,0:T(8,128)S(1)}, f32[2,264,128]{2,1,0:T(8,128)S(1)}, u32[]{:S(2)}, u32[]{:S(2)}) collective-permute-start(f32[2,264,128]{2,1,0:T(8,128)S(1)} %get-tuple-element.37), channel_id=1, source_target_pairs={{0,6},{2,4},{4,2},{6,0},{8,14},{10,12},{12,10},{14,8},{16,22},{18,... | collective-permute-start | bytes 811016 | tf_op jit(solution)/shard_map/ppermute | solution.py:503
  8.2 11.2 %collective-permute-start = (f32[8,128]{1,0:T(8,128)S(1)}, f32[8,128]{1,0:T(8,128)S(1)}, u32[]{:S(2)}, u32[]{:S(2)}) collective-permute-start(f32[8,128]{1,0:T(8,128)S(1)} %get-tuple-element.30), channel_id=1, source_target_pairs={{0,2},{2,0},{4,6},{6,4},{8,10},{10,8},{12,14},{14,12},{16,18},{18,... | collective-permute-start | bytes 12296 | tf_op jit(solution)/shard_map/ppermute | solution.py:496
  19.4 3.6 %collective-permute-start.1 = (f32[8,128]{1,0:T(8,128)S(1)}, f32[8,128]{1,0:T(8,128)S(1)}, u32[]{:S(2)}, u32[]{:S(2)}) collective-permute-start(f32[8,128]{1,0:T(8,128)S(1)} %add.22), channel_id=1, source_target_pairs={{0,4},{2,6},{4,0},{6,2},{8,12},{10,14},{12,8},{14,10},{16,20},{18,... | collective-permute-start | bytes 12296 | tf_op jit(solution)/shard_map/ppermute | solution.py:496
  23.1 3.6 %collective-permute-start.2 = (f32[8,128]{1,0:T(8,128)S(1)}, f32[8,128]{1,0:T(8,128)S(1)}, u32[]{:S(2)}, u32[]{:S(2)}) collective-permute-start(f32[8,128]{1,0:T(8,128)S(1)} %add.23), channel_id=1, source_target_pairs={{0,8},{2,10},{4,12},{6,14},{8,0},{10,2},{12,4},{14,6},{16,24},{18,... | collective-permute-start | bytes 12296 | tf_op jit(solution)/shard_map/ppermute | solution.py:496
  26.7 4.5 %collective-permute-start.3 = (f32[8,128]{1,0:T(8,128)S(1)}, f32[8,128]{1,0:T(8,128)S(1)}, u32[]{:S(2)}, u32[]{:S(2)}) collective-permute-start(f32[8,128]{1,0:T(8,128)S(1)} %add.24), channel_id=1, source_target_pairs={{0,16},{2,18},{4,20},{6,22},{8,24},{10,26},{12,28},{14,30},{16,0},... | collective-permute-start | bytes 12296 | tf_op jit(solution)/shard_map/ppermute | solution.py:496
  35.1 6.4 %collective-permute-start.8 = (f32[2,128,256]{2,1,0:T(8,128)S(1)}, f32[2,128,256]{2,1,0:T(8,128)S(1)}, u32[]{:S(2)}, u32[]{:S(2)}) collective-permute-start(f32[2,128,256]{2,1,0:T(8,128)S(1)} %get-tuple-element.38.mine_ref), channel_id=1, source_target_pairs={{0,8},{2,10},{4,12},{6,14},{8,0},{10,2},{12,4},{14,6},{16,24},{18,... | collective-permute-start | bytes 786440 | tf_op jit(solution)/shard_map/ppermute | solution.py:532
  40.1 1.0 %copy-start.8 = (f32[8,128,256]{2,1,0:T(8,128)}, f32[8,128,256]{2,1,0:T(8,128)S(1)}, u32[]{:S(2)}) copy-start(f32[8,128,256]{2,1,0:T(8,128)S(1)} %shard_map.99.wu_ref) | copy-start | bytes 3145732
  41.5 6.1 %copy-start.9 = (f32[8,128,256]{2,1,0:T(8,128)S(1)}, f32[8,128,256]{2,1,0:T(8,128)}, u32[]{:S(2)}) copy-start(f32[8,128,256]{2,1,0:T(8,128)} %copy-done.8) | copy-start | bytes 3145732
  42.0 8.4 %collective-permute-start.9 = (f32[2,128,128]{2,1,0:T(8,128)S(1)}, f32[2,128,128]{2,1,0:T(8,128)S(1)}, u32[]{:S(2)}, u32[]{:S(2)}) collective-permute-start(f32[2,128,128]{2,1,0:T(8,128)S(1)} %shard_map.100), channel_id=1, source_target_pairs={{0,24},{2,26},{4,28},{6,30},{8,16},{10,18},{12,20},{14,22},{16,8},... | collective-permute-start | bytes 393224 | tf_op jit(solution)/shard_map/ppermute | solution.py:550
  47.3 0.9 %copy-start.5 = (bf16[128,8,128]{2,1,0:T(8,128)(2,1)S(1)}, bf16[128,8,128]{2,1,0:T(8,128)(2,1)}, u32[]{:S(2)}) copy-start(bf16[128,8,128]{2,1,0:T(8,128)(2,1)} %param.8) | copy-start | bytes 786436
  50.3 6.4 %copy-start.1 = (bf16[128,8,128]{2,1,0:T(8,128)(2,1)S(1)}, bf16[128,8,128]{2,1,0:T(8,128)(2,1)}, u32[]{:S(2)}) copy-start(bf16[128,8,128]{2,1,0:T(8,128)(2,1)} %param.11) | copy-start | bytes 786436
  50.7 5.9 %collective-permute-start.12 = (f32[2,128,128]{2,1,0:T(8,128)S(1)}, f32[2,128,128]{2,1,0:T(8,128)S(1)}, u32[]{:S(2)}, u32[]{:S(2)}) collective-permute-start(f32[2,128,128]{2,1,0:T(8,128)S(1)} %get-tuple-element.53), channel_id=1, source_target_pairs={{0,6},{2,4},{4,2},{6,0},{8,14},{10,12},{12,10},{14,8},{16,22},{18,... | collective-permute-start | bytes 393224 | tf_op jit(solution)/shard_map/ppermute | solution.py:579
  53.2 5.0 %collective-permute-start.10 = (f32[2,128,128]{2,1,0:T(8,128)S(1)}, f32[2,128,128]{2,1,0:T(8,128)S(1)}, u32[]{:S(2)}, u32[]{:S(2)}) collective-permute-start(f32[2,128,128]{2,1,0:T(8,128)S(1)} %get-tuple-element.48), channel_id=1, source_target_pairs={{0,2},{2,0},{4,6},{6,4},{8,10},{10,8},{12,14},{14,12},{16,18},{18,... | collective-permute-start | bytes 393224 | tf_op jit(solution)/shard_map/ppermute | solution.py:579
  53.8 5.0 %collective-permute-start.11 = (f32[2,128,128]{2,1,0:T(8,128)S(1)}, f32[2,128,128]{2,1,0:T(8,128)S(1)}, u32[]{:S(2)}, u32[]{:S(2)}) collective-permute-start(f32[2,128,128]{2,1,0:T(8,128)S(1)} %get-tuple-element.49), channel_id=1, source_target_pairs={{0,4},{2,6},{4,0},{6,2},{8,12},{10,14},{12,8},{14,10},{16,20},{18,... | collective-permute-start | bytes 393224 | tf_op jit(solution)/shard_map/ppermute | solution.py:579
